TPU v7x, 32 devices: a whole 2x2x4 slice. The times are simulated.
32 devices in a mesh: aux: 8 (over y, x, core), half: 4 (over z).
Axes of the slice: x: 2, y: 2, z: 4, core: 2. Of those that a mesh axis runs over, the one named last changes fastest.
Arguments:
- half_slabs: bfloat16 [1536, 4, 8, 960], P('aux', 'half'), may hold values from -1 to 1
- vir_coeff: bfloat16 [960, 384], replicated, may hold values from -0.1875 to 0.1875
- occ_energy: int32 [32], replicated, may hold values from -3000 to -401
- vir_energy: int32 [384], replicated, may hold values from 200 to 3999
- plan: int32 [1, 4], replicated, may hold values from 0 to 31, as said below
Outputs:
- density: bfloat16 [4, 8, 384, 1536], P('half', 'aux')
- pair_energy: float32 [4, 8], P('half', 'aux')
Inputs may be any that keep to these rules, and one draw needn't show every extreme that they name: `plan`: all 4 partner indices are distinct.
All inputs are finite; a program needn't handle non-finite values.
Results may differ from a plain program's by a relative error of at most 0.006.
Values may be sent and summed in bfloat16 or wider, within the bound.
No kernel may reach another device: no remote copies, remote signals or barrier semaphores. Data moves between devices by JAX's collectives and lax.ppermute only.
A program may use at most 64 MiB of HBM per device.

v0:
```python
import jax
import jax.numpy as jnp
from jax import lax
from jax.sharding import PartitionSpec as P


def broadcast(x, axis, root):
    mine = lax.axis_index(axis) == root
    return lax.psum(jnp.where(mine, x, jnp.zeros_like(x)), axis)


def on_device(half_slabs, vir_coeff, occ_energy, vir_energy, plan):
    local_aux = half_slabs.shape[0]
    ohalf = half_slabs.shape[2]
    flat = half_slabs.reshape(local_aux * ohalf, half_slabs.shape[3])
    prod = jnp.dot(flat, vir_coeff, preferred_element_type=jnp.float32)
    transformed = prod.reshape(local_aux, ohalf, vir_coeff.shape[1]).astype(jnp.bfloat16)
    owned = lax.all_to_all(transformed, "aux", split_axis=1, concat_axis=0, tiled=True)
    n_half = lax.axis_size("half")
    aux_index = lax.axis_index("aux")
    half_index = lax.axis_index("half")
    o_dev = owned.shape[1]
    n_virt = owned.shape[2]
    own_start = half_index * ohalf + aux_index * o_dev
    occ_e = occ_energy.astype(jnp.float32) * 0.001
    own_e = lax.dynamic_slice_in_dim(occ_e, own_start, o_dev)
    vir_e = vir_energy.astype(jnp.float32) * 0.001
    gamma = jnp.zeros((o_dev, n_virt, owned.shape[0]), jnp.float32)
    energy = jnp.zeros((o_dev,), jnp.float32)
    owners = plan.shape[1]
    for slot in range(owners):
        partner = plan[0, slot]
        part_half = partner // ohalf
        part_aux = partner % ohalf // o_dev
        piece = lax.dynamic_index_in_dim(owned, partner % o_dev, 1, keepdims=False)
        other = broadcast(piece, ("aux", "half"), part_aux * n_half + part_half)
        part_e = lax.dynamic_index_in_dim(occ_e, partner, 0, keepdims=False)
        kmat = jnp.einsum("pia,pb->iab", owned, other, preferred_element_type=jnp.float32)
        denom = own_e[:, None, None] + part_e - vir_e[None, :, None] - vir_e[None, None, :]
        tilde = (2.0 * kmat - jnp.swapaxes(kmat, 1, 2)) / denom
        energy = energy + jnp.sum(kmat * tilde, axis=(1, 2))
        gamma = gamma + jnp.einsum(
            "iab,pb->iap", tilde.astype(jnp.bfloat16), other, preferred_element_type=jnp.float32
        )
    density = gamma.astype(jnp.bfloat16)[None]
    pair_energy = (energy / (n_virt * n_virt))[None]
    return (density, pair_energy)


def solution(mesh):
    in_specs = (P("aux", "half", None, None), P(), P(), P(), P())
    out_specs = (P("half", "aux", None, None), P("half", "aux"))
    return jax.shard_map(
        on_device, mesh=mesh, in_specs=in_specs, out_specs=out_specs, check_vma=False
    )
```

profile of v0, /device:TPU:0, one launch (start us, length us, event | category | flops | bytes accessed | tf_op | source)
XLA Modules:
  0.0 238.7 jit_solution(14202534869236613495)
XLA Ops:
  7.2 1.9 copy-done
  9.1 2.9 %fusion.4 = bf16[192,8,384]{2,1,0:T(8,128)(2,1)S(1)} fusion(bf16[192,1,8,960]{3,2,1,0:T(8,128)(2,1)S(1)} %copy-done, bf16[960,384]{1,0:T(8,128)(2,1)} %param.6), kind=kOutput, calls=%fused_computation.7 | convolution fusion | flops 1133051904 | bytes 4866048 | tf_op jit(solution)/shard_map/dot_general | solution.py:16
  12.0 1.2 copy.32
  13.1 5.3 %all-to-all-start = ((bf16[192,8,384]{2,0,1:T(8,128)(2,1)}), bf16[192,8,384]{2,0,1:T(8,128)(2,1)}, u32[]{:S(2)}, u32[]{:S(2)}) async-start(bf16[192,8,384]{2,0,1:T(8,128)(2,1)} %copy.32), calls=%async_computation | async-start | bytes 2359296 | tf_op jit(solution)/shard_map/all_to_all | solution.py:18
  18.5 0.0 all-reduce.3.cloned.1.call-start
  18.5 0.7 fusion.26
  29.3 6.0 %all-to-all-done = bf16[192,8,384]{2,0,1:T(8,128)(2,1)} async-done(((bf16[192,8,384]{2,0,1:T(8,128)(2,1)}), bf16[192,8,384]{2,0,1:T(8,128)(2,1)}, u32[]{:S(2)}, u32[]{:S(2)}) %all-to-all-start) | async-done | bytes 1179680 | tf_op jit(solution)/shard_map/all_to_all | solution.py:18
  35.4 3.7 %broadcast_select_fusion = (bf16[1536,384]{1,0:T(8,128)(2,1)}, bf16[1536,384]{1,0:T(8,128)(2,1)}, bf16[1536,384]{1,0:T(8,128)(2,1)}, bf16[1536,384]{1,0:T(8,128)(2,1)}) fusion(pred[]{:T(512)S(6)} %eq.24, bf16[192,8,384]{2,0,1:T(8,128)(2,1)} %all-to-all-done, pred[]{:T(512)S(6)} %eq.21, pred[]{:T(512)S(6)} %eq.22, pred[]{:T(512)S(6)} %eq.23), kind=kLoop, calls=%fused_computation.8 | loop fusion | flops 2359296 | bytes 5898244 | tf_op jit(solution)/shard_map/jit(_where)/select_n | solution.py:9
  39.0 0.0 all-reduce.3.cloned.1.call-update
  44.1 0.7 fusion.25
  50.0 134.9 %all-reduce.3.cloned.1.call-done = (bf16[1536,384]{1,0:T(8,128)(2,1)}, bf16[1536,384]{1,0:T(8,128)(2,1)}, bf16[1536,384]{1,0:T(8,128)(2,1)}, bf16[1536,384]{1,0:T(8,128)(2,1)}) async-done(((bf16[1536,384]{1,0:T(8,128)(2,1)}, bf16[1536,384]{1,0:T(8,128)(2,1)}, bf16[1536,384]{1,0:T(8,128)(2,1)}, bf16[1536,384]{1,0:T(8,128)(2,1)}), (bf16[1536,384]{1,0:T(8,128)(2,1)}, bf16[1536,384]{1,0:T(8,128)(2,1)}, ...) | async-done | bytes 4718608 | tf_op jit(solution)/shard_map/psum | solution.py:9
  184.9 3.2 %fusion.27 = f32[384,384]{1,0:T(8,128)} fusion(bf16[1536,384]{1,0:T(8,128)(2,1)} %bitcast.4, bf16[1536,384]{1,0:T(8,128)(2,1)} %get-tuple-element.6), kind=kOutput, calls=%fused_computation.46 | convolution fusion | flops 452984832 | bytes 2949120 | tf_op jit(solution)/shard_map/pia,pb->iab/dot_general | solution.py:38
  188.1 2.1 copy.33
  190.2 2.1 bitcast_subtract_fusion.1
  192.4 2.1 copy.34
  194.5 3.3 %fusion.28 = f32[384,384]{0,1:T(8,128)} fusion(bf16[1536,384]{1,0:T(8,128)(2,1)} %bitcast.4, bf16[1536,384]{1,0:T(8,128)(2,1)} %get-tuple-element.7), kind=kOutput, calls=%fused_computation.47 | convolution fusion | flops 452984832 | bytes 2949120 | tf_op jit(solution)/shard_map/pia,pb->iab/dot_general | solution.py:38
  197.8 2.2 copy.37
  200.0 3.3 %fusion.29 = f32[384,384]{0,1:T(8,128)} fusion(bf16[1536,384]{1,0:T(8,128)(2,1)} %bitcast.4, bf16[1536,384]{1,0:T(8,128)(2,1)} %get-tuple-element.8), kind=kOutput, calls=%fused_computation.48 | convolution fusion | flops 452984832 | bytes 2949120 | tf_op jit(solution)/shard_map/pia,pb->iab/dot_general | solution.py:38
  203.3 2.1 copy.41
  205.4 2.4 %fusion.17 = f32[384,1536]{1,0:T(8,128)S(1)} fusion(bf16[1536,384]{1,0:T(8,128)(2,1)} %get-tuple-element.6, f32[1,384,384]{2,1,0:T(8,128)} %copy.34, f32[384]{0:T(512)S(1)} %get-tuple-element.18, f32[384]{0:T(512)S(1)} %get-tuple-element.15), kind=kOutput, calls=%fused_computation.32 | convolution fusion | flops 453427200 | bytes 4131840 | tf_op jit(solution)/shard_map/iab,pb->iap/dot_general | solution.py:42
  207.9 1.0 convolution_add_fusion.2
  208.8 0.1 copy-done.2
  208.9 0.2 copy-done.3
  209.1 1.1 fusion.9
  210.2 0.2 copy-done.7
  210.4 2.4 convolution_add_fusion.1
  212.7 2.9 %fusion.30 = f32[384,384]{1,0:T(8,128)} fusion(bf16[1536,384]{1,0:T(8,128)(2,1)} %bitcast.4, bf16[1536,384]{1,0:T(8,128)(2,1)S(1)} %copy-done.6), kind=kOutput, calls=%fused_computation.49 | convolution fusion | flops 452984832 | bytes 2949120 | tf_op jit(solution)/shard_map/pia,pb->iab/dot_general | solution.py:38
  215.6 2.1 copy.43
  217.8 2.1 bitcast_subtract_fusion
  219.9 2.1 copy.44
  222.1 2.7 %fusion.8 = (f32[]{:T(128)}, f32[]{:T(128)}) fusion(f32[384,384]{1,0:T(8,128)} %fusion.30, f32[1,384,384]{2,1,0:T(8,128)} %copy.44, f32[384]{0:T(512)S(1)} %get-tuple-element.18, f32[384]{0:T(512)S(1)} %get-tuple-element.14, f32[1,384,384]{2,1,0:T(8,128)} %copy.34, f32[384]{0:T(512)S(1)} %get-tuple-element.15, f32[384,384]{1,0:T(8,128)} %fusion.27), kind=kLoop, calls=%fused_computation.16 | loop fusion | flops 1179646 | bytes 2363912 | tf_op jit(solution)/shard_map/reduce_sum | solution.py:41
  224.8 3.3 %fusion.3 = bf16[1,1,384,1536]{3,2,1,0:T(8,128)(2,1)} fusion(f32[384,1536]{1,0:T(8,128)S(1)} %copy-done.1, bf16[1536,384]{1,0:T(8,128)(2,1)} %get-tuple-element.9, f32[1,384,384]{2,1,0:T(8,128)} %copy.44, f32[384]{0:T(512)S(1)} %get-tuple-element.14, f32[384]{0:T(512)S(1)} %get-tuple-element.18), kind=kOutput, calls=%fused_computation.6 | convolution fusion | flops 454606848 | bytes 5311488 | tf_op jit(solution)/shard_map/iab,pb->iap/dot_general | solution.py:42
  (22 shorter events, 0.1 us)
Async XLA Ops:
  7.2 1.9 copy-start
  13.1 5.4 %copy-start.9 = (s32[1,4]{1,0:T(1,128)S(1)}, s32[1,4]{1,0:T(1,128)}, u32[]{:S(2)}) copy-start(s32[1,4]{1,0:T(1,128)} %param.9) | copy-start | bytes 52
  13.1 22.2 %all-to-all-start = ((bf16[192,8,384]{2,0,1:T(8,128)(2,1)}), bf16[192,8,384]{2,0,1:T(8,128)(2,1)}, u32[]{:S(2)}, u32[]{:S(2)}) async-start(bf16[192,8,384]{2,0,1:T(8,128)(2,1)} %copy.32), calls=%async_computation | async-start | bytes 2359296 | tf_op jit(solution)/shard_map/all_to_all | solution.py:18
  18.5 166.4 %all-reduce.3.cloned.1.call-start = ((), (), s32[]{:S(2)}) async-start(), calls=%async_computation.1 | async-start | bytes 9437184 | tf_op jit(solution)/shard_map/psum | solution.py:9
  39.0 5.0 %copy-start.11 = (s32[32]{0:T(128)S(1)}, s32[32]{0:T(128)}, u32[]{:S(2)}) copy-start(s32[32]{0:T(128)} %param.7) | copy-start | bytes 388
  39.0 10.9 %copy-start.10 = (s32[384]{0:T(512)S(1)}, s32[384]{0:T(512)}, u32[]{:S(2)}) copy-start(s32[384]{0:T(512)} %param.8) | copy-start | bytes 4612
  205.4 2.4 %copy-start.4 = (f32[384,384]{0,1:T(8,128)S(1)}, f32[384,384]{0,1:T(8,128)}, u32[]{:S(2)}) copy-start(f32[384,384]{0,1:T(8,128)} %fusion.28) | copy-start | bytes 1769476
  205.4 2.5 %copy-start.5 = (f32[1,384,384]{1,2,0:T(8,128)S(1)}, f32[1,384,384]{1,2,0:T(8,128)}, u32[]{:S(2)}) copy-start(f32[1,384,384]{1,2,0:T(8,128)} %copy.37) | copy-start | bytes 1769476
  205.4 2.5 %copy-start.8 = (bf16[1536,384]{1,0:T(8,128)(2,1)S(1)}, bf16[1536,384]{1,0:T(8,128)(2,1)}, u32[]{:S(2)}) copy-start(bf16[1536,384]{1,0:T(8,128)(2,1)} %get-tuple-element.7) | copy-start | bytes 3538948
  207.8 1.1 copy-start.2
  207.8 1.2 copy-start.3
  209.1 1.3 copy-start.7
  210.4 2.4 copy-start.6
  222.1 2.7 %copy-start.1 = (f32[384,1536]{1,0:T(8,128)S(1)}, f32[384,1536]{1,0:T(8,128)}, u32[]{:S(2)}) copy-start(f32[384,1536]{1,0:T(8,128)} %convolution_add_fusion.1) | copy-start | bytes 7077892
Sparse Core Ops, SparseCore 0:
  39.2 145.6 all-reduce.2
where the time goes:
time: 240 us; the launch traced here: 239 us
  waiting for transfers between devices  141 us (59%)
  between operations  38.3 us (16%)
  matrix products  24.7 us (10%)
  local copies, waits for them, and re-layouts  17.6 us (7%)
  other arithmetic  11.8 us (5%)
  starting transfers between devices  5.37 us (2%)
    psum x1, waiting for transfers between devices, broadcast(): return lax.psum(jnp.where(mine, x, jnp.zeros_like(x)), axis)  135 us
    dot_general x4, matrix products, on_device(): jnp.einsum('pia,pb->iab', owned, other, preferred_element_type=jnp.float32)  12.7 us
    dot_general x4, matrix products, on_device(): jnp.einsum('iab,pb->iap', tilde.astype(jnp.bfloat16), other, preferred_el...  9.09 us
    all_to_all x1, waiting for transfers between devices, on_device(): lax.all_to_all(transformed, 'aux', split_axis=1, concat_axis=0, tiled=True)  6.05 us
    all_to_all x1, starting transfers between devices, on_device(): lax.all_to_all(transformed, 'aux', split_axis=1, concat_axis=0, tiled=True)  5.34 us
  transfers between devices with their start and end apart: 2, of which 2 were waited for; matrix products, arithmetic and copies ran while one was open for 1% of the time, Pallas kernels for 0%

commit v1 on v0

v1 whole, which is shorter than its diff:
```python
import functools

import jax
import jax.numpy as jnp
from jax import lax
from jax.experimental import pallas as pl
from jax.experimental.pallas import tpu as pltpu
from jax.sharding import PartitionSpec as P


F32 = jnp.float32
BF16 = jnp.bfloat16


def broadcast(x, axis, root):
    mine = lax.axis_index(axis) == root
    return lax.psum(jnp.where(mine, x, jnp.zeros_like(x)), axis)


def any_mesh(half_slabs, vir_coeff, occ_energy, vir_energy, plan):
    local_aux = half_slabs.shape[0]
    ohalf = half_slabs.shape[2]
    flat = half_slabs.reshape(local_aux * ohalf, half_slabs.shape[3])
    prod = jnp.dot(flat, vir_coeff, preferred_element_type=F32)
    transformed = prod.reshape(local_aux, ohalf, vir_coeff.shape[1]).astype(BF16)
    owned = lax.all_to_all(transformed, "aux", split_axis=1, concat_axis=0, tiled=True)
    n_half = lax.axis_size("half")
    aux_index = lax.axis_index("aux")
    half_index = lax.axis_index("half")
    o_dev = owned.shape[1]
    n_virt = owned.shape[2]
    own_start = half_index * ohalf + aux_index * o_dev
    occ_e = occ_energy.astype(F32) * 0.001
    own_e = lax.dynamic_slice_in_dim(occ_e, own_start, o_dev)
    vir_e = vir_energy.astype(F32) * 0.001
    gamma = jnp.zeros((o_dev, n_virt, owned.shape[0]), F32)
    energy = jnp.zeros((o_dev,), F32)
    for partner in plan.reshape(-1):
        part_half = partner // ohalf
        part_aux = partner % ohalf // o_dev
        piece = lax.dynamic_index_in_dim(owned, partner % o_dev, 1, keepdims=False)
        other = broadcast(piece, ("aux", "half"), part_aux * n_half + part_half)
        part_e = lax.dynamic_index_in_dim(occ_e, partner, 0, keepdims=False)
        kmat = jnp.einsum("pia,pb->iab", owned, other, preferred_element_type=F32)
        denom = own_e[:, None, None] + part_e - vir_e[None, :, None] - vir_e[None, None, :]
        tilde = (2.0 * kmat - jnp.swapaxes(kmat, 1, 2)) / denom
        energy = energy + jnp.sum(kmat * tilde, axis=(1, 2))
        gamma = gamma + jnp.einsum("iab,pb->iap", tilde.astype(BF16), other, preferred_element_type=F32)
    return gamma.astype(BF16)[None], (energy / (n_virt * n_virt))[None]


def transform_kernel(plan_ref, slab_hbm, coeff_hbm, *rest, n_half, order, joined):
    rest = rest[1:] if joined else rest
    own_hbm, lists = rest[0], rest[1:1 + len(order)]
    slab_v, coeff_v, acc_ref, own_v, in_sem, out_sem = rest[1 + len(order):]
    n_orb, _, _ = own_hbm.shape
    tiles, block, lanes = acc_ref.shape
    rows = block // n_orb
    z = lax.axis_index("half")
    loads, saves = [], []
    coeff_copy = pltpu.make_async_copy(coeff_hbm, coeff_v, in_sem.at[len(order)])
    coeff_copy.start()
    for i, d in enumerate(order):
        at = pl.multiple_of(lax.rem(z + d, n_half) * rows, rows)
        at_flat = pl.multiple_of(at * n_orb, block)
        loads.append(pltpu.make_async_copy(slab_hbm.at[pl.ds(at_flat, block)], slab_v.at[i], in_sem.at[i]))
        saves.append(pltpu.make_async_copy(own_v.at[i], own_hbm.at[:, pl.ds(at, rows)], out_sem.at[i]))
        loads[i].start()
    coeff_copy.wait()
    for i in range(len(order)):
        loads[i].wait()
        acc = jnp.dot(slab_v[i], coeff_v[...], preferred_element_type=F32)
        for t in range(tiles):
            acc_ref[t] = acc[:, t * lanes:(t + 1) * lanes]
        for t in range(tiles):
            cols = slice(t * lanes, (t + 1) * lanes)
            for o in range(n_orb):
                own_v[i, o, :, cols] = acc_ref[t, pl.ds(o, rows, stride=n_orb), :].astype(BF16)
        saves[i].start()
        for k in range(lists[i].shape[0]):
            lists[i][k] = own_v[i, lax.rem(plan_ref[0, k], n_orb)]
    for c in saves:
        c.wait()


def transform(half_slabs, coeff, plan, n_half, order, own=()):
    local_aux, _, n_orb, n_ao = half_slabs.shape
    n_virt = coeff.shape[1]
    count = plan.shape[1]
    rows = local_aux // n_half
    n = len(order)
    hbm = pl.BlockSpec(memory_space=pltpu.HBM)
    vmem = pl.BlockSpec(memory_space=pltpu.VMEM)
    return pl.pallas_call(
        functools.partial(transform_kernel, n_half=n_half, order=order, joined=bool(own)),
        in_specs=[pl.BlockSpec(memory_space=pltpu.SMEM), hbm, hbm] + [hbm] * len(own),
        out_specs=[hbm] + [vmem] * n,
        out_shape=[jax.ShapeDtypeStruct((n_orb, local_aux, n_virt), BF16)]
        + [jax.ShapeDtypeStruct((count, rows, n_virt), BF16)] * n,
        scratch_shapes=[
            pltpu.VMEM((n, rows * n_orb, n_ao), BF16),
            pltpu.VMEM((n_ao, n_virt), BF16),
            pltpu.VMEM((n_virt // 128, rows * n_orb, 128), F32),
            pltpu.VMEM((n, n_orb, rows, n_virt), BF16),
            pltpu.SemaphoreType.DMA((n + 1,)),
            pltpu.SemaphoreType.DMA((n,)),
        ],
        input_output_aliases={3: 0} if own else {},
        compiler_params=pltpu.CompilerParams(vmem_limit_bytes=60 << 20),
        name="transform",
    )(plan, half_slabs.reshape(local_aux * n_orb, n_ao), coeff, *own)


def merge_kernel(plan_ref, *refs, n_orb, n_half):
    lists, outs, sem = refs[:n_half], refs[n_half:-1], refs[-1]
    per = outs[0].shape[0]
    z = lax.axis_index("half")

    def copy(d, s):
        return pltpu.make_async_copy(lists[d].at[s], outs[s // per].at[s % per], sem.at[s])

    for s in range(per * len(outs)):
        far = lax.rem(z - lax.div(plan_ref[0, s], n_orb) + n_half, n_half)
        for d in range(n_half):

            @pl.when(far == d)
            def _():
                copy(d, s).start()

    for s in range(per * len(outs)):
        copy(0, s).wait()


def merge(plan, lists, n_orb, per):
    count, rows, n_virt = lists[0].shape
    shape = jax.ShapeDtypeStruct((per, rows, n_virt), BF16)
    return pl.pallas_call(
        functools.partial(merge_kernel, n_orb=n_orb, n_half=len(lists)),
        in_specs=[pl.BlockSpec(memory_space=pltpu.SMEM)] + [pl.BlockSpec(memory_space=pl.ANY)] * len(lists),
        out_specs=[pl.BlockSpec(memory_space=pltpu.VMEM)] * (count // per),
        out_shape=[shape] * (count // per),
        scratch_shapes=[pltpu.SemaphoreType.DMA((count,))],
        compiler_params=pltpu.CompilerParams(vmem_limit_bytes=4 << 20),
        name="merge",
    )(plan, *lists)


def pack_kernel(*refs):
    parts, out = refs[:-1], refs[-1]
    n_half = len(parts)
    per, sub, _ = parts[0].shape
    z = lax.axis_index("half")
    for d, part in enumerate(parts):
        at = pl.multiple_of(lax.rem(z - d + n_half, n_half) * sub, sub)
        for s in range(per):
            out[s, pl.ds(at, sub)] = part[s]


def pack(parts):
    vmem = pl.BlockSpec(memory_space=pltpu.VMEM)
    per, sub, n_virt = parts[0].shape
    return pl.pallas_call(
        pack_kernel,
        in_specs=[vmem] * len(parts),
        out_specs=vmem,
        out_shape=jax.ShapeDtypeStruct((per, len(parts) * sub, n_virt), BF16),
        compiler_params=pltpu.CompilerParams(vmem_limit_bytes=4 << 20),
        name="pack",
    )(*parts)


def join_kernel(*refs):
    parts, out, sem = refs[:-2], refs[-2], refs[-1]
    copies = [pltpu.make_async_copy(part, out.at[i], sem.at[i]) for i, part in enumerate(parts)]
    for c in copies:
        c.start()
    for c in copies:
        c.wait()


def join(parts):
    return pl.pallas_call(
        join_kernel,
        in_specs=[pl.BlockSpec(memory_space=pl.ANY)] * len(parts),
        out_specs=pl.BlockSpec(memory_space=pltpu.VMEM),
        out_shape=jax.ShapeDtypeStruct((len(parts),) + parts[0].shape, BF16),
        scratch_shapes=[pltpu.SemaphoreType.DMA((len(parts),))],
        compiler_params=pltpu.CompilerParams(vmem_limit_bytes=4 << 20),
        name="join",
    )(*parts)


CORE, X, Y = 1, 2, 4


def prep_kernel(own_hbm, own_t, own_v, sem):
    copy = pltpu.make_async_copy(own_hbm, own_v, sem)
    copy.start()
    copy.wait()
    own_t[...] = jnp.transpose(own_v[...].reshape(own_t.shape[1], own_t.shape[0]))


def prep(own):
    n_src, rows, n_virt = own.shape
    return pl.pallas_call(
        prep_kernel,
        in_specs=[pl.BlockSpec(memory_space=pl.ANY)],
        out_specs=pl.BlockSpec(memory_space=pltpu.VMEM),
        out_shape=jax.ShapeDtypeStruct((n_virt, n_src * rows), BF16),
        scratch_shapes=[pltpu.VMEM(own.shape, BF16), pltpu.SemaphoreType.DMA],
        compiler_params=pltpu.CompilerParams(vmem_limit_bytes=8 << 20),
        name="prep",
    )(own)


def amp_kernel(own_t, early, other, out_ref, part_v, sem):
    _, per, rows, _ = early.shape
    aux = lax.axis_index("aux")
    core = lax.rem(aux, 2)
    half = part_v.shape[1]
    side = lax.rem(aux, Y)
    copies = []
    for src, bits in ((early.at[0], 0), (early.at[1 + core], X), (other.at[0], CORE), (other.at[2 - core], X | CORE)):
        at = pl.multiple_of(lax.bitwise_xor(side, bits) * rows, rows)
        copies.append(pltpu.make_async_copy(src, part_v.at[:, pl.ds(at, rows)], sem.at[len(copies)]))
    for c in copies:
        c.start()
    for c in copies:
        c.wait()
    part = jnp.concatenate([part_v[s] for s in range(per)], axis=1)
    own = own_t[:, pl.ds(pl.multiple_of(lax.div(aux, Y) * half, half), half)]
    out_ref[...] = jnp.dot(own, part, preferred_element_type=F32)


def amplitudes(own, early, other):
    _, per, _, n_virt = early.shape
    n_aux = own.shape[1]
    anym = pl.BlockSpec(memory_space=pl.ANY)
    vmem = pl.BlockSpec(memory_space=pltpu.VMEM)
    return pl.pallas_call(
        amp_kernel,
        in_specs=[vmem, anym, anym],
        out_specs=[vmem, vmem],
        out_shape=[
            jax.ShapeDtypeStruct((n_virt, per * n_virt), F32),
            jax.ShapeDtypeStruct((per, n_aux // 2, n_virt), BF16),
        ],
        scratch_shapes=[pltpu.SemaphoreType.DMA((4,))],
        compiler_params=pltpu.CompilerParams(vmem_limit_bytes=12 << 20),
        cost_estimate=pl.CostEstimate(flops=per * n_virt * n_virt * n_aux, bytes_accessed=3 << 20, transcendentals=0),
        name="amplitudes",
    )(own, early, other)


def pair_kernel(occ_ref, plan_ref, row_ref, col_ref, own_t, *rest, n_orb, groups):
    ins = rest[:4 * groups]
    late, late_other = rest[4 * groups:4 * groups + 2]
    dens_ref, energy_ref, part_v, dens_v, sem, out_sem = rest[4 * groups + 2:]
    _, per, rows, n_virt = late.shape
    half = part_v.shape[1]
    z, aux = lax.axis_index("half"), lax.axis_index("aux")
    core = lax.rem(aux, 2)
    here = pl.multiple_of(lax.div(aux, Y) * half, half)
    there = pl.multiple_of((1 - lax.div(aux, Y)) * half, half)
    side = lax.rem(aux, Y)
    copies = []
    for g in range(groups):
        early, other = ins[4 * g:4 * g + 2]
        for src, bits in (
            (early.at[2 - core], 0),
            (late.at[g], X),
            (other.at[1 + core], CORE),
            (late_other.at[g], X | CORE),
        ):
            at = pl.multiple_of(lax.bitwise_xor(side, bits) * rows, rows)
            dst = part_v.at[pl.ds(g * per, per), pl.ds(at, rows)]
            copies.append(pltpu.make_async_copy(src, dst, sem.at[len(copies)]))
    for c in copies:
        c.start()
    own_e = occ_ref[z * n_orb + aux].astype(F32) * 0.001
    row = row_ref[...].astype(F32) * 0.001
    col = col_ref[...].astype(F32) * 0.001
    energy = jnp.zeros((1, 1), F32)
    for c in copies:
        c.wait()
    tildes = []
    for g in range(groups):
        part = jnp.concatenate([part_v[g * per + s] for s in range(per)], axis=1)
        kk = ins[4 * g + 2][...] + jnp.dot(own_t[:, pl.ds(there, half)], part, preferred_element_type=F32)
        for s in range(per):
            k = kk[:, s * n_virt:(s + 1) * n_virt]
            part_e = occ_ref[plan_ref[0, g * per + s]].astype(F32) * 0.001
            denom = own_e + part_e - col - row
            tilde = (2.0 * k - jnp.transpose(k)) / denom
            energy = energy + jnp.sum(jnp.sum(k * tilde, axis=1, keepdims=True), axis=0, keepdims=True)
            tildes.append(tilde.astype(BF16))
    tb = jnp.concatenate(tildes, axis=1)
    saves = []
    for i, (at, parts) in enumerate((
        (here, [ins[4 * g + 3][s] for g in range(groups) for s in range(per)]),
        (there, [part_v[s] for s in range(groups * per)]),
    )):
        part = jnp.concatenate(parts, axis=1)
        total = lax.dot_general(tb, part, (((1,), (1,)), ((), ())), preferred_element_type=F32)
        dens_v[i] = total.astype(BF16)
        saves.append(pltpu.make_async_copy(dens_v.at[i], dens_ref.at[:, pl.ds(at, half)], out_sem.at[i]))
        saves[-1].start()
    for c in saves:
        c.wait()
    energy_ref[...] = energy / (n_virt * n_virt)


def pair_terms(own, ins, late, late_other, occ, plan, vir, n_orb):
    groups, per, _, n_virt = late.shape
    n_aux = own.shape[1]
    smem = pl.BlockSpec(memory_space=pltpu.SMEM)
    vmem = pl.BlockSpec(memory_space=pltpu.VMEM)
    anym = pl.BlockSpec(memory_space=pl.ANY)
    return pl.pallas_call(
        functools.partial(pair_kernel, n_orb=n_orb, groups=groups),
        in_specs=[smem] * 2 + [vmem] * 3 + [anym, anym, vmem, vmem] * groups + [anym] * 2,
        out_specs=[pl.BlockSpec(memory_space=pltpu.HBM), vmem],
        out_shape=[jax.ShapeDtypeStruct((n_virt, n_aux), BF16), jax.ShapeDtypeStruct((1, 1), F32)],
        scratch_shapes=[
            pltpu.VMEM((groups * per, n_aux // 2, n_virt), BF16),
            pltpu.VMEM((2, n_virt, n_aux // 2), BF16),
            pltpu.SemaphoreType.DMA((groups * 4,)),
            pltpu.SemaphoreType.DMA((2,)),
        ],
        compiler_params=pltpu.CompilerParams(vmem_limit_bytes=24 << 20),
        name="pair_terms",
    )(occ, plan, vir.reshape(1, n_virt), vir.reshape(n_virt, 1), own, *ins, late, late_other)


def swap(x, n):
    return lax.ppermute(x, "aux", [(a, a ^ CORE) for a in range(n)])


def plane(x, n, flip):
    return lax.ppermute(x, "aux", [(a, a ^ (Y if (a & CORE) ^ flip else X)) for a in range(n)])


def shift(x, d, n):
    return lax.ppermute(x, "half", [(h, (h + d) % n) for h in range(n)])


GROUPS = 2
FIRST = (1, 2, 3, 0)


def on_device(half_slabs, vir_coeff, occ_energy, vir_energy, plan):
    return stages(half_slabs, vir_coeff, occ_energy, vir_energy, plan)


def stages(half_slabs, vir_coeff, occ_energy, vir_energy, plan):
    n_aux = lax.axis_size("aux")
    n_half = lax.axis_size("half")
    _, _, ohalf, _ = half_slabs.shape
    count = plan.size
    per = count // GROUPS
    own8, *lists_0 = transform(half_slabs, vir_coeff, plan, n_half, FIRST)
    lists = dict(zip(FIRST, lists_0))
    got = [lists[0]]
    for d in range(1, n_half):
        got.append(shift(lists[d], d, n_half))
    own = lax.all_to_all(own8, "aux", split_axis=0, concat_axis=0, tiled=True)
    own = prep(own)
    mine = merge(plan, got, ohalf, per)
    ins, late = [], []
    for g in range(GROUPS):
        parts = [mine[g]]
        for d in range(1, n_half):
            parts.append(shift(mine[g], d, n_half))
        z0 = pack(parts)
        r1 = plane(z0, n_aux, 0)
        r2 = plane(z0, n_aux, 1)
        late.append(plane(r1, n_aux, 1))
        early = join([z0, r1, r2])
        other = swap(early, n_aux)
        ins += [early, other, *amplitudes(own, early, other)]
    late = join(late)
    late_other = swap(late, n_aux)
    density, energy = pair_terms(own, ins, late, late_other, occ_energy, plan, vir_energy, ohalf)
    return density[None, None], energy


def solution(mesh):
    fast = dict(mesh.shape) == {"aux": 8, "half": 4}
    in_specs = (P("aux", "half", None, None), P(), P(), P(), P())
    out_specs = (P("half", "aux", None, None), P("half", "aux"))
    return jax.shard_map(
        on_device if fast else any_mesh, mesh=mesh, in_specs=in_specs, out_specs=out_specs, check_vma=False
    )
```

time: 240 us -> 85.5 us (0.36)
  waiting for transfers between devices: 141 us -> 31.2 us
  between operations: 38.3 us -> 0.83 us
  starting transfers between devices: 5.37 us -> 30.3 us
  matrix products: 24.7 us -> 0 us
  Pallas kernels: 0 us -> 19.5 us
  local copies, waits for them, and re-layouts: 17.6 us -> 3.39 us
  other arithmetic: 11.8 us -> 0 us
    psum x1 -> x0, waiting for transfers between devices: 135 us -> none  [broadcast(): return lax.psum(jnp.where(mine, x, jnp.zeros_like(x)), axis)]
    ppermute x0 -> x18, waiting for transfers between devices: none -> 31.2 us  [the longest x6 17.6 us: plane(): lax.ppermute(x, 'aux', [(a, a ^ (Y if a & CORE ^ flip else X)) for a in r...]
    ppermute x0 -> x18, starting transfers between devices: none -> 26.7 us  [the longest x9 18.1 us: shift(): return lax.ppermute(x, 'half', [(h, (h + d) % n) for h in range(n)])]
    dot_general x9 -> x0, matrix products: 24.7 us -> none  [the longest x4 12.7 us: on_device(): jnp.einsum('pia,pb->iab', owned, other, preferred_element_type=jnp.float32)]
    pallas_call x0 -> x11, Pallas kernels: none -> 19.5 us  [the longest x1 6.46 us: pair_terms(): pl.pallas_call(functools.partial(pair_kernel, n_orb=n_orb, groups=groups)...]
    all_to_all x1, waiting for transfers between devices: 6.05 us -> 0.01 us  [stages(): own = lax.all_to_all(own8, 'aux', split_axis=0, concat_axis=0, tiled=True)]
    sub x3 -> x0, other arithmetic: 4.28 us -> none  [the longest x2 4.28 us: on_device(): tilde = (2.0 * kmat - jnp.swapaxes(kmat, 1, 2)) / denom]
    transpose x2 -> x0, local copies, waits for them, and re-layouts: 4.27 us -> none  [on_device(): tilde = (2.0 * kmat - jnp.swapaxes(kmat, 1, 2)) / denom]
  transfers between devices with their start and end apart: 2 -> 19, of which waited for: 2 -> 8; matrix products, arithmetic and copies ran while one was open for 1% -> 1% of each run, Pallas kernels for 0% -> 7%
where the time goes in v1:
time: 85.5 us; the launch traced here: 85.2 us
  waiting for transfers between devices  31.2 us (36%)
  starting transfers between devices  30.3 us (35%)
  Pallas kernels  19.5 us (23%)
  local copies, waits for them, and re-layouts  3.39 us (4%)
    ppermute x9, starting transfers between devices, shift(): return lax.ppermute(x, 'half', [(h, (h + d) % n) for h in range(n)])  18.1 us
    ppermute x6, waiting for transfers between devices, plane(): lax.ppermute(x, 'aux', [(a, a ^ (Y if a & CORE ^ flip else X)) for a in r...  17.6 us
    ppermute x9, waiting for transfers between devices, shift(): return lax.ppermute(x, 'half', [(h, (h + d) % n) for h in range(n)])  13.5 us
    ppermute x6, starting transfers between devices, plane(): lax.ppermute(x, 'aux', [(a, a ^ (Y if a & CORE ^ flip else X)) for a in r...  7.62 us
    pallas_call x1, Pallas kernels, pair_terms(): pl.pallas_call(functools.partial(pair_kernel, n_orb=n_orb, groups=groups)...  6.46 us
    pallas_call x1, Pallas kernels, transform(): pl.pallas_call(functools.partial(transform_kernel, n_half=n_half, order=o...  6.34 us
    pallas_call x2, Pallas kernels, amplitudes(): pl.pallas_call(amp_kernel, in_specs=[vmem, anym, anym], out_specs=[vmem,...  3.65 us
    all_to_all x1, starting transfers between devices, stages(): own = lax.all_to_all(own8, 'aux', split_axis=0, concat_axis=0, tiled=True)  3.56 us
  transfers between devices with their start and end apart: 19, of which 8 were waited for; matrix products, arithmetic and copies ran while one was open for 1% of the time, Pallas kernels for 7%

profile of v1, /device:TPU:0, one launch (start us, length us, event | category | flops | bytes accessed | tf_op | source)
XLA Modules:
  0.0 85.2 jit_solution(16748114317377169945)
XLA Ops:
  0.6 6.3 %transform.1 = (bf16[8,192,384]{2,1,0:T(8,128)(2,1)}, bf16[4,48,384]{2,1,0:T(8,128)(2,1)}, bf16[4,48,384]{2,1,0:T(8,128)(2,1)}, bf16[4,48,384]{2,1,0:T(8,128)(2,1)}, bf16[4,48,384]{2,1,0:T(8,128)(2,1)}) custom-call(s32[1,4]{1,0:T(1,128)} %plan_ref.5, bf16[1536,960]{1,0:T(8,128)(2,1)} %bitcast.2, bf16[960,384]{1,0:T(8,128)(2,1)} %coeff_hbm.1), custom_call_target="tpu_custom_call" | custom-call | tf_op jit(solution)/shard_map/transform/pallas_call | solution.py:94
  7.0 3.1 %collective-permute-start = (bf16[4,48,384]{2,1,0:T(8,128)(2,1)}, bf16[4,48,384]{2,1,0:T(8,128)(2,1)S(1)}, u32[]{:S(2)}, u32[]{:S(2)}) collective-permute-start(bf16[4,48,384]{2,1,0:T(8,128)(2,1)} %get-tuple-element.17), channel_id=1, source_target_pairs={{0,1},{1,2},{2,3},{3,0},{4,5},{5,6},{6,7},{7,4},{8,9},{9,10},{10,1... | collective-permute-start | bytes 442376 | tf_op jit(solution)/shard_map/ppermute | solution.py:344
  10.1 2.6 %collective-permute-start.1 = (bf16[4,48,384]{2,1,0:T(8,128)(2,1)}, bf16[4,48,384]{2,1,0:T(8,128)(2,1)S(1)}, u32[]{:S(2)}, u32[]{:S(2)}) collective-permute-start(bf16[4,48,384]{2,1,0:T(8,128)(2,1)} %get-tuple-element.18), channel_id=1, source_target_pairs={{0,2},{1,3},{2,0},{3,1},{4,6},{5,7},{6,4},{7,5},{8,10},{9,11},{10,... | collective-permute-start | bytes 442376 | tf_op jit(solution)/shard_map/ppermute | solution.py:344
  12.7 1.3 %collective-permute-start.2 = (bf16[4,48,384]{2,1,0:T(8,128)(2,1)}, bf16[4,48,384]{2,1,0:T(8,128)(2,1)S(1)}, u32[]{:S(2)}, u32[]{:S(2)}) collective-permute-start(bf16[4,48,384]{2,1,0:T(8,128)(2,1)} %get-tuple-element.19), channel_id=1, source_target_pairs={{0,3},{1,0},{2,1},{3,2},{4,7},{5,4},{6,5},{7,6},{8,11},{9,8},{10,9... | collective-permute-start | bytes 442376 | tf_op jit(solution)/shard_map/ppermute | solution.py:344
  14.0 3.1 %collective-permute-done.refs_1_ = bf16[4,48,384]{2,1,0:T(8,128)(2,1)S(1)} collective-permute-done((bf16[4,48,384]{2,1,0:T(8,128)(2,1)}, bf16[4,48,384]{2,1,0:T(8,128)(2,1)S(1)}, u32[]{:S(2)}, u32[]{:S(2)}) %collective-permute-start) | collective-permute-done | bytes 147488 | tf_op jit(solution)/shard_map/ppermute | solution.py:344
  17.1 5.5 %collective-permute-done.1.refs_2_ = bf16[4,48,384]{2,1,0:T(8,128)(2,1)S(1)} collective-permute-done((bf16[4,48,384]{2,1,0:T(8,128)(2,1)}, bf16[4,48,384]{2,1,0:T(8,128)(2,1)S(1)}, u32[]{:S(2)}, u32[]{:S(2)}) %collective-permute-start.1) | collective-permute-done | bytes 147488 | tf_op jit(solution)/shard_map/ppermute | solution.py:344
  22.6 0.9 %copy-done.3 = bf16[4,48,384]{2,1,0:T(8,128)(2,1)S(1)} copy-done((bf16[4,48,384]{2,1,0:T(8,128)(2,1)S(1)}, bf16[4,48,384]{2,1,0:T(8,128)(2,1)}, u32[]{:S(2)}) %copy-start.3) | copy-done | bytes 147480
  23.5 0.9 %merge.1 = (bf16[2,48,384]{2,1,0:T(8,128)(2,1)S(1)}, bf16[2,48,384]{2,1,0:T(8,128)(2,1)S(1)}) custom-call(s32[1,4]{1,0:T(1,128)S(1)} %copy-done.4, bf16[4,48,384]{2,1,0:T(8,128)(2,1)S(1)} %copy-done.3, bf16[4,48,384]{2,1,0:T(8,128)(2,1)S(1)} %collective-permute-done.refs_1_, bf16[4,48,384]{2,1,0:T(8,128)(2,1)S(1)} %collective-permute-done.1.refs_2_, ...), custom_call_target="tpu_custom_call" | custom-call | tf_op jit(solution)/shard_map/merge/pallas_call | solution.py:137
  24.4 4.7 %collective-permute-start.11 = (bf16[2,48,384]{2,1,0:T(8,128)(2,1)S(1)}, bf16[2,48,384]{2,1,0:T(8,128)(2,1)S(1)}, u32[]{:S(2)}, u32[]{:S(2)}) collective-permute-start(bf16[2,48,384]{2,1,0:T(8,128)(2,1)S(1)} %get-tuple-element.23.refs_0_), channel_id=1, source_target_pairs={{0,3},{1,0},{2,1},{3,2},{4,7},{5,4},{6,5},{7,6},{8,11},{9,8},{10,9... | collective-permute-start | bytes 221192 | tf_op jit(solution)/shard_map/ppermute | solution.py:344
  29.8 3.6 %collective-permute-start.5 = (bf16[2,48,384]{2,1,0:T(8,128)(2,1)S(1)}, bf16[2,48,384]{2,1,0:T(8,128)(2,1)S(1)}, u32[]{:S(2)}, u32[]{:S(2)}) collective-permute-start(bf16[2,48,384]{2,1,0:T(8,128)(2,1)S(1)} %get-tuple-element.20.refs_0_), channel_id=1, source_target_pairs={{0,3},{1,0},{2,1},{3,2},{4,7},{5,4},{6,5},{7,6},{8,11},{9,8},{10,9... | collective-permute-start | bytes 221192 | tf_op jit(solution)/shard_map/ppermute | solution.py:344
  33.4 0.7 collective-permute-start.4
  34.1 1.3 %collective-permute-start.3 = (bf16[2,48,384]{2,1,0:T(8,128)(2,1)S(1)}, bf16[2,48,384]{2,1,0:T(8,128)(2,1)S(1)}, u32[]{:S(2)}, u32[]{:S(2)}) collective-permute-start(bf16[2,48,384]{2,1,0:T(8,128)(2,1)S(1)} %get-tuple-element.20.refs_0_), channel_id=1, source_target_pairs={{0,1},{1,2},{2,3},{3,0},{4,5},{5,6},{6,7},{7,4},{8,9},{9,10},{10,1... | collective-permute-start | bytes 221192 | tf_op jit(solution)/shard_map/ppermute | solution.py:344
  35.5 5.0 %collective-permute-done.10.refs_2_ = bf16[2,48,384]{2,1,0:T(8,128)(2,1)S(1)} collective-permute-done((bf16[2,48,384]{2,1,0:T(8,128)(2,1)S(1)}, bf16[2,48,384]{2,1,0:T(8,128)(2,1)S(1)}, u32[]{:S(2)}, u32[]{:S(2)}) %collective-permute-start.10) | collective-permute-done | bytes 73760 | tf_op jit(solution)/shard_map/ppermute | solution.py:344
  40.5 1.6 %collective-permute-start.13 = (bf16[2,192,384]{2,1,0:T(8,128)(2,1)S(1)}, bf16[2,192,384]{2,1,0:T(8,128)(2,1)S(1)}, u32[]{:S(2)}, u32[]{:S(2)}) collective-permute-start(bf16[2,192,384]{2,1,0:T(8,128)(2,1)S(1)} %pack.3.refs_0_), channel_id=1, source_target_pairs={{0,16},{4,12},{8,24},{12,4},{16,0},{20,28},{24,8},{28,20},{1,17},{... | collective-permute-start | bytes 884744 | tf_op jit(solution)/shard_map/ppermute | solution.py:340
  42.0 1.5 %collective-permute-start.12 = (bf16[2,192,384]{2,1,0:T(8,128)(2,1)S(1)}, bf16[2,192,384]{2,1,0:T(8,128)(2,1)S(1)}, u32[]{:S(2)}, u32[]{:S(2)}) collective-permute-start(bf16[2,192,384]{2,1,0:T(8,128)(2,1)S(1)} %pack.3.refs_0_), channel_id=1, source_target_pairs={{0,8},{4,20},{8,0},{12,28},{16,24},{20,4},{24,16},{28,12},{1,9},{5... | collective-permute-start | bytes 884744 | tf_op jit(solution)/shard_map/ppermute | solution.py:340
  43.6 1.0 %collective-permute-start.7 = (bf16[2,192,384]{2,1,0:T(8,128)(2,1)S(1)}, bf16[2,192,384]{2,1,0:T(8,128)(2,1)}, u32[]{:S(2)}, u32[]{:S(2)}) collective-permute-start(bf16[2,192,384]{2,1,0:T(8,128)(2,1)S(1)} %pack.2.refs_0_), channel_id=1, source_target_pairs={{0,16},{4,12},{8,24},{12,4},{16,0},{20,28},{24,8},{28,20},{1,17},{... | collective-permute-start | bytes 884744 | tf_op jit(solution)/shard_map/ppermute | solution.py:340
  44.6 1.5 %collective-permute-start.6 = (bf16[2,192,384]{2,1,0:T(8,128)(2,1)S(1)}, bf16[2,192,384]{2,1,0:T(8,128)(2,1)S(1)}, u32[]{:S(2)}, u32[]{:S(2)}) collective-permute-start(bf16[2,192,384]{2,1,0:T(8,128)(2,1)S(1)} %pack.2.refs_0_), channel_id=1, source_target_pairs={{0,8},{4,20},{8,0},{12,28},{16,24},{20,4},{24,16},{28,12},{1,9},{5... | collective-permute-start | bytes 884744 | tf_op jit(solution)/shard_map/ppermute | solution.py:340
  46.1 3.6 %all-to-all-start = ((bf16[8,192,384]{2,1,0:T(8,128)(2,1)}), bf16[8,192,384]{2,1,0:T(8,128)(2,1)S(1)}, u32[]{:S(2)}, u32[]{:S(2)}) async-start(bf16[8,192,384]{2,1,0:T(8,128)(2,1)} %get-tuple-element.15), calls=%async_computation | async-start | bytes 2359296 | tf_op jit(solution)/shard_map/all_to_all | solution.py:366
  49.6 1.8 %collective-permute-done.12.refs_1_ = bf16[2,192,384]{2,1,0:T(8,128)(2,1)S(1)} collective-permute-done((bf16[2,192,384]{2,1,0:T(8,128)(2,1)S(1)}, bf16[2,192,384]{2,1,0:T(8,128)(2,1)S(1)}, u32[]{:S(2)}, u32[]{:S(2)}) %collective-permute-start.12) | collective-permute-done | bytes 294944 | tf_op jit(solution)/shard_map/ppermute | solution.py:340
  51.7 2.8 %collective-permute-done.7.refs_2_ = bf16[2,192,384]{2,1,0:T(8,128)(2,1)} collective-permute-done((bf16[2,192,384]{2,1,0:T(8,128)(2,1)S(1)}, bf16[2,192,384]{2,1,0:T(8,128)(2,1)}, u32[]{:S(2)}, u32[]{:S(2)}) %collective-permute-start.7) | collective-permute-done | bytes 294944 | tf_op jit(solution)/shard_map/ppermute | solution.py:340
  54.5 2.0 %collective-permute-done.6.refs_1_ = bf16[2,192,384]{2,1,0:T(8,128)(2,1)S(1)} collective-permute-done((bf16[2,192,384]{2,1,0:T(8,128)(2,1)S(1)}, bf16[2,192,384]{2,1,0:T(8,128)(2,1)S(1)}, u32[]{:S(2)}, u32[]{:S(2)}) %collective-permute-start.6) | collective-permute-done | bytes 294944 | tf_op jit(solution)/shard_map/ppermute | solution.py:340
  56.5 0.7 copy-done.1
  57.3 1.0 %copy-done.2 = bf16[2,192,384]{2,1,0:T(8,128)(2,1)S(1)} copy-done((bf16[2,192,384]{2,1,0:T(8,128)(2,1)S(1)}, bf16[2,192,384]{2,1,0:T(8,128)(2,1)}, u32[]{:S(2)}) %copy-start.2) | copy-done | bytes 294936
  58.2 1.1 %join.3.early.rest_0_ = bf16[3,2,192,384]{3,2,1,0:T(8,128)(2,1)S(1)} custom-call(bf16[2,192,384]{2,1,0:T(8,128)(2,1)S(1)} %pack.2.refs_0_, bf16[2,192,384]{2,1,0:T(8,128)(2,1)S(1)} %copy-done.2, bf16[2,192,384]{2,1,0:T(8,128)(2,1)} %collective-permute-done.7.refs_2_), custom_call_target="tpu_custom_call" | custom-call | tf_op jit(solution)/shard_map/join/pallas_call | solution.py:182
  59.9 1.6 %collective-permute-start.15 = (bf16[2,192,384]{2,1,0:T(8,128)(2,1)S(1)}, bf16[2,192,384]{2,1,0:T(8,128)(2,1)S(1)}, u32[]{:S(2)}, u32[]{:S(2)}) collective-permute-start(bf16[2,192,384]{2,1,0:T(8,128)(2,1)S(1)} %copy-done.2), channel_id=1, source_target_pairs={{0,16},{4,12},{8,24},{12,4},{16,0},{20,28},{24,8},{28,20},{1,17},{... | collective-permute-start | bytes 884744 | tf_op jit(solution)/shard_map/ppermute | solution.py:340
  61.5 7.9 %collective-permute-done.16.refs_1_ = bf16[2,192,384]{2,1,0:T(8,128)(2,1)S(1)} collective-permute-done((bf16[2,192,384]{2,1,0:T(8,128)(2,1)S(1)}, bf16[2,192,384]{2,1,0:T(8,128)(2,1)S(1)}, u32[]{:S(2)}, u32[]{:S(2)}) %collective-permute-start.16) | collective-permute-done | bytes 294944 | tf_op jit(solution)/shard_map/ppermute | solution.py:340
  69.4 3.2 %collective-permute-done.15.refs_0_ = bf16[2,192,384]{2,1,0:T(8,128)(2,1)S(1)} collective-permute-done((bf16[2,192,384]{2,1,0:T(8,128)(2,1)S(1)}, bf16[2,192,384]{2,1,0:T(8,128)(2,1)S(1)}, u32[]{:S(2)}, u32[]{:S(2)}) %collective-permute-start.15) | collective-permute-done | bytes 294944 | tf_op jit(solution)/shard_map/ppermute | solution.py:340
  72.7 0.9 %collective-permute-start.17 = (bf16[2,2,192,384]{3,2,1,0:T(8,128)(2,1)S(1)}, bf16[2,2,192,384]{3,2,1,0:T(8,128)(2,1)}, u32[]{:S(2)}, u32[]{:S(2)}) collective-permute-start(bf16[2,2,192,384]{3,2,1,0:T(8,128)(2,1)S(1)} %join.5.rest_8_), channel_id=1, source_target_pairs={{0,4},{4,0},{8,12},{12,8},{16,20},{20,16},{24,28},{28,24},{1,5},{5... | collective-permute-start | bytes 1769480 | tf_op jit(solution)/shard_map/ppermute | solution.py:336
  73.6 0.8 reshape.16.col_ref
  75.0 1.8 %amplitudes.3 = (f32[384,768]{1,0:T(8,128)S(1)}, bf16[2,768,384]{2,1,0:T(8,128)(2,1)S(1)}) custom-call(bf16[384,1536]{1,0:T(8,128)(2,1)S(1)} %prep.1.own_t, bf16[3,2,192,384]{3,2,1,0:T(8,128)(2,1)S(1)} %join.4.early.rest_4_, bf16[3,2,192,384]{3,2,1,0:T(8,128)(2,1)} %collective-permute-done.14.other.rest_5_), custom_call_target="tpu_custom_call" | custom-call | flops 452984832 | bytes 3145728 | tf_op jit(solution)/shard_map/amplitudes/pallas_call | solution.py:240
  76.9 1.8 %amplitudes.2 = (f32[384,768]{1,0:T(8,128)S(1)}, bf16[2,768,384]{2,1,0:T(8,128)(2,1)S(1)}) custom-call(bf16[384,1536]{1,0:T(8,128)(2,1)S(1)} %prep.1.own_t, bf16[3,2,192,384]{3,2,1,0:T(8,128)(2,1)S(1)} %join.3.early.rest_0_, bf16[3,2,192,384]{3,2,1,0:T(8,128)(2,1)} %collective-permute-done.8.other.rest_1_), custom_call_target="tpu_custom_call" | custom-call | flops 452984832 | bytes 3145728 | tf_op jit(solution)/shard_map/amplitudes/pallas_call | solution.py:240
  78.7 6.5 %pair_terms.1 = (bf16[384,1536]{1,0:T(8,128)(2,1)}, f32[1,1]{1,0:T(1,128)}) custom-call(s32[32]{0:T(128)S(1)} %copy-done.5, s32[1,4]{1,0:T(1,128)S(1)} %copy-done.4, s32[1,384]{1,0:T(1,128)S(1)} %reshape.13.row_ref, s32[384,1]{1,0:T(8,128)S(1)} %copy-done, bf16[384,1536]{1,0:T(8,128)(2,1)S(1)} %prep.1.own_t, bf16[3,2,192,384]{3,2,1,0:T(8,128)(2,1)S(1)} %join.3.early.rest_0_, ...), custom_call_target="tpu_custom_call" | custom-call | tf_op jit(solution)/shard_map/pair_terms/pallas_call | solution.py:319
  (33 shorter events, 2.4 us)
Async XLA Ops:
  0.6 22.0 %copy-start.4 = (s32[1,4]{1,0:T(1,128)S(1)}, s32[1,4]{1,0:T(1,128)}, u32[]{:S(2)}) copy-start(s32[1,4]{1,0:T(1,128)} %plan_ref.5) | copy-start | bytes 52
  7.0 10.1 %collective-permute-start = (bf16[4,48,384]{2,1,0:T(8,128)(2,1)}, bf16[4,48,384]{2,1,0:T(8,128)(2,1)S(1)}, u32[]{:S(2)}, u32[]{:S(2)}) collective-permute-start(bf16[4,48,384]{2,1,0:T(8,128)(2,1)} %get-tuple-element.17), channel_id=1, source_target_pairs={{0,1},{1,2},{2,3},{3,0},{4,5},{5,6},{6,7},{7,4},{8,9},{9,10},{10,1... | collective-permute-start | bytes 442376 | tf_op jit(solution)/shard_map/ppermute | solution.py:344
  10.1 12.5 %collective-permute-start.1 = (bf16[4,48,384]{2,1,0:T(8,128)(2,1)}, bf16[4,48,384]{2,1,0:T(8,128)(2,1)S(1)}, u32[]{:S(2)}, u32[]{:S(2)}) collective-permute-start(bf16[4,48,384]{2,1,0:T(8,128)(2,1)} %get-tuple-element.18), channel_id=1, source_target_pairs={{0,2},{1,3},{2,0},{3,1},{4,6},{5,7},{6,4},{7,5},{8,10},{9,11},{10,... | collective-permute-start | bytes 442376 | tf_op jit(solution)/shard_map/ppermute | solution.py:344
  12.7 9.9 %collective-permute-start.2 = (bf16[4,48,384]{2,1,0:T(8,128)(2,1)}, bf16[4,48,384]{2,1,0:T(8,128)(2,1)S(1)}, u32[]{:S(2)}, u32[]{:S(2)}) collective-permute-start(bf16[4,48,384]{2,1,0:T(8,128)(2,1)} %get-tuple-element.19), channel_id=1, source_target_pairs={{0,3},{1,0},{2,1},{3,2},{4,7},{5,4},{6,5},{7,6},{8,11},{9,8},{10,9... | collective-permute-start | bytes 442376 | tf_op jit(solution)/shard_map/ppermute | solution.py:344
  22.6 0.9 %copy-start.3 = (bf16[4,48,384]{2,1,0:T(8,128)(2,1)S(1)}, bf16[4,48,384]{2,1,0:T(8,128)(2,1)}, u32[]{:S(2)}) copy-start(bf16[4,48,384]{2,1,0:T(8,128)(2,1)} %get-tuple-element.16.refs_0_) | copy-start | bytes 442372
  24.4 9.7 %collective-permute-start.11 = (bf16[2,48,384]{2,1,0:T(8,128)(2,1)S(1)}, bf16[2,48,384]{2,1,0:T(8,128)(2,1)S(1)}, u32[]{:S(2)}, u32[]{:S(2)}) collective-permute-start(bf16[2,48,384]{2,1,0:T(8,128)(2,1)S(1)} %get-tuple-element.23.refs_0_), channel_id=1, source_target_pairs={{0,3},{1,0},{2,1},{3,2},{4,7},{5,4},{6,5},{7,6},{8,11},{9,8},{10,9... | collective-permute-start | bytes 221192 | tf_op jit(solution)/shard_map/ppermute | solution.py:344
  29.1 11.3 %collective-permute-start.10 = (bf16[2,48,384]{2,1,0:T(8,128)(2,1)S(1)}, bf16[2,48,384]{2,1,0:T(8,128)(2,1)S(1)}, u32[]{:S(2)}, u32[]{:S(2)}) collective-permute-start(bf16[2,48,384]{2,1,0:T(8,128)(2,1)S(1)} %get-tuple-element.23.refs_0_), channel_id=1, source_target_pairs={{0,2},{1,3},{2,0},{3,1},{4,6},{5,7},{6,4},{7,5},{8,10},{9,11},{10,... | collective-permute-start | bytes 221192 | tf_op jit(solution)/shard_map/ppermute | solution.py:344
  29.5 10.9 %collective-permute-start.9 = (bf16[2,48,384]{2,1,0:T(8,128)(2,1)S(1)}, bf16[2,48,384]{2,1,0:T(8,128)(2,1)S(1)}, u32[]{:S(2)}, u32[]{:S(2)}) collective-permute-start(bf16[2,48,384]{2,1,0:T(8,128)(2,1)S(1)} %get-tuple-element.23.refs_0_), channel_id=1, source_target_pairs={{0,1},{1,2},{2,3},{3,0},{4,5},{5,6},{6,7},{7,4},{8,9},{9,10},{10,1... | collective-permute-start | bytes 221192 | tf_op jit(solution)/shard_map/ppermute | solution.py:344
  29.8 13.7 %collective-permute-start.5 = (bf16[2,48,384]{2,1,0:T(8,128)(2,1)S(1)}, bf16[2,48,384]{2,1,0:T(8,128)(2,1)S(1)}, u32[]{:S(2)}, u32[]{:S(2)}) collective-permute-start(bf16[2,48,384]{2,1,0:T(8,128)(2,1)S(1)} %get-tuple-element.20.refs_0_), channel_id=1, source_target_pairs={{0,3},{1,0},{2,1},{3,2},{4,7},{5,4},{6,5},{7,6},{8,11},{9,8},{10,9... | collective-permute-start | bytes 221192 | tf_op jit(solution)/shard_map/ppermute | solution.py:344
  33.4 10.2 %collective-permute-start.4 = (bf16[2,48,384]{2,1,0:T(8,128)(2,1)S(1)}, bf16[2,48,384]{2,1,0:T(8,128)(2,1)S(1)}, u32[]{:S(2)}, u32[]{:S(2)}) collective-permute-start(bf16[2,48,384]{2,1,0:T(8,128)(2,1)S(1)} %get-tuple-element.20.refs_0_), channel_id=1, source_target_pairs={{0,2},{1,3},{2,0},{3,1},{4,6},{5,7},{6,4},{7,5},{8,10},{9,11},{10,... | collective-permute-start | bytes 221192 | tf_op jit(solution)/shard_map/ppermute | solution.py:344
  34.1 9.4 %collective-permute-start.3 = (bf16[2,48,384]{2,1,0:T(8,128)(2,1)S(1)}, bf16[2,48,384]{2,1,0:T(8,128)(2,1)S(1)}, u32[]{:S(2)}, u32[]{:S(2)}) collective-permute-start(bf16[2,48,384]{2,1,0:T(8,128)(2,1)S(1)} %get-tuple-element.20.refs_0_), channel_id=1, source_target_pairs={{0,1},{1,2},{2,3},{3,0},{4,5},{5,6},{6,7},{7,4},{8,9},{9,10},{10,1... | collective-permute-start | bytes 221192 | tf_op jit(solution)/shard_map/ppermute | solution.py:344
  40.5 9.2 %collective-permute-start.13 = (bf16[2,192,384]{2,1,0:T(8,128)(2,1)S(1)}, bf16[2,192,384]{2,1,0:T(8,128)(2,1)S(1)}, u32[]{:S(2)}, u32[]{:S(2)}) collective-permute-start(bf16[2,192,384]{2,1,0:T(8,128)(2,1)S(1)} %pack.3.refs_0_), channel_id=1, source_target_pairs={{0,16},{4,12},{8,24},{12,4},{16,0},{20,28},{24,8},{28,20},{1,17},{... | collective-permute-start | bytes 884744 | tf_op jit(solution)/shard_map/ppermute | solution.py:340
  42.0 9.4 %collective-permute-start.12 = (bf16[2,192,384]{2,1,0:T(8,128)(2,1)S(1)}, bf16[2,192,384]{2,1,0:T(8,128)(2,1)S(1)}, u32[]{:S(2)}, u32[]{:S(2)}) collective-permute-start(bf16[2,192,384]{2,1,0:T(8,128)(2,1)S(1)} %pack.3.refs_0_), channel_id=1, source_target_pairs={{0,8},{4,20},{8,0},{12,28},{16,24},{20,4},{24,16},{28,12},{1,9},{5... | collective-permute-start | bytes 884744 | tf_op jit(solution)/shard_map/ppermute | solution.py:340
  43.6 10.9 %collective-permute-start.7 = (bf16[2,192,384]{2,1,0:T(8,128)(2,1)S(1)}, bf16[2,192,384]{2,1,0:T(8,128)(2,1)}, u32[]{:S(2)}, u32[]{:S(2)}) collective-permute-start(bf16[2,192,384]{2,1,0:T(8,128)(2,1)S(1)} %pack.2.refs_0_), channel_id=1, source_target_pairs={{0,16},{4,12},{8,24},{12,4},{16,0},{20,28},{24,8},{28,20},{1,17},{... | collective-permute-start | bytes 884744 | tf_op jit(solution)/shard_map/ppermute | solution.py:340
  44.6 12.0 %collective-permute-start.6 = (bf16[2,192,384]{2,1,0:T(8,128)(2,1)S(1)}, bf16[2,192,384]{2,1,0:T(8,128)(2,1)S(1)}, u32[]{:S(2)}, u32[]{:S(2)}) collective-permute-start(bf16[2,192,384]{2,1,0:T(8,128)(2,1)S(1)} %pack.2.refs_0_), channel_id=1, source_target_pairs={{0,8},{4,20},{8,0},{12,28},{16,24},{20,4},{24,16},{28,12},{1,9},{5... | collective-permute-start | bytes 884744 | tf_op jit(solution)/shard_map/ppermute | solution.py:340
  46.1 28.3 %all-to-all-start = ((bf16[8,192,384]{2,1,0:T(8,128)(2,1)}), bf16[8,192,384]{2,1,0:T(8,128)(2,1)S(1)}, u32[]{:S(2)}, u32[]{:S(2)}) async-start(bf16[8,192,384]{2,1,0:T(8,128)(2,1)} %get-tuple-element.15), calls=%async_computation | async-start | bytes 2359296 | tf_op jit(solution)/shard_map/all_to_all | solution.py:366
  51.4 22.2 %copy-start.6 = (s32[384]{0:T(512)S(1)}, s32[384]{0:T(512)}, u32[]{:S(2)}) copy-start(s32[384]{0:T(512)} %param.8) | copy-start | bytes 4612
  51.6 23.4 %collective-permute-start.14 = (bf16[3,2,192,384]{3,2,1,0:T(8,128)(2,1)S(1)}, bf16[3,2,192,384]{3,2,1,0:T(8,128)(2,1)}, u32[]{:S(2)}, u32[]{:S(2)}) collective-permute-start(bf16[3,2,192,384]{3,2,1,0:T(8,128)(2,1)S(1)} %join.4.early.rest_4_), channel_id=1, source_target_pairs={{0,4},{4,0},{8,12},{12,8},{16,20},{20,16},{24,28},{28,24},{1,5},{5... | collective-permute-start | bytes 2654216 | tf_op jit(solution)/shard_map/ppermute | solution.py:336
  56.5 0.7 copy-start.1
  57.3 1.0 %copy-start.2 = (bf16[2,192,384]{2,1,0:T(8,128)(2,1)S(1)}, bf16[2,192,384]{2,1,0:T(8,128)(2,1)}, u32[]{:S(2)}) copy-start(bf16[2,192,384]{2,1,0:T(8,128)(2,1)} %copy-done.1) | copy-start | bytes 884740
  59.3 17.5 %collective-permute-start.8 = (bf16[3,2,192,384]{3,2,1,0:T(8,128)(2,1)S(1)}, bf16[3,2,192,384]{3,2,1,0:T(8,128)(2,1)}, u32[]{:S(2)}, u32[]{:S(2)}) collective-permute-start(bf16[3,2,192,384]{3,2,1,0:T(8,128)(2,1)S(1)} %join.3.early.rest_0_), channel_id=1, source_target_pairs={{0,4},{4,0},{8,12},{12,8},{16,20},{20,16},{24,28},{28,24},{1,5},{5... | collective-permute-start | bytes 2654216 | tf_op jit(solution)/shard_map/ppermute | solution.py:336
  59.4 10.0 %collective-permute-start.16 = (bf16[2,192,384]{2,1,0:T(8,128)(2,1)S(1)}, bf16[2,192,384]{2,1,0:T(8,128)(2,1)S(1)}, u32[]{:S(2)}, u32[]{:S(2)}) collective-permute-start(bf16[2,192,384]{2,1,0:T(8,128)(2,1)S(1)} %collective-permute-done.12.refs_1_), channel_id=1, source_target_pairs={{0,16},{4,12},{8,24},{12,4},{16,0},{20,28},{24,8},{28,20},{1,17},{... | collective-permute-start | bytes 884744 | tf_op jit(solution)/shard_map/ppermute | solution.py:340
  59.9 12.6 %collective-permute-start.15 = (bf16[2,192,384]{2,1,0:T(8,128)(2,1)S(1)}, bf16[2,192,384]{2,1,0:T(8,128)(2,1)S(1)}, u32[]{:S(2)}, u32[]{:S(2)}) collective-permute-start(bf16[2,192,384]{2,1,0:T(8,128)(2,1)S(1)} %copy-done.2), channel_id=1, source_target_pairs={{0,16},{4,12},{8,24},{12,4},{16,0},{20,28},{24,8},{28,20},{1,17},{... | collective-permute-start | bytes 884744 | tf_op jit(solution)/shard_map/ppermute | solution.py:340
  72.7 6.0 %collective-permute-start.17 = (bf16[2,2,192,384]{3,2,1,0:T(8,128)(2,1)S(1)}, bf16[2,2,192,384]{3,2,1,0:T(8,128)(2,1)}, u32[]{:S(2)}, u32[]{:S(2)}) collective-permute-start(bf16[2,2,192,384]{3,2,1,0:T(8,128)(2,1)S(1)} %join.5.rest_8_), channel_id=1, source_target_pairs={{0,4},{4,0},{8,12},{12,8},{16,20},{20,16},{24,28},{28,24},{1,5},{5... | collective-permute-start | bytes 1769480 | tf_op jit(solution)/shard_map/ppermute | solution.py:336
  76.8 1.9 %copy-start = (s32[384,1]{1,0:T(8,128)S(1)}, s32[384,1]{1,0:T(8,128)}, u32[]{:S(2)}) copy-start(s32[384,1]{1,0:T(8,128)} %reshape.16.col_ref) | copy-start | bytes 4612
  76.8 1.9 %copy-start.5 = (s32[32]{0:T(128)S(1)}, s32[32]{0:T(128)}, u32[]{:S(2)}) copy-start(s32[32]{0:T(128)} %occ_ref.1) | copy-start | bytes 388

commit v2 on v1

--- a/solution.py
+++ b/solution.py
@@ -49,23 +49,49 @@
     return gamma.astype(BF16)[None], (energy / (n_virt * n_virt))[None]
 
 
-def transform_kernel(plan_ref, slab_hbm, coeff_hbm, *rest, n_half, order, joined):
-    rest = rest[1:] if joined else rest
-    own_hbm, lists = rest[0], rest[1:1 + len(order)]
-    slab_v, coeff_v, acc_ref, own_v, in_sem, out_sem = rest[1 + len(order):]
-    n_orb, _, _ = own_hbm.shape
+def partner_half(plan_ref, s, n_orb):
+    return lax.div(plan_ref[0, s], n_orb)
+
+
+def rank_in_half(plan_ref, s, n_orb):
+    home = partner_half(plan_ref, s, n_orb)
+    return sum([(partner_half(plan_ref, t, n_orb) == home).astype(jnp.int32) for t in range(s)], jnp.int32(0))
+
+
+def transform_kernel(plan_ref, slab_hbm, coeff_hbm, *rest, n_half, order, chips):
+    n = len(order)
+    crowd_ref, rest = rest[0], rest[1:]
+    outs, lists, spill = rest[:chips], rest[chips:chips + n], rest[chips + n:chips + 2 * n]
+    slab_v, coeff_v, acc_ref, own_v, in_sem = rest[chips + 2 * n:]
+    cap = lists[0].shape[0]
+    count = cap + spill[0].shape[0]
+    n_orb = 2 * chips
+    aux = lax.axis_index("aux")
     tiles, block, lanes = acc_ref.shape
     rows = block // n_orb
     z = lax.axis_index("half")
-    loads, saves = [], []
+    loads, starts = [], []
     coeff_copy = pltpu.make_async_copy(coeff_hbm, coeff_v, in_sem.at[len(order)])
     coeff_copy.start()
     for i, d in enumerate(order):
         at = pl.multiple_of(lax.rem(z + d, n_half) * rows, rows)
         at_flat = pl.multiple_of(at * n_orb, block)
         loads.append(pltpu.make_async_copy(slab_hbm.at[pl.ds(at_flat, block)], slab_v.at[i], in_sem.at[i]))
-        saves.append(pltpu.make_async_copy(own_v.at[i], own_hbm.at[:, pl.ds(at, rows)], out_sem.at[i]))
+        starts.append(at)
         loads[i].start()
+    ranks = [rank_in_half(plan_ref, s, n_orb) for s in range(count)]
+    here = [partner_half(plan_ref, s, n_orb) == z for s in range(count)]
+    pick = []
+    for k in range(count):
+        hits = [
+            jnp.where(jnp.logical_and(here[s], ranks[s] == k), lax.rem(plan_ref[0, s], n_orb), 0)
+            for s in range(count)
+        ]
+        pick.append(sum(hits, jnp.int32(0)))
+    most = ranks[0]
+    for r in ranks[1:]:
+        most = jnp.maximum(most, r)
+    crowd_ref[0] = (most >= cap).astype(jnp.int32)
     coeff_copy.wait()
     for i in range(len(order)):
         loads[i].wait()
@@ -75,15 +101,19 @@
         for t in range(tiles):
             cols = slice(t * lanes, (t + 1) * lanes)
             for o in range(n_orb):
-                own_v[i, o, :, cols] = acc_ref[t, pl.ds(o, rows, stride=n_orb), :].astype(BF16)
-        saves[i].start()
-        for k in range(lists[i].shape[0]):
-            lists[i][k] = own_v[i, lax.rem(plan_ref[0, k], n_orb)]
-    for c in saves:
-        c.wait()
-
-
-def transform(half_slabs, coeff, plan, n_half, order, own=()):
+                own_v[o, :, cols] = acc_ref[t, pl.ds(o, rows, stride=n_orb), :].astype(BF16)
+        for r, out in enumerate(outs):
+            for j in range(2):
+                out[j, pl.ds(starts[i], rows)] = own_v[lax.bitwise_xor(aux, 2 * r + j)]
+        for k in range(count):
+            if k < cap:
+                lists[i][k] = own_v[pick[k]]
+            else:
+                spill[i][k - cap] = own_v[pick[k]]
+
+
+def transform(half_slabs, coeff, plan, n_half, order, cap):
+    chips = half_slabs.shape[2] // 2
     local_aux, _, n_orb, n_ao = half_slabs.shape
     n_virt = coeff.shape[1]
     count = plan.shape[1]
@@ -91,51 +121,62 @@
     n = len(order)
     hbm = pl.BlockSpec(memory_space=pltpu.HBM)
     vmem = pl.BlockSpec(memory_space=pltpu.VMEM)
-    return pl.pallas_call(
-        functools.partial(transform_kernel, n_half=n_half, order=order, joined=bool(own)),
-        in_specs=[pl.BlockSpec(memory_space=pltpu.SMEM), hbm, hbm] + [hbm] * len(own),
-        out_specs=[hbm] + [vmem] * n,
-        out_shape=[jax.ShapeDtypeStruct((n_orb, local_aux, n_virt), BF16)]
-        + [jax.ShapeDtypeStruct((count, rows, n_virt), BF16)] * n,
+    smem = pl.BlockSpec(memory_space=pltpu.SMEM)
+    return pl.pallas_call(
+        functools.partial(transform_kernel, n_half=n_half, order=order, chips=chips),
+        in_specs=[smem, hbm, hbm],
+        out_specs=[smem] + [vmem] * (chips + 2 * n),
+        out_shape=[
+            jax.ShapeDtypeStruct((1,), jnp.int32),
+        ]
+        + [jax.ShapeDtypeStruct((2, local_aux, n_virt), BF16)] * chips
+        + [jax.ShapeDtypeStruct((cap, rows, n_virt), BF16)] * n
+        + [jax.ShapeDtypeStruct((count - cap, rows, n_virt), BF16)] * n,
         scratch_shapes=[
             pltpu.VMEM((n, rows * n_orb, n_ao), BF16),
             pltpu.VMEM((n_ao, n_virt), BF16),
             pltpu.VMEM((n_virt // 128, rows * n_orb, 128), F32),
-            pltpu.VMEM((n, n_orb, rows, n_virt), BF16),
+            pltpu.VMEM((n_orb, rows, n_virt), BF16),
             pltpu.SemaphoreType.DMA((n + 1,)),
-            pltpu.SemaphoreType.DMA((n,)),
         ],
-        input_output_aliases={3: 0} if own else {},
         compiler_params=pltpu.CompilerParams(vmem_limit_bytes=60 << 20),
         name="transform",
-    )(plan, half_slabs.reshape(local_aux * n_orb, n_ao), coeff, *own)
-
-
-def merge_kernel(plan_ref, *refs, n_orb, n_half):
-    lists, outs, sem = refs[:n_half], refs[n_half:-1], refs[-1]
+    )(plan, half_slabs.reshape(local_aux * n_orb, n_ao), coeff)
+
+
+def merge_kernel(plan_ref, *refs, n_orb, n_half, spilled):
+    n_in = 2 * n_half if spilled else n_half
+    lists, outs, sem = refs[:n_in], refs[n_in:-1], refs[-1]
+    cap = lists[0].shape[0]
     per = outs[0].shape[0]
     z = lax.axis_index("half")
-
-    def copy(d, s):
-        return pltpu.make_async_copy(lists[d].at[s], outs[s // per].at[s % per], sem.at[s])
-
     for s in range(per * len(outs)):
-        far = lax.rem(z - lax.div(plan_ref[0, s], n_orb) + n_half, n_half)
+        far = lax.rem(z - partner_half(plan_ref, s, n_orb) + n_half, n_half)
+        rank = rank_in_half(plan_ref, s, n_orb)
         for d in range(n_half):
 
-            @pl.when(far == d)
+            @pl.when(jnp.logical_and(far == d, rank < cap))
             def _():
-                copy(d, s).start()
+                src = lists[d].at[jnp.minimum(rank, cap - 1)]
+                pltpu.make_async_copy(src, outs[s // per].at[s % per], sem.at[s]).start()
+
+            if spilled:
+
+                @pl.when(jnp.logical_and(far == d, rank >= cap))
+                def _():
+                    src = lists[n_half + d].at[jnp.maximum(rank - cap, 0)]
+                    pltpu.make_async_copy(src, outs[s // per].at[s % per], sem.at[s]).start()
 
     for s in range(per * len(outs)):
-        copy(0, s).wait()
-
-
-def merge(plan, lists, n_orb, per):
-    count, rows, n_virt = lists[0].shape
+        pltpu.make_async_copy(lists[0].at[0], outs[s // per].at[s % per], sem.at[s]).wait()
+
+
+def merge(plan, lists, n_orb, n_half, per):
+    count = plan.shape[1]
+    _, rows, n_virt = lists[0].shape
     shape = jax.ShapeDtypeStruct((per, rows, n_virt), BF16)
     return pl.pallas_call(
-        functools.partial(merge_kernel, n_orb=n_orb, n_half=len(lists)),
+        functools.partial(merge_kernel, n_orb=n_orb, n_half=n_half, spilled=len(lists) > n_half),
         in_specs=[pl.BlockSpec(memory_space=pltpu.SMEM)] + [pl.BlockSpec(memory_space=pl.ANY)] * len(lists),
         out_specs=[pl.BlockSpec(memory_space=pltpu.VMEM)] * (count // per),
         out_shape=[shape] * (count // per),
@@ -169,8 +210,9 @@
     )(*parts)
 
 
-def join_kernel(*refs):
+def join_kernel(*refs, entry):
     parts, out, sem = refs[:-2], refs[-2], refs[-1]
+    parts = parts if entry is None else [part.at[entry] for part in parts]
     copies = [pltpu.make_async_copy(part, out.at[i], sem.at[i]) for i, part in enumerate(parts)]
     for c in copies:
         c.start()
@@ -178,12 +220,13 @@
         c.wait()
 
 
-def join(parts):
-    return pl.pallas_call(
-        join_kernel,
+def join(parts, entry=None):
+    shape = parts[0].shape if entry is None else parts[0].shape[1:]
+    return pl.pallas_call(
+        functools.partial(join_kernel, entry=entry),
         in_specs=[pl.BlockSpec(memory_space=pl.ANY)] * len(parts),
         out_specs=pl.BlockSpec(memory_space=pltpu.VMEM),
-        out_shape=jax.ShapeDtypeStruct((len(parts),) + parts[0].shape, BF16),
+        out_shape=jax.ShapeDtypeStruct((len(parts),) + shape, BF16),
         scratch_shapes=[pltpu.SemaphoreType.DMA((len(parts),))],
         compiler_params=pltpu.CompilerParams(vmem_limit_bytes=4 << 20),
         name="join",
@@ -193,24 +236,32 @@
 CORE, X, Y = 1, 2, 4
 
 
-def prep_kernel(own_hbm, own_t, own_v, sem):
-    copy = pltpu.make_async_copy(own_hbm, own_v, sem)
-    copy.start()
-    copy.wait()
+def prep_kernel(*refs):
+    near, other, own_t, own_v, sem = refs[:-4], refs[-4], refs[-3], refs[-2], refs[-1]
+    aux = lax.axis_index("aux")
+    copies = []
+    for r in range(len(near)):
+        for src, bits in ((near[r].at[0], 2 * r), (other.at[r], 2 * r + 1)):
+            at = lax.bitwise_xor(aux, bits)
+            copies.append(pltpu.make_async_copy(src, own_v.at[at], sem.at[len(copies)]))
+    for c in copies:
+        c.start()
+    for c in copies:
+        c.wait()
     own_t[...] = jnp.transpose(own_v[...].reshape(own_t.shape[1], own_t.shape[0]))
 
 
-def prep(own):
-    n_src, rows, n_virt = own.shape
+def prep(near, other):
+    chips, rows, n_virt = other.shape
     return pl.pallas_call(
         prep_kernel,
-        in_specs=[pl.BlockSpec(memory_space=pl.ANY)],
+        in_specs=[pl.BlockSpec(memory_space=pl.ANY)] * (chips + 1),
         out_specs=pl.BlockSpec(memory_space=pltpu.VMEM),
-        out_shape=jax.ShapeDtypeStruct((n_virt, n_src * rows), BF16),
-        scratch_shapes=[pltpu.VMEM(own.shape, BF16), pltpu.SemaphoreType.DMA],
+        out_shape=jax.ShapeDtypeStruct((n_virt, 2 * chips * rows), BF16),
+        scratch_shapes=[pltpu.VMEM((2 * chips, rows, n_virt), BF16), pltpu.SemaphoreType.DMA((2 * chips,))],
         compiler_params=pltpu.CompilerParams(vmem_limit_bytes=8 << 20),
         name="prep",
-    )(own)
+    )(*near, other)
 
 
 def amp_kernel(own_t, early, other, out_ref, part_v, sem):
@@ -345,7 +396,6 @@
 
 
 GROUPS = 2
-FIRST = (1, 2, 3, 0)
 
 
 def on_device(half_slabs, vir_coeff, occ_energy, vir_energy, plan):
@@ -358,14 +408,29 @@
     _, _, ohalf, _ = half_slabs.shape
     count = plan.size
     per = count // GROUPS
-    own8, *lists_0 = transform(half_slabs, vir_coeff, plan, n_half, FIRST)
-    lists = dict(zip(FIRST, lists_0))
+    cap = max(1, count // 2)
+    order = tuple(range(1, n_half)) + (0,)
+    crowd, *lists = transform(half_slabs, vir_coeff, plan, n_half, order, cap)
+    near, lists = lists[:n_aux // 2], lists[n_aux // 2:]
+    lists, spill = lists[:n_half], lists[n_half:]
+    lists, spill = [lists[-1]] + lists[:-1], [spill[-1]] + spill[:-1]
     got = [lists[0]]
     for d in range(1, n_half):
         got.append(shift(lists[d], d, n_half))
-    own = lax.all_to_all(own8, "aux", split_axis=0, concat_axis=0, tiled=True)
-    own = prep(own)
-    mine = merge(plan, got, ohalf, per)
+    for r in range(1, n_aux // 2):
+        near[r] = lax.ppermute(near[r], "aux", [(a, a ^ (2 * r)) for a in range(n_aux)])
+    other = join(near, 1)
+    other = swap(other, n_aux)
+    own = prep(near, other)
+
+    def roomy(got, spill):
+        return merge(plan, got, ohalf, n_half, per)
+
+    def crowded(got, spill):
+        more = [spill[0]] + [shift(spill[d], d, n_half) for d in range(1, n_half)]
+        return merge(plan, got + more, ohalf, n_half, per)
+
+    mine = lax.switch(crowd[0], [roomy, crowded], got, spill)
     ins, late = [], []
     for g in range(GROUPS):
         parts = [mine[g]]

time: 85.5 us -> 77.6 us (0.908)
  starting transfers between devices: 30.3 us -> 25 us
  local copies, waits for them, and re-layouts: 3.39 us -> 0.14 us
  waiting for transfers between devices: 31.2 us -> 33.6 us
  Pallas kernels: 19.5 us -> 17.2 us
    ppermute x0 -> x3, waiting for transfers between devices: none -> 11 us  [stages(): lax.ppermute(near[r], 'aux', [(a, a ^ 2 * r) for a in range(n_aux)])]
    ppermute x6, waiting for transfers between devices: 17.6 us -> 8.56 us  [plane(): lax.ppermute(x, 'aux', [(a, a ^ (Y if a & CORE ^ flip else X)) for a in r...]
    ppermute x9, starting transfers between devices: 18.1 us -> 14.2 us  [shift(): return lax.ppermute(x, 'half', [(h, (h + d) % n) for h in range(n)])]
    all_to_all x1 -> x0, starting transfers between devices: 3.56 us -> none  [stages(): own = lax.all_to_all(own8, 'aux', split_axis=0, concat_axis=0, tiled=True)]
    ppermute x0 -> x3, starting transfers between devices: none -> 3.49 us  [stages(): lax.ppermute(near[r], 'aux', [(a, a ^ 2 * r) for a in range(n_aux)])]
    unnamed x14, local copies, waits for them, and re-layouts: 2.59 us -> 0.03 us
    pallas_call x2, Pallas kernels: 3.65 us -> 1.7 us  [amplitudes(): pl.pallas_call(amp_kernel, in_specs=[vmem, anym, anym], out_specs=[vmem,...]
    pallas_call x5 -> x6, Pallas kernels: 2.93 us -> 4.22 us  [the longest x1 1.98 us: prep(): pl.pallas_call(prep_kernel, in_specs=[pl.BlockSpec(memory_space=pl.ANY)]...]
  transfers between devices with their start and end apart: 19 -> 22, of which waited for: 8 -> 13; matrix products, arithmetic and copies ran while one was open for 1% -> 0% of each run, Pallas kernels for 7% -> 7%
where the time goes in v2:
time: 77.6 us; the launch traced here: 77.5 us
  waiting for transfers between devices  33.6 us (43%)
  starting transfers between devices  25 us (32%)
  Pallas kernels  17.2 us (22%)
  between operations  1.51 us (2%)
    ppermute x9, starting transfers between devices, shift(): return lax.ppermute(x, 'half', [(h, (h + d) % n) for h in range(n)])  14.2 us
    ppermute x9, waiting for transfers between devices, shift(): return lax.ppermute(x, 'half', [(h, (h + d) % n) for h in range(n)])  14 us
    ppermute x3, waiting for transfers between devices, stages(): lax.ppermute(near[r], 'aux', [(a, a ^ 2 * r) for a in range(n_aux)])  11 us
    ppermute x6, waiting for transfers between devices, plane(): lax.ppermute(x, 'aux', [(a, a ^ (Y if a & CORE ^ flip else X)) for a in r...  8.56 us
    ppermute x6, starting transfers between devices, plane(): lax.ppermute(x, 'aux', [(a, a ^ (Y if a & CORE ^ flip else X)) for a in r...  7.11 us
    pallas_call x1, Pallas kernels, transform(): pl.pallas_call(functools.partial(transform_kernel, n_half=n_half, order=o...  5.83 us
    pallas_call x1, Pallas kernels, pair_terms(): pl.pallas_call(functools.partial(pair_kernel, n_orb=n_orb, groups=groups)...  5.4 us
    ppermute x3, starting transfers between devices, stages(): lax.ppermute(near[r], 'aux', [(a, a ^ 2 * r) for a in range(n_aux)])  3.49 us
  transfers between devices with their start and end apart: 22, of which 13 were waited for; matrix products, arithmetic and copies ran while one was open for 0% of the time, Pallas kernels for 7%

profile of v2, /device:TPU:0, one launch (start us, length us, event | category | flops | bytes accessed | tf_op | source)
XLA Modules:
  0.0 77.5 jit_solution(5525741858745437510)
XLA Ops:
  0.6 5.8 %transform.1 = (s32[1]{0:T(128)}, bf16[2,192,384]{2,1,0:T(8,128)(2,1)}, bf16[2,192,384]{2,1,0:T(8,128)(2,1)}, bf16[2,192,384]{2,1,0:T(8,128)(2,1)}, bf16[2,192,3...) custom-call(s32[1,4]{1,0:T(1,128)} %plan_ref.3, ...), custom_call_target="tpu_custom_call" | custom-call | tf_op jit(solution)/shard_map/transform/pallas_call | solution.py:125
  6.5 3.1 %collective-permute-start.7 = (bf16[2,48,384]{2,1,0:T(8,128)(2,1)}, bf16[2,48,384]{2,1,0:T(8,128)(2,1)S(1)}, u32[]{:S(2)}, u32[]{:S(2)}) collective-permute-start(bf16[2,48,384]{2,1,0:T(8,128)(2,1)} %get-tuple-element.71), channel_id=1, source_target_pairs={{0,1},{1,2},{2,3},{3,0},{4,5},{5,6},{6,7},{7,4},{8,9},{9,10},{10,1... | collective-permute-start | bytes 221192 | tf_op jit(solution)/shard_map/ppermute | solution.py:395
  9.6 2.6 %collective-permute-start.8 = (bf16[2,48,384]{2,1,0:T(8,128)(2,1)}, bf16[2,48,384]{2,1,0:T(8,128)(2,1)S(1)}, u32[]{:S(2)}, u32[]{:S(2)}) collective-permute-start(bf16[2,48,384]{2,1,0:T(8,128)(2,1)} %get-tuple-element.72), channel_id=1, source_target_pairs={{0,2},{1,3},{2,0},{3,1},{4,6},{5,7},{6,4},{7,5},{8,10},{9,11},{10,... | collective-permute-start | bytes 221192 | tf_op jit(solution)/shard_map/ppermute | solution.py:395
  12.2 1.3 %collective-permute-start.9 = (bf16[2,48,384]{2,1,0:T(8,128)(2,1)}, bf16[2,48,384]{2,1,0:T(8,128)(2,1)S(1)}, u32[]{:S(2)}, u32[]{:S(2)}) collective-permute-start(bf16[2,48,384]{2,1,0:T(8,128)(2,1)} %get-tuple-element.73), channel_id=1, source_target_pairs={{0,3},{1,0},{2,1},{3,2},{4,7},{5,4},{6,5},{7,6},{8,11},{9,8},{10,9... | collective-permute-start | bytes 221192 | tf_op jit(solution)/shard_map/ppermute | solution.py:395
  14.5 2.9 %collective-permute-done.8 = bf16[2,48,384]{2,1,0:T(8,128)(2,1)S(1)} collective-permute-done((bf16[2,48,384]{2,1,0:T(8,128)(2,1)}, bf16[2,48,384]{2,1,0:T(8,128)(2,1)S(1)}, u32[]{:S(2)}, u32[]{:S(2)}) %collective-permute-start.8) | collective-permute-done | bytes 73760 | tf_op jit(solution)/shard_map/ppermute | solution.py:395
  17.6 0.9 %conditional.1 = ((bf16[2,48,384]{2,1,0:T(8,128)(2,1)S(1)}, bf16[2,48,384]{2,1,0:T(8,128)(2,1)S(1)})) conditional(s32[]{:T(128)} %bitcast.1, (s32[1,4]{1,0:T(1,128)S(1)}, bf16[2,48,384]{2,1,0:T(8,128)(2,1)S(1)}, bf16[2,48,384]{2,1,0:T(8,128)(2,1)S(1)}, bf16[2,48,384]{2,1,0:T(8,128)(2,1)S(1)}, bf16[2,48,384]{2,1,0:T(8,128)(2,1)S(1)}) %tuple.21, ...), branch_computations={%region_0.0_spmd, %region_1.0_spmd} | conditional | bytes 884864 | solution.py:433
  17.6 0.9 %merge.2 = (bf16[2,48,384]{2,1,0:T(8,128)(2,1)S(1)}, bf16[2,48,384]{2,1,0:T(8,128)(2,1)S(1)}) custom-call(s32[1,4]{1,0:T(1,128)S(1)} %get-tuple-element.28.plan_ref, bf16[2,48,384]{2,1,0:T(8,128)(2,1)S(1)} %get-tuple-element.29.refs_0_, bf16[2,48,384]{2,1,0:T(8,128)(2,1)S(1)} %get-tuple-element.30.refs_1_, ...), custom_call_target="tpu_custom_call" | custom-call | tf_op jit(solution)/shard_map/cond/branch_0_fun/merge/pallas_call | solution.py:178
  18.5 3.2 %collective-permute-start.18 = (bf16[2,48,384]{2,1,0:T(8,128)(2,1)S(1)}, bf16[2,48,384]{2,1,0:T(8,128)(2,1)S(1)}, u32[]{:S(2)}, u32[]{:S(2)}) collective-permute-start(bf16[2,48,384]{2,1,0:T(8,128)(2,1)S(1)} %get-tuple-element.81.refs_0_), channel_id=1, source_target_pairs={{0,3},{1,0},{2,1},{3,2},{4,7},{5,4},{6,5},{7,6},{8,11},{9,8},{10,9... | collective-permute-start | bytes 221192 | tf_op jit(solution)/shard_map/ppermute | solution.py:395
  21.9 0.5 collective-permute-start.16
  22.4 1.9 %collective-permute-done.18.refs_3_ = bf16[2,48,384]{2,1,0:T(8,128)(2,1)S(1)} collective-permute-done((bf16[2,48,384]{2,1,0:T(8,128)(2,1)S(1)}, bf16[2,48,384]{2,1,0:T(8,128)(2,1)S(1)}, u32[]{:S(2)}, u32[]{:S(2)}) %collective-permute-start.18) | collective-permute-done | bytes 73760 | tf_op jit(solution)/shard_map/ppermute | solution.py:395
  24.3 4.6 %collective-permute-done.17.refs_2_ = bf16[2,48,384]{2,1,0:T(8,128)(2,1)S(1)} collective-permute-done((bf16[2,48,384]{2,1,0:T(8,128)(2,1)S(1)}, bf16[2,48,384]{2,1,0:T(8,128)(2,1)S(1)}, u32[]{:S(2)}, u32[]{:S(2)}) %collective-permute-start.17) | collective-permute-done | bytes 73760 | tf_op jit(solution)/shard_map/ppermute | solution.py:395
  29.0 1.5 %collective-permute-start.20 = (bf16[2,192,384]{2,1,0:T(8,128)(2,1)S(1)}, bf16[2,192,384]{2,1,0:T(8,128)(2,1)S(1)}, u32[]{:S(2)}, u32[]{:S(2)}) collective-permute-start(bf16[2,192,384]{2,1,0:T(8,128)(2,1)S(1)} %pack.3.refs_0_), channel_id=1, source_target_pairs={{0,16},{4,12},{8,24},{12,4},{16,0},{20,28},{24,8},{28,20},{1,17},{... | collective-permute-start | bytes 884744 | tf_op jit(solution)/shard_map/ppermute | solution.py:391
  30.4 1.3 %collective-permute-start.12 = (bf16[2,48,384]{2,1,0:T(8,128)(2,1)S(1)}, bf16[2,48,384]{2,1,0:T(8,128)(2,1)S(1)}, u32[]{:S(2)}, u32[]{:S(2)}) collective-permute-start(bf16[2,48,384]{2,1,0:T(8,128)(2,1)S(1)} %get-tuple-element.78.refs_0_), channel_id=1, source_target_pairs={{0,3},{1,0},{2,1},{3,2},{4,7},{5,4},{6,5},{7,6},{8,11},{9,8},{10,9... | collective-permute-start | bytes 221192 | tf_op jit(solution)/shard_map/ppermute | solution.py:395
  31.7 2.0 %collective-permute-start.10 = (bf16[2,48,384]{2,1,0:T(8,128)(2,1)S(1)}, bf16[2,48,384]{2,1,0:T(8,128)(2,1)S(1)}, u32[]{:S(2)}, u32[]{:S(2)}) collective-permute-start(bf16[2,48,384]{2,1,0:T(8,128)(2,1)S(1)} %get-tuple-element.78.refs_0_), channel_id=1, source_target_pairs={{0,1},{1,2},{2,3},{3,0},{4,5},{5,6},{6,7},{7,4},{8,9},{9,10},{10,1... | collective-permute-start | bytes 221192 | tf_op jit(solution)/shard_map/ppermute | solution.py:395
  33.7 1.5 %collective-permute-start.19 = (bf16[2,192,384]{2,1,0:T(8,128)(2,1)S(1)}, bf16[2,192,384]{2,1,0:T(8,128)(2,1)S(1)}, u32[]{:S(2)}, u32[]{:S(2)}) collective-permute-start(bf16[2,192,384]{2,1,0:T(8,128)(2,1)S(1)} %pack.3.refs_0_), channel_id=1, source_target_pairs={{0,8},{4,20},{8,0},{12,28},{16,24},{20,4},{24,16},{28,12},{1,9},{5... | collective-permute-start | bytes 884744 | tf_op jit(solution)/shard_map/ppermute | solution.py:391
  35.3 4.0 %collective-permute-done.11.refs_2_ = bf16[2,48,384]{2,1,0:T(8,128)(2,1)S(1)} collective-permute-done((bf16[2,48,384]{2,1,0:T(8,128)(2,1)S(1)}, bf16[2,48,384]{2,1,0:T(8,128)(2,1)S(1)}, u32[]{:S(2)}, u32[]{:S(2)}) %collective-permute-start.11) | collective-permute-done | bytes 73760 | tf_op jit(solution)/shard_map/ppermute | solution.py:395
  39.3 0.8 %collective-permute-start.14 = (bf16[2,192,384]{2,1,0:T(8,128)(2,1)S(1)}, bf16[2,192,384]{2,1,0:T(8,128)(2,1)S(1)}, u32[]{:S(2)}, u32[]{:S(2)}) collective-permute-start(bf16[2,192,384]{2,1,0:T(8,128)(2,1)S(1)} %pack.2.refs_0_), channel_id=1, source_target_pairs={{0,16},{4,12},{8,24},{12,4},{16,0},{20,28},{24,8},{28,20},{1,17},{... | collective-permute-start | bytes 884744 | tf_op jit(solution)/shard_map/ppermute | solution.py:391
  40.1 1.3 %collective-permute-start.13 = (bf16[2,192,384]{2,1,0:T(8,128)(2,1)S(1)}, bf16[2,192,384]{2,1,0:T(8,128)(2,1)S(1)}, u32[]{:S(2)}, u32[]{:S(2)}) collective-permute-start(bf16[2,192,384]{2,1,0:T(8,128)(2,1)S(1)} %pack.2.refs_0_), channel_id=1, source_target_pairs={{0,8},{4,20},{8,0},{12,28},{16,24},{20,4},{24,16},{28,12},{1,9},{5... | collective-permute-start | bytes 884744 | tf_op jit(solution)/shard_map/ppermute | solution.py:391
  41.4 0.7 collective-permute-start.3
  42.2 1.3 %collective-permute-start.4 = (bf16[2,192,384]{2,1,0:T(8,128)(2,1)S(1)}, bf16[2,192,384]{2,1,0:T(8,128)(2,1)S(1)}, u32[]{:S(2)}, u32[]{:S(2)}) collective-permute-start(bf16[2,192,384]{2,1,0:T(8,128)(2,1)S(1)} %copy-done.5), channel_id=1, source_target_pairs={{0,16},{4,20},{8,24},{12,28},{16,0},{20,4},{24,8},{28,12},{1,17},{... | collective-permute-start | bytes 884744 | tf_op jit(solution)/shard_map/ppermute | solution.py:421
  43.4 1.5 %collective-permute-start.5 = (bf16[2,192,384]{2,1,0:T(8,128)(2,1)S(1)}, bf16[2,192,384]{2,1,0:T(8,128)(2,1)S(1)}, u32[]{:S(2)}, u32[]{:S(2)}) collective-permute-start(bf16[2,192,384]{2,1,0:T(8,128)(2,1)S(1)} %copy-done.4), channel_id=1, source_target_pairs={{0,24},{4,28},{8,16},{12,20},{16,8},{20,12},{24,0},{28,4},{1,25},{... | collective-permute-start | bytes 884744 | tf_op jit(solution)/shard_map/ppermute | solution.py:421
  45.2 4.4 %collective-permute-done.14.refs_2_ = bf16[2,192,384]{2,1,0:T(8,128)(2,1)S(1)} collective-permute-done((bf16[2,192,384]{2,1,0:T(8,128)(2,1)S(1)}, bf16[2,192,384]{2,1,0:T(8,128)(2,1)S(1)}, u32[]{:S(2)}, u32[]{:S(2)}) %collective-permute-start.14) | collective-permute-done | bytes 294944 | tf_op jit(solution)/shard_map/ppermute | solution.py:391
  50.3 6.0 %collective-permute-done.3.refs_1_ = bf16[2,192,384]{2,1,0:T(8,128)(2,1)S(1)} collective-permute-done((bf16[2,192,384]{2,1,0:T(8,128)(2,1)S(1)}, bf16[2,192,384]{2,1,0:T(8,128)(2,1)S(1)}, u32[]{:S(2)}, u32[]{:S(2)}) %collective-permute-start.3) | collective-permute-done | bytes 294944 | tf_op jit(solution)/shard_map/ppermute | solution.py:421
  56.3 1.3 %collective-permute-start.23 = (bf16[2,192,384]{2,1,0:T(8,128)(2,1)S(1)}, bf16[2,192,384]{2,1,0:T(8,128)(2,1)S(1)}, u32[]{:S(2)}, u32[]{:S(2)}) collective-permute-start(bf16[2,192,384]{2,1,0:T(8,128)(2,1)S(1)} %collective-permute-done.19.refs_1_), channel_id=1, source_target_pairs={{0,16},{4,12},{8,24},{12,4},{16,0},{20,28},{24,8},{28,20},{1,17},{... | collective-permute-start | bytes 884744 | tf_op jit(solution)/shard_map/ppermute | solution.py:391
  57.6 0.8 collective-permute-start.22
  58.4 5.0 %collective-permute-done.5.refs_3_ = bf16[2,192,384]{2,1,0:T(8,128)(2,1)S(1)} collective-permute-done((bf16[2,192,384]{2,1,0:T(8,128)(2,1)S(1)}, bf16[2,192,384]{2,1,0:T(8,128)(2,1)S(1)}, u32[]{:S(2)}, u32[]{:S(2)}) %collective-permute-start.5) | collective-permute-done | bytes 294944 | tf_op jit(solution)/shard_map/ppermute | solution.py:421
  63.4 0.8 %join.4 = bf16[4,192,384]{2,1,0:T(8,128)(2,1)S(1)} custom-call(bf16[2,192,384]{2,1,0:T(8,128)(2,1)S(1)} %copy-done, bf16[2,192,384]{2,1,0:T(8,128)(2,1)S(1)} %collective-permute-done.3.refs_1_, bf16[2,192,384]{2,1,0:T(8,128)(2,1)S(1)} %collective-permute-done.4.refs_2_, bf16[2,192,384]{2,1,0:T(8,128)(2,1)S(1)} %collective-permute-done.5.refs_3_), custom_call_target="tpu_custom_call" | custom-call | tf_op jit(solution)/shard_map/join/pallas_call | solution.py:225
  64.8 3.2 %collective-permute-done.22.refs_0_ = bf16[2,192,384]{2,1,0:T(8,128)(2,1)S(1)} collective-permute-done((bf16[2,192,384]{2,1,0:T(8,128)(2,1)S(1)}, bf16[2,192,384]{2,1,0:T(8,128)(2,1)S(1)}, u32[]{:S(2)}, u32[]{:S(2)}) %collective-permute-start.22) | collective-permute-done | bytes 294944 | tf_op jit(solution)/shard_map/ppermute | solution.py:391
  68.3 2.0 %prep.1.own_t = bf16[384,1536]{1,0:T(8,128)(2,1)S(1)} custom-call(bf16[2,192,384]{2,1,0:T(8,128)(2,1)S(1)} %copy-done, bf16[2,192,384]{2,1,0:T(8,128)(2,1)S(1)} %collective-permute-done.3.refs_1_, bf16[2,192,384]{2,1,0:T(8,128)(2,1)S(1)} %collective-permute-done.4.refs_2_, bf16[2,192,384]{2,1,0:T(8,128)(2,1)S(1)} %collective-permute-done.5.refs_3_, ...), custom_call_target="tpu_custom_call" | custom-call | tf_op jit(solution)/shard_map/prep/pallas_call | solution.py:256
  70.3 0.9 %amplitudes.3 = (f32[384,768]{1,0:T(8,128)S(1)}, bf16[2,768,384]{2,1,0:T(8,128)(2,1)S(1)}) custom-call(bf16[384,1536]{1,0:T(8,128)(2,1)S(1)} %prep.1.own_t, bf16[3,2,192,384]{3,2,1,0:T(8,128)(2,1)S(1)} %join.6.early.rest_4_, bf16[3,2,192,384]{3,2,1,0:T(8,128)(2,1)S(1)} %collective-permute-done.21.other.rest_5_), custom_call_target="tpu_custom_call" | custom-call | flops 452984832 | bytes 3145728 | tf_op jit(solution)/shard_map/amplitudes/pallas_call | solution.py:291
  71.2 0.9 %amplitudes.2 = (f32[384,768]{1,0:T(8,128)S(1)}, bf16[2,768,384]{2,1,0:T(8,128)(2,1)S(1)}) custom-call(bf16[384,1536]{1,0:T(8,128)(2,1)S(1)} %prep.1.own_t, bf16[3,2,192,384]{3,2,1,0:T(8,128)(2,1)S(1)} %join.5.early.rest_0_, bf16[3,2,192,384]{3,2,1,0:T(8,128)(2,1)S(1)} %collective-permute-done.15.other.rest_1_), custom_call_target="tpu_custom_call" | custom-call | flops 452984832 | bytes 3145728 | tf_op jit(solution)/shard_map/amplitudes/pallas_call | solution.py:291
  72.1 5.4 %pair_terms.1 = (bf16[384,1536]{1,0:T(8,128)(2,1)}, f32[1,1]{1,0:T(1,128)}) custom-call(s32[32]{0:T(128)S(1)} %copy-done.1, s32[1,4]{1,0:T(1,128)S(1)} %copy-done.3, s32[1,384]{1,0:T(1,128)S(1)} %reshape.16.row_ref, s32[384,1]{1,0:T(8,128)S(1)} %reshape.19.col_ref, bf16[384,1536]{1,0:T(8,128)(2,1)S(1)} %prep.1.own_t, ...), custom_call_target="tpu_custom_call" | custom-call | tf_op jit(solution)/shard_map/pair_terms/pallas_call | solution.py:370
  (41 shorter events, 2.8 us)
Async XLA Ops:
  0.6 17.0 %copy-start.3 = (s32[1,4]{1,0:T(1,128)S(1)}, s32[1,4]{1,0:T(1,128)}, u32[]{:S(2)}) copy-start(s32[1,4]{1,0:T(1,128)} %plan_ref.3) | copy-start | bytes 52
  6.5 35.0 %copy-start.6 = (bf16[2,192,384]{2,1,0:T(8,128)(2,1)S(1)}, bf16[2,192,384]{2,1,0:T(8,128)(2,1)}, u32[]{:S(2)}) copy-start(bf16[2,192,384]{2,1,0:T(8,128)(2,1)} %get-tuple-element.66) | copy-start | bytes 884740
  6.5 35.7 %copy-start.5 = (bf16[2,192,384]{2,1,0:T(8,128)(2,1)S(1)}, bf16[2,192,384]{2,1,0:T(8,128)(2,1)}, u32[]{:S(2)}) copy-start(bf16[2,192,384]{2,1,0:T(8,128)(2,1)} %get-tuple-element.67) | copy-start | bytes 884740
  6.5 36.9 %copy-start.4 = (bf16[2,192,384]{2,1,0:T(8,128)(2,1)S(1)}, bf16[2,192,384]{2,1,0:T(8,128)(2,1)}, u32[]{:S(2)}) copy-start(bf16[2,192,384]{2,1,0:T(8,128)(2,1)} %get-tuple-element.68) | copy-start | bytes 884740
  6.5 8.0 %collective-permute-start.7 = (bf16[2,48,384]{2,1,0:T(8,128)(2,1)}, bf16[2,48,384]{2,1,0:T(8,128)(2,1)S(1)}, u32[]{:S(2)}, u32[]{:S(2)}) collective-permute-start(bf16[2,48,384]{2,1,0:T(8,128)(2,1)} %get-tuple-element.71), channel_id=1, source_target_pairs={{0,1},{1,2},{2,3},{3,0},{4,5},{5,6},{6,7},{7,4},{8,9},{9,10},{10,1... | collective-permute-start | bytes 221192 | tf_op jit(solution)/shard_map/ppermute | solution.py:395
  9.6 7.8 %collective-permute-start.8 = (bf16[2,48,384]{2,1,0:T(8,128)(2,1)}, bf16[2,48,384]{2,1,0:T(8,128)(2,1)S(1)}, u32[]{:S(2)}, u32[]{:S(2)}) collective-permute-start(bf16[2,48,384]{2,1,0:T(8,128)(2,1)} %get-tuple-element.72), channel_id=1, source_target_pairs={{0,2},{1,3},{2,0},{3,1},{4,6},{5,7},{6,4},{7,5},{8,10},{9,11},{10,... | collective-permute-start | bytes 221192 | tf_op jit(solution)/shard_map/ppermute | solution.py:395
  12.2 5.4 %collective-permute-start.9 = (bf16[2,48,384]{2,1,0:T(8,128)(2,1)}, bf16[2,48,384]{2,1,0:T(8,128)(2,1)S(1)}, u32[]{:S(2)}, u32[]{:S(2)}) collective-permute-start(bf16[2,48,384]{2,1,0:T(8,128)(2,1)} %get-tuple-element.73), channel_id=1, source_target_pairs={{0,3},{1,0},{2,1},{3,2},{4,7},{5,4},{6,5},{7,6},{8,11},{9,8},{10,9... | collective-permute-start | bytes 221192 | tf_op jit(solution)/shard_map/ppermute | solution.py:395
  18.5 5.7 %collective-permute-start.18 = (bf16[2,48,384]{2,1,0:T(8,128)(2,1)S(1)}, bf16[2,48,384]{2,1,0:T(8,128)(2,1)S(1)}, u32[]{:S(2)}, u32[]{:S(2)}) collective-permute-start(bf16[2,48,384]{2,1,0:T(8,128)(2,1)S(1)} %get-tuple-element.81.refs_0_), channel_id=1, source_target_pairs={{0,3},{1,0},{2,1},{3,2},{4,7},{5,4},{6,5},{7,6},{8,11},{9,8},{10,9... | collective-permute-start | bytes 221192 | tf_op jit(solution)/shard_map/ppermute | solution.py:395
  21.8 7.2 %collective-permute-start.17 = (bf16[2,48,384]{2,1,0:T(8,128)(2,1)S(1)}, bf16[2,48,384]{2,1,0:T(8,128)(2,1)S(1)}, u32[]{:S(2)}, u32[]{:S(2)}) collective-permute-start(bf16[2,48,384]{2,1,0:T(8,128)(2,1)S(1)} %get-tuple-element.81.refs_0_), channel_id=1, source_target_pairs={{0,2},{1,3},{2,0},{3,1},{4,6},{5,7},{6,4},{7,5},{8,10},{9,11},{10,... | collective-permute-start | bytes 221192 | tf_op jit(solution)/shard_map/ppermute | solution.py:395
  21.9 7.1 %collective-permute-start.16 = (bf16[2,48,384]{2,1,0:T(8,128)(2,1)S(1)}, bf16[2,48,384]{2,1,0:T(8,128)(2,1)S(1)}, u32[]{:S(2)}, u32[]{:S(2)}) collective-permute-start(bf16[2,48,384]{2,1,0:T(8,128)(2,1)S(1)} %get-tuple-element.81.refs_0_), channel_id=1, source_target_pairs={{0,1},{1,2},{2,3},{3,0},{4,5},{5,6},{6,7},{7,4},{8,9},{9,10},{10,1... | collective-permute-start | bytes 221192 | tf_op jit(solution)/shard_map/ppermute | solution.py:395
  29.0 13.2 %collective-permute-start.20 = (bf16[2,192,384]{2,1,0:T(8,128)(2,1)S(1)}, bf16[2,192,384]{2,1,0:T(8,128)(2,1)S(1)}, u32[]{:S(2)}, u32[]{:S(2)}) collective-permute-start(bf16[2,192,384]{2,1,0:T(8,128)(2,1)S(1)} %pack.3.refs_0_), channel_id=1, source_target_pairs={{0,16},{4,12},{8,24},{12,4},{16,0},{20,28},{24,8},{28,20},{1,17},{... | collective-permute-start | bytes 884744 | tf_op jit(solution)/shard_map/ppermute | solution.py:391
  30.4 4.8 %collective-permute-start.12 = (bf16[2,48,384]{2,1,0:T(8,128)(2,1)S(1)}, bf16[2,48,384]{2,1,0:T(8,128)(2,1)S(1)}, u32[]{:S(2)}, u32[]{:S(2)}) collective-permute-start(bf16[2,48,384]{2,1,0:T(8,128)(2,1)S(1)} %get-tuple-element.78.refs_0_), channel_id=1, source_target_pairs={{0,3},{1,0},{2,1},{3,2},{4,7},{5,4},{6,5},{7,6},{8,11},{9,8},{10,9... | collective-permute-start | bytes 221192 | tf_op jit(solution)/shard_map/ppermute | solution.py:395
  31.7 7.5 %collective-permute-start.11 = (bf16[2,48,384]{2,1,0:T(8,128)(2,1)S(1)}, bf16[2,48,384]{2,1,0:T(8,128)(2,1)S(1)}, u32[]{:S(2)}, u32[]{:S(2)}) collective-permute-start(bf16[2,48,384]{2,1,0:T(8,128)(2,1)S(1)} %get-tuple-element.78.refs_0_), channel_id=1, source_target_pairs={{0,2},{1,3},{2,0},{3,1},{4,6},{5,7},{6,4},{7,5},{8,10},{9,11},{10,... | collective-permute-start | bytes 221192 | tf_op jit(solution)/shard_map/ppermute | solution.py:395
  31.7 7.5 %collective-permute-start.10 = (bf16[2,48,384]{2,1,0:T(8,128)(2,1)S(1)}, bf16[2,48,384]{2,1,0:T(8,128)(2,1)S(1)}, u32[]{:S(2)}, u32[]{:S(2)}) collective-permute-start(bf16[2,48,384]{2,1,0:T(8,128)(2,1)S(1)} %get-tuple-element.78.refs_0_), channel_id=1, source_target_pairs={{0,1},{1,2},{2,3},{3,0},{4,5},{5,6},{6,7},{7,4},{8,9},{9,10},{10,1... | collective-permute-start | bytes 221192 | tf_op jit(solution)/shard_map/ppermute | solution.py:395
  33.7 9.7 %collective-permute-start.19 = (bf16[2,192,384]{2,1,0:T(8,128)(2,1)S(1)}, bf16[2,192,384]{2,1,0:T(8,128)(2,1)S(1)}, u32[]{:S(2)}, u32[]{:S(2)}) collective-permute-start(bf16[2,192,384]{2,1,0:T(8,128)(2,1)S(1)} %pack.3.refs_0_), channel_id=1, source_target_pairs={{0,8},{4,20},{8,0},{12,28},{16,24},{20,4},{24,16},{28,12},{1,9},{5... | collective-permute-start | bytes 884744 | tf_op jit(solution)/shard_map/ppermute | solution.py:391
  39.3 10.2 %collective-permute-start.14 = (bf16[2,192,384]{2,1,0:T(8,128)(2,1)S(1)}, bf16[2,192,384]{2,1,0:T(8,128)(2,1)S(1)}, u32[]{:S(2)}, u32[]{:S(2)}) collective-permute-start(bf16[2,192,384]{2,1,0:T(8,128)(2,1)S(1)} %pack.2.refs_0_), channel_id=1, source_target_pairs={{0,16},{4,12},{8,24},{12,4},{16,0},{20,28},{24,8},{28,20},{1,17},{... | collective-permute-start | bytes 884744 | tf_op jit(solution)/shard_map/ppermute | solution.py:391
  40.1 9.9 %collective-permute-start.13 = (bf16[2,192,384]{2,1,0:T(8,128)(2,1)S(1)}, bf16[2,192,384]{2,1,0:T(8,128)(2,1)S(1)}, u32[]{:S(2)}, u32[]{:S(2)}) collective-permute-start(bf16[2,192,384]{2,1,0:T(8,128)(2,1)S(1)} %pack.2.refs_0_), channel_id=1, source_target_pairs={{0,8},{4,20},{8,0},{12,28},{16,24},{20,4},{24,16},{28,12},{1,9},{5... | collective-permute-start | bytes 884744 | tf_op jit(solution)/shard_map/ppermute | solution.py:391
  41.4 14.9 %collective-permute-start.3 = (bf16[2,192,384]{2,1,0:T(8,128)(2,1)S(1)}, bf16[2,192,384]{2,1,0:T(8,128)(2,1)S(1)}, u32[]{:S(2)}, u32[]{:S(2)}) collective-permute-start(bf16[2,192,384]{2,1,0:T(8,128)(2,1)S(1)} %copy-done.6), channel_id=1, source_target_pairs={{0,8},{4,12},{8,0},{12,4},{16,24},{20,28},{24,16},{28,20},{1,9},{5... | collective-permute-start | bytes 884744 | tf_op jit(solution)/shard_map/ppermute | solution.py:421
  42.2 15.4 %collective-permute-start.4 = (bf16[2,192,384]{2,1,0:T(8,128)(2,1)S(1)}, bf16[2,192,384]{2,1,0:T(8,128)(2,1)S(1)}, u32[]{:S(2)}, u32[]{:S(2)}) collective-permute-start(bf16[2,192,384]{2,1,0:T(8,128)(2,1)S(1)} %copy-done.5), channel_id=1, source_target_pairs={{0,16},{4,20},{8,24},{12,28},{16,0},{20,4},{24,8},{28,12},{1,17},{... | collective-permute-start | bytes 884744 | tf_op jit(solution)/shard_map/ppermute | solution.py:421
  43.4 19.9 %collective-permute-start.5 = (bf16[2,192,384]{2,1,0:T(8,128)(2,1)S(1)}, bf16[2,192,384]{2,1,0:T(8,128)(2,1)S(1)}, u32[]{:S(2)}, u32[]{:S(2)}) collective-permute-start(bf16[2,192,384]{2,1,0:T(8,128)(2,1)S(1)} %copy-done.4), channel_id=1, source_target_pairs={{0,24},{4,28},{8,16},{12,20},{16,8},{20,12},{24,0},{28,4},{1,25},{... | collective-permute-start | bytes 884744 | tf_op jit(solution)/shard_map/ppermute | solution.py:421
  45.2 18.2 %copy-start = (bf16[2,192,384]{2,1,0:T(8,128)(2,1)S(1)}, bf16[2,192,384]{2,1,0:T(8,128)(2,1)}, u32[]{:S(2)}) copy-start(bf16[2,192,384]{2,1,0:T(8,128)(2,1)} %get-tuple-element.65.refs_0_) | copy-start | bytes 884740
  49.5 20.8 %collective-permute-start.21 = (bf16[3,2,192,384]{3,2,1,0:T(8,128)(2,1)S(1)}, bf16[3,2,192,384]{3,2,1,0:T(8,128)(2,1)S(1)}, u32[]{:S(2)}, u32[]{:S(2)}) collective-permute-start(bf16[3,2,192,384]{3,2,1,0:T(8,128)(2,1)S(1)} %join.6.early.rest_4_), channel_id=1, source_target_pairs={{0,4},{4,0},{8,12},{12,8},{16,20},{20,16},{24,28},{28,24},{1,5},{5... | collective-permute-start | bytes 2654216 | tf_op jit(solution)/shard_map/ppermute | solution.py:387
  50.2 21.0 %collective-permute-start.15 = (bf16[3,2,192,384]{3,2,1,0:T(8,128)(2,1)S(1)}, bf16[3,2,192,384]{3,2,1,0:T(8,128)(2,1)S(1)}, u32[]{:S(2)}, u32[]{:S(2)}) collective-permute-start(bf16[3,2,192,384]{3,2,1,0:T(8,128)(2,1)S(1)} %join.5.early.rest_0_), channel_id=1, source_target_pairs={{0,4},{4,0},{8,12},{12,8},{16,20},{20,16},{24,28},{28,24},{1,5},{5... | collective-permute-start | bytes 2654216 | tf_op jit(solution)/shard_map/ppermute | solution.py:387
  56.3 8.5 %collective-permute-start.23 = (bf16[2,192,384]{2,1,0:T(8,128)(2,1)S(1)}, bf16[2,192,384]{2,1,0:T(8,128)(2,1)S(1)}, u32[]{:S(2)}, u32[]{:S(2)}) collective-permute-start(bf16[2,192,384]{2,1,0:T(8,128)(2,1)S(1)} %collective-permute-done.19.refs_1_), channel_id=1, source_target_pairs={{0,16},{4,12},{8,24},{12,4},{16,0},{20,28},{24,8},{28,20},{1,17},{... | collective-permute-start | bytes 884744 | tf_op jit(solution)/shard_map/ppermute | solution.py:391
  57.6 10.3 %collective-permute-start.22 = (bf16[2,192,384]{2,1,0:T(8,128)(2,1)S(1)}, bf16[2,192,384]{2,1,0:T(8,128)(2,1)S(1)}, u32[]{:S(2)}, u32[]{:S(2)}) collective-permute-start(bf16[2,192,384]{2,1,0:T(8,128)(2,1)S(1)} %collective-permute-done.13.refs_1_), channel_id=1, source_target_pairs={{0,16},{4,12},{8,24},{12,4},{16,0},{20,28},{24,8},{28,20},{1,17},{... | collective-permute-start | bytes 884744 | tf_op jit(solution)/shard_map/ppermute | solution.py:391
  63.4 4.8 %copy-start.2 = (s32[384]{0:T(512)S(1)}, s32[384]{0:T(512)}, u32[]{:S(2)}) copy-start(s32[384]{0:T(512)} %param.10) | copy-start | bytes 4612
  64.2 4.1 %collective-permute-start.6 = (bf16[4,192,384]{2,1,0:T(8,128)(2,1)S(1)}, bf16[4,192,384]{2,1,0:T(8,128)(2,1)S(1)}, u32[]{:S(2)}, u32[]{:S(2)}) collective-permute-start(bf16[4,192,384]{2,1,0:T(8,128)(2,1)S(1)} %join.4), channel_id=1, source_target_pairs={{0,4},{4,0},{8,12},{12,8},{16,20},{20,16},{24,28},{28,24},{1,5},{5... | collective-permute-start | bytes 1769480 | tf_op jit(solution)/shard_map/ppermute | solution.py:387
  68.1 4.0 %collective-permute-start.24 = (bf16[2,2,192,384]{3,2,1,0:T(8,128)(2,1)S(1)}, bf16[2,2,192,384]{3,2,1,0:T(8,128)(2,1)S(1)}, u32[]{:S(2)}, u32[]{:S(2)}) collective-permute-start(bf16[2,2,192,384]{3,2,1,0:T(8,128)(2,1)S(1)} %join.7.rest_8_), channel_id=1, source_target_pairs={{0,4},{4,0},{8,12},{12,8},{16,20},{20,16},{24,28},{28,24},{1,5},{5... | collective-permute-start | bytes 1769480 | tf_op jit(solution)/shard_map/ppermute | solution.py:387
  71.2 0.9 %copy-start.1 = (s32[32]{0:T(128)S(1)}, s32[32]{0:T(128)}, u32[]{:S(2)}) copy-start(s32[32]{0:T(128)} %occ_ref.1) | copy-start | bytes 388

commit v3 on v2

--- a/solution.py
+++ b/solution.py
@@ -139,9 +139,13 @@
             pltpu.VMEM((n_orb, rows, n_virt), BF16),
             pltpu.SemaphoreType.DMA((n + 1,)),
         ],
-        compiler_params=pltpu.CompilerParams(vmem_limit_bytes=60 << 20),
+        compiler_params=pltpu.CompilerParams(vmem_limit_bytes=20 << 20),
         name="transform",
-    )(plan, half_slabs.reshape(local_aux * n_orb, n_ao), coeff)
+    )(
+        plan,
+        pltpu.with_memory_space_constraint(half_slabs.reshape(local_aux * n_orb, n_ao), pltpu.HBM),
+        pltpu.with_memory_space_constraint(coeff, pltpu.HBM),
+    )
 
 
 def merge_kernel(plan_ref, *refs, n_orb, n_half, spilled):
@@ -237,50 +241,58 @@
 
 
 def prep_kernel(*refs):
-    near, other, own_t, own_v, sem = refs[:-4], refs[-4], refs[-3], refs[-2], refs[-1]
+    near, other, own_t = refs[:-2], refs[-2], refs[-1]
+    chips = len(near)
     aux = lax.axis_index("aux")
+    core = lax.rem(aux, 2)
+    width = 2 * other.shape[1]
+    for r in range(chips):
+        mine, theirs = near[r][0], other[r]
+        pair = jnp.concatenate([jnp.where(core == 0, mine, theirs), jnp.where(core == 0, theirs, mine)], axis=0)
+        at = pl.multiple_of(lax.bitwise_xor(lax.div(aux, 2), r) * width, width)
+        own_t[:, pl.ds(at, width)] = jnp.transpose(pair)
+
+
+def prep(near, other):
+    _, rows, n_virt = other.shape
+    vmem = pl.BlockSpec(memory_space=pltpu.VMEM)
+    return pl.pallas_call(
+        prep_kernel,
+        in_specs=[vmem] * (len(near) + 1),
+        out_specs=vmem,
+        out_shape=jax.ShapeDtypeStruct((n_virt, 2 * len(near) * rows), BF16),
+        compiler_params=pltpu.CompilerParams(vmem_limit_bytes=8 << 20),
+        name="prep",
+    )(*near, other)
+
+
+def amp_kernel(own_t, early, other, k_ref, here_ref, beside_ref, sem):
+    _, per, rows, _ = early.shape
+    aux = lax.axis_index("aux")
+    core = lax.rem(aux, 2)
+    half, quarter = here_ref.shape[1], beside_ref.shape[1]
+    side = lax.rem(aux, Y)
     copies = []
-    for r in range(len(near)):
-        for src, bits in ((near[r].at[0], 2 * r), (other.at[r], 2 * r + 1)):
-            at = lax.bitwise_xor(aux, bits)
-            copies.append(pltpu.make_async_copy(src, own_v.at[at], sem.at[len(copies)]))
+    for src, block, out in (
+        (early.at[0], side, here_ref),
+        (early.at[1 + core], lax.bitwise_xor(side, X), here_ref),
+        (other.at[0], lax.bitwise_xor(side, CORE), here_ref),
+        (other.at[2 - core], lax.bitwise_xor(side, X | CORE), here_ref),
+        (early.at[2 - core], core, beside_ref),
+        (other.at[1 + core], 1 - core, beside_ref),
+    ):
+        at = pl.multiple_of(block * rows, rows)
+        copies.append(pltpu.make_async_copy(src, out.at[:, pl.ds(at, rows)], sem.at[len(copies)]))
     for c in copies:
         c.start()
     for c in copies:
         c.wait()
-    own_t[...] = jnp.transpose(own_v[...].reshape(own_t.shape[1], own_t.shape[0]))
-
-
-def prep(near, other):
-    chips, rows, n_virt = other.shape
-    return pl.pallas_call(
-        prep_kernel,
-        in_specs=[pl.BlockSpec(memory_space=pl.ANY)] * (chips + 1),
-        out_specs=pl.BlockSpec(memory_space=pltpu.VMEM),
-        out_shape=jax.ShapeDtypeStruct((n_virt, 2 * chips * rows), BF16),
-        scratch_shapes=[pltpu.VMEM((2 * chips, rows, n_virt), BF16), pltpu.SemaphoreType.DMA((2 * chips,))],
-        compiler_params=pltpu.CompilerParams(vmem_limit_bytes=8 << 20),
-        name="prep",
-    )(*near, other)
-
-
-def amp_kernel(own_t, early, other, out_ref, part_v, sem):
-    _, per, rows, _ = early.shape
-    aux = lax.axis_index("aux")
-    core = lax.rem(aux, 2)
-    half = part_v.shape[1]
-    side = lax.rem(aux, Y)
-    copies = []
-    for src, bits in ((early.at[0], 0), (early.at[1 + core], X), (other.at[0], CORE), (other.at[2 - core], X | CORE)):
-        at = pl.multiple_of(lax.bitwise_xor(side, bits) * rows, rows)
-        copies.append(pltpu.make_async_copy(src, part_v.at[:, pl.ds(at, rows)], sem.at[len(copies)]))
-    for c in copies:
-        c.start()
-    for c in copies:
-        c.wait()
-    part = jnp.concatenate([part_v[s] for s in range(per)], axis=1)
-    own = own_t[:, pl.ds(pl.multiple_of(lax.div(aux, Y) * half, half), half)]
-    out_ref[...] = jnp.dot(own, part, preferred_element_type=F32)
+    here = pl.multiple_of(lax.div(aux, Y) * half, half)
+    beside = pl.multiple_of(lax.bitwise_xor(lax.div(aux, 2), Y // 2) * quarter, quarter)
+    part = jnp.concatenate([here_ref[s] for s in range(per)], axis=1)
+    k = jnp.dot(own_t[:, pl.ds(here, half)], part, preferred_element_type=F32)
+    part = jnp.concatenate([beside_ref[s] for s in range(per)], axis=1)
+    k_ref[...] = k + jnp.dot(own_t[:, pl.ds(beside, quarter)], part, preferred_element_type=F32)
 
 
 def amplitudes(own, early, other):
@@ -291,12 +303,13 @@
     return pl.pallas_call(
         amp_kernel,
         in_specs=[vmem, anym, anym],
-        out_specs=[vmem, vmem],
+        out_specs=[vmem] * 3,
         out_shape=[
             jax.ShapeDtypeStruct((n_virt, per * n_virt), F32),
             jax.ShapeDtypeStruct((per, n_aux // 2, n_virt), BF16),
+            jax.ShapeDtypeStruct((per, n_aux // 4, n_virt), BF16),
         ],
-        scratch_shapes=[pltpu.SemaphoreType.DMA((4,))],
+        scratch_shapes=[pltpu.SemaphoreType.DMA((6,))],
         compiler_params=pltpu.CompilerParams(vmem_limit_bytes=12 << 20),
         cost_estimate=pl.CostEstimate(flops=per * n_virt * n_virt * n_aux, bytes_accessed=3 << 20, transcendentals=0),
         name="amplitudes",
@@ -304,40 +317,29 @@
 
 
 def pair_kernel(occ_ref, plan_ref, row_ref, col_ref, own_t, *rest, n_orb, groups):
-    ins = rest[:4 * groups]
-    late, late_other = rest[4 * groups:4 * groups + 2]
-    dens_ref, energy_ref, part_v, dens_v, sem, out_sem = rest[4 * groups + 2:]
+    ins = rest[:3 * groups]
+    late, late_other, dens_ref, energy_ref, part_v, dens_v, sem, out_sem = rest[3 * groups:]
     _, per, rows, n_virt = late.shape
-    half = part_v.shape[1]
+    quarter = part_v.shape[2]
+    half = 2 * quarter
     z, aux = lax.axis_index("half"), lax.axis_index("aux")
     core = lax.rem(aux, 2)
-    here = pl.multiple_of(lax.div(aux, Y) * half, half)
-    there = pl.multiple_of((1 - lax.div(aux, Y)) * half, half)
-    side = lax.rem(aux, Y)
     copies = []
-    for g in range(groups):
-        early, other = ins[4 * g:4 * g + 2]
-        for src, bits in (
-            (early.at[2 - core], 0),
-            (late.at[g], X),
-            (other.at[1 + core], CORE),
-            (late_other.at[g], X | CORE),
-        ):
-            at = pl.multiple_of(lax.bitwise_xor(side, bits) * rows, rows)
-            dst = part_v.at[pl.ds(g * per, per), pl.ds(at, rows)]
-            copies.append(pltpu.make_async_copy(src, dst, sem.at[len(copies)]))
-    for c in copies:
-        c.start()
+    for i, (src, block) in enumerate(((late, core), (late_other, 1 - core))):
+        at = pl.multiple_of(block * rows, rows)
+        copies.append(pltpu.make_async_copy(src, part_v.at[:, :, pl.ds(at, rows)], sem.at[i]))
+        copies[-1].start()
     own_e = occ_ref[z * n_orb + aux].astype(F32) * 0.001
     row = row_ref[...].astype(F32) * 0.001
     col = col_ref[...].astype(F32) * 0.001
     energy = jnp.zeros((1, 1), F32)
+    across = pl.multiple_of(lax.bitwise_xor(lax.div(aux, 2), (X | Y) // 2) * quarter, quarter)
     for c in copies:
         c.wait()
     tildes = []
     for g in range(groups):
-        part = jnp.concatenate([part_v[g * per + s] for s in range(per)], axis=1)
-        kk = ins[4 * g + 2][...] + jnp.dot(own_t[:, pl.ds(there, half)], part, preferred_element_type=F32)
+        part = jnp.concatenate([part_v[g, s] for s in range(per)], axis=1)
+        kk = ins[3 * g][...] + jnp.dot(own_t[:, pl.ds(across, quarter)], part, preferred_element_type=F32)
         for s in range(per):
             k = kk[:, s * n_virt:(s + 1) * n_virt]
             part_e = occ_ref[plan_ref[0, g * per + s]].astype(F32) * 0.001
@@ -347,18 +349,32 @@
             tildes.append(tilde.astype(BF16))
     tb = jnp.concatenate(tildes, axis=1)
     saves = []
-    for i, (at, parts) in enumerate((
-        (here, [ins[4 * g + 3][s] for g in range(groups) for s in range(per)]),
-        (there, [part_v[s] for s in range(groups * per)]),
-    )):
-        part = jnp.concatenate(parts, axis=1)
-        total = lax.dot_general(tb, part, (((1,), (1,)), ((), ())), preferred_element_type=F32)
-        dens_v[i] = total.astype(BF16)
-        saves.append(pltpu.make_async_copy(dens_v.at[i], dens_ref.at[:, pl.ds(at, half)], out_sem.at[i]))
+
+    def save(i, block, at, size):
+        dst = dens_ref.at[:, pl.ds(pl.multiple_of(at, size), size)]
+        saves.append(pltpu.make_async_copy(block, dst, out_sem.at[i]))
         saves[-1].start()
+
+    slots = [(g, s) for g in range(groups) for s in range(per)]
+    part = jnp.concatenate([ins[3 * g + 1][s] for g, s in slots], axis=1)
+    total = lax.dot_general(tb, part, (((1,), (1,)), ((), ())), preferred_element_type=F32)
+    dens_v[0] = total.astype(BF16)
+    save(0, dens_v.at[0], lax.div(aux, Y) * half, half)
+    part = jnp.concatenate(
+        [
+            jnp.concatenate([ins[3 * g + 2][s] for g, s in slots], axis=1),
+            jnp.concatenate([part_v[g, s] for g, s in slots], axis=1),
+        ],
+        axis=0,
+    )
+    total = lax.dot_general(tb, part, (((1,), (1,)), ((), ())), preferred_element_type=F32)
+    dens_v[1] = total.astype(BF16)
+    beside = lax.bitwise_xor(lax.div(aux, 2), Y // 2) * quarter
+    save(1, dens_v.at[1, :, pl.ds(0, quarter)], beside, quarter)
+    save(2, dens_v.at[1, :, pl.ds(quarter, quarter)], across, quarter)
+    energy_ref[...] = energy / (n_virt * n_virt)
     for c in saves:
         c.wait()
-    energy_ref[...] = energy / (n_virt * n_virt)
 
 
 def pair_terms(own, ins, late, late_other, occ, plan, vir, n_orb):
@@ -369,14 +385,14 @@
     anym = pl.BlockSpec(memory_space=pl.ANY)
     return pl.pallas_call(
         functools.partial(pair_kernel, n_orb=n_orb, groups=groups),
-        in_specs=[smem] * 2 + [vmem] * 3 + [anym, anym, vmem, vmem] * groups + [anym] * 2,
+        in_specs=[smem] * 2 + [vmem] * (3 + len(ins)) + [anym] * 2,
         out_specs=[pl.BlockSpec(memory_space=pltpu.HBM), vmem],
         out_shape=[jax.ShapeDtypeStruct((n_virt, n_aux), BF16), jax.ShapeDtypeStruct((1, 1), F32)],
         scratch_shapes=[
-            pltpu.VMEM((groups * per, n_aux // 2, n_virt), BF16),
+            pltpu.VMEM((groups, per, n_aux // 4, n_virt), BF16),
             pltpu.VMEM((2, n_virt, n_aux // 2), BF16),
-            pltpu.SemaphoreType.DMA((groups * 4,)),
             pltpu.SemaphoreType.DMA((2,)),
+            pltpu.SemaphoreType.DMA((3,)),
         ],
         compiler_params=pltpu.CompilerParams(vmem_limit_bytes=24 << 20),
         name="pair_terms",
@@ -442,7 +458,7 @@
         late.append(plane(r1, n_aux, 1))
         early = join([z0, r1, r2])
         other = swap(early, n_aux)
-        ins += [early, other, *amplitudes(own, early, other)]
+        ins += amplitudes(own, early, other)
     late = join(late)
     late_other = swap(late, n_aux)
     density, energy = pair_terms(own, ins, late, late_other, occ_energy, plan, vir_energy, ohalf)

time: 77.6 us -> 73.9 us (0.952)
  waiting for transfers between devices: 33.6 us -> 30.7 us
  Pallas kernels: 17.2 us -> 14.9 us
  starting transfers between devices: 25 us -> 26.5 us
    ppermute x9, waiting for transfers between devices: 14 us -> 11 us  [shift(): return lax.ppermute(x, 'half', [(h, (h + d) % n) for h in range(n)])]
    ppermute x6, waiting for transfers between devices: 8.56 us -> 10 us  [plane(): lax.ppermute(x, 'aux', [(a, a ^ (Y if a & CORE ^ flip else X)) for a in r...]
    ppermute x9, starting transfers between devices: 14.2 us -> 15.6 us  [shift(): return lax.ppermute(x, 'half', [(h, (h + d) % n) for h in range(n)])]
    ppermute x3, waiting for transfers between devices: 11 us -> 9.73 us  [stages(): lax.ppermute(near[r], 'aux', [(a, a ^ 2 * r) for a in range(n_aux)])]
    pallas_call x1, Pallas kernels: 5.83 us -> 4.83 us  [transform(): pl.pallas_call(functools.partial(transform_kernel, n_half=n_half, order=o...]
    pallas_call x3, Pallas kernels: 3.68 us -> 2.88 us  [the longest x2 2.49 us: amplitudes(): pl.pallas_call(amp_kernel, in_specs=[vmem, anym, anym], out_specs=[vmem]...]
  transfers between devices with their start and end apart: 22 -> 22, of which waited for: 13 -> 14; matrix products, arithmetic and copies ran while one was open for 0% -> 0% of each run, Pallas kernels for 7% -> 6%
where the time goes in v3:
time: 73.9 us; the launch traced here: 73.7 us
  waiting for transfers between devices  30.7 us (42%)
  starting transfers between devices  26.5 us (36%)
  Pallas kernels  14.9 us (20%)
  between operations  1.49 us (2%)
    ppermute x9, starting transfers between devices, shift(): return lax.ppermute(x, 'half', [(h, (h + d) % n) for h in range(n)])  15.6 us
    ppermute x9, waiting for transfers between devices, shift(): return lax.ppermute(x, 'half', [(h, (h + d) % n) for h in range(n)])  11 us
    ppermute x6, waiting for transfers between devices, plane(): lax.ppermute(x, 'aux', [(a, a ^ (Y if a & CORE ^ flip else X)) for a in r...  10 us
    ppermute x3, waiting for transfers between devices, stages(): lax.ppermute(near[r], 'aux', [(a, a ^ 2 * r) for a in range(n_aux)])  9.73 us
    ppermute x6, starting transfers between devices, plane(): lax.ppermute(x, 'aux', [(a, a ^ (Y if a & CORE ^ flip else X)) for a in r...  7.16 us
    pallas_call x1, Pallas kernels, pair_terms(): pl.pallas_call(functools.partial(pair_kernel, n_orb=n_orb, groups=groups)...  4.85 us
    pallas_call x1, Pallas kernels, transform(): pl.pallas_call(functools.partial(transform_kernel, n_half=n_half, order=o...  4.83 us
    ppermute x3, starting transfers between devices, stages(): lax.ppermute(near[r], 'aux', [(a, a ^ 2 * r) for a in range(n_aux)])  3.49 us
  transfers between devices with their start and end apart: 22, of which 14 were waited for; matrix products, arithmetic and copies ran while one was open for 0% of the time, Pallas kernels for 6%

profile of v3, /device:TPU:0, one launch (start us, length us, event | category | flops | bytes accessed | tf_op | source)
XLA Modules:
  0.0 73.7 jit_solution(15245669487217527812)
XLA Ops:
  0.6 4.8 %transform.1 = (s32[1]{0:T(128)}, bf16[2,192,384]{2,1,0:T(8,128)(2,1)S(1)}, bf16[2,192,384]{2,1,0:T(8,128)(2,1)S(1)}, bf16[2,192,384]{2,1,0:T(8,128)(2,1)S(1)}, ...) custom-call(s32[1,4]{1,0:T(1,128)} %plan_ref.3, ...), custom_call_target="tpu_custom_call" | custom-call | tf_op jit(solution)/shard_map/transform/pallas_call | solution.py:125
  5.5 3.1 %collective-permute-start.7 = (bf16[2,48,384]{2,1,0:T(8,128)(2,1)S(1)}, bf16[2,48,384]{2,1,0:T(8,128)(2,1)S(1)}, u32[]{:S(2)}, u32[]{:S(2)}) collective-permute-start(bf16[2,48,384]{2,1,0:T(8,128)(2,1)S(1)} %get-tuple-element.73), channel_id=1, source_target_pairs={{0,1},{1,2},{2,3},{3,0},{4,5},{5,6},{6,7},{7,4},{8,9},{9,10},{10,1... | collective-permute-start | bytes 221192 | tf_op jit(solution)/shard_map/ppermute | solution.py:411
  8.6 2.6 %collective-permute-start.8 = (bf16[2,48,384]{2,1,0:T(8,128)(2,1)S(1)}, bf16[2,48,384]{2,1,0:T(8,128)(2,1)S(1)}, u32[]{:S(2)}, u32[]{:S(2)}) collective-permute-start(bf16[2,48,384]{2,1,0:T(8,128)(2,1)S(1)} %get-tuple-element.74), channel_id=1, source_target_pairs={{0,2},{1,3},{2,0},{3,1},{4,6},{5,7},{6,4},{7,5},{8,10},{9,11},{10,... | collective-permute-start | bytes 221192 | tf_op jit(solution)/shard_map/ppermute | solution.py:411
  11.2 1.3 %collective-permute-start.9 = (bf16[2,48,384]{2,1,0:T(8,128)(2,1)S(1)}, bf16[2,48,384]{2,1,0:T(8,128)(2,1)S(1)}, u32[]{:S(2)}, u32[]{:S(2)}) collective-permute-start(bf16[2,48,384]{2,1,0:T(8,128)(2,1)S(1)} %get-tuple-element.75), channel_id=1, source_target_pairs={{0,3},{1,0},{2,1},{3,2},{4,7},{5,4},{6,5},{7,6},{8,11},{9,8},{10,9... | collective-permute-start | bytes 221192 | tf_op jit(solution)/shard_map/ppermute | solution.py:411
  13.3 2.9 %collective-permute-done.8 = bf16[2,48,384]{2,1,0:T(8,128)(2,1)S(1)} collective-permute-done((bf16[2,48,384]{2,1,0:T(8,128)(2,1)S(1)}, bf16[2,48,384]{2,1,0:T(8,128)(2,1)S(1)}, u32[]{:S(2)}, u32[]{:S(2)}) %collective-permute-start.8) | collective-permute-done | bytes 73760 | tf_op jit(solution)/shard_map/ppermute | solution.py:411
  16.4 0.9 %conditional.1 = ((bf16[2,48,384]{2,1,0:T(8,128)(2,1)S(1)}, bf16[2,48,384]{2,1,0:T(8,128)(2,1)S(1)})) conditional(s32[]{:T(128)} %bitcast.1, (s32[1,4]{1,0:T(1,128)S(1)}, bf16[2,48,384]{2,1,0:T(8,128)(2,1)S(1)}, bf16[2,48,384]{2,1,0:T(8,128)(2,1)S(1)}, bf16[2,48,384]{2,1,0:T(8,128)(2,1)S(1)}, bf16[2,48,384]{2,1,0:T(8,128)(2,1)S(1)}) %tuple.21, ...), branch_computations={%region_0.0_spmd, %region_1.0_spmd} | conditional | bytes 884864 | solution.py:449
  16.4 0.9 %merge.2 = (bf16[2,48,384]{2,1,0:T(8,128)(2,1)S(1)}, bf16[2,48,384]{2,1,0:T(8,128)(2,1)S(1)}) custom-call(s32[1,4]{1,0:T(1,128)S(1)} %get-tuple-element.28.plan_ref, bf16[2,48,384]{2,1,0:T(8,128)(2,1)S(1)} %get-tuple-element.29.refs_0_, bf16[2,48,384]{2,1,0:T(8,128)(2,1)S(1)} %get-tuple-element.30.refs_1_, ...), custom_call_target="tpu_custom_call" | custom-call | tf_op jit(solution)/shard_map/cond/branch_0_fun/merge/pallas_call | solution.py:182
  17.3 1.9 %collective-permute-start.10 = (bf16[2,48,384]{2,1,0:T(8,128)(2,1)S(1)}, bf16[2,48,384]{2,1,0:T(8,128)(2,1)S(1)}, u32[]{:S(2)}, u32[]{:S(2)}) collective-permute-start(bf16[2,48,384]{2,1,0:T(8,128)(2,1)S(1)} %get-tuple-element.80.refs_0_), channel_id=1, source_target_pairs={{0,1},{1,2},{2,3},{3,0},{4,5},{5,6},{6,7},{7,4},{8,9},{9,10},{10,1... | collective-permute-start | bytes 221192 | tf_op jit(solution)/shard_map/ppermute | solution.py:411
  19.2 1.9 %collective-permute-start.11 = (bf16[2,48,384]{2,1,0:T(8,128)(2,1)S(1)}, bf16[2,48,384]{2,1,0:T(8,128)(2,1)S(1)}, u32[]{:S(2)}, u32[]{:S(2)}) collective-permute-start(bf16[2,48,384]{2,1,0:T(8,128)(2,1)S(1)} %get-tuple-element.80.refs_0_), channel_id=1, source_target_pairs={{0,2},{1,3},{2,0},{3,1},{4,6},{5,7},{6,4},{7,5},{8,10},{9,11},{10,... | collective-permute-start | bytes 221192 | tf_op jit(solution)/shard_map/ppermute | solution.py:411
  21.8 2.2 %collective-permute-done.10.refs_1_ = bf16[2,48,384]{2,1,0:T(8,128)(2,1)S(1)} collective-permute-done((bf16[2,48,384]{2,1,0:T(8,128)(2,1)S(1)}, bf16[2,48,384]{2,1,0:T(8,128)(2,1)S(1)}, u32[]{:S(2)}, u32[]{:S(2)}) %collective-permute-start.10) | collective-permute-done | bytes 73760 | tf_op jit(solution)/shard_map/ppermute | solution.py:411
  24.0 2.2 %collective-permute-done.11.refs_2_ = bf16[2,48,384]{2,1,0:T(8,128)(2,1)S(1)} collective-permute-done((bf16[2,48,384]{2,1,0:T(8,128)(2,1)S(1)}, bf16[2,48,384]{2,1,0:T(8,128)(2,1)S(1)}, u32[]{:S(2)}, u32[]{:S(2)}) %collective-permute-start.11) | collective-permute-done | bytes 73760 | tf_op jit(solution)/shard_map/ppermute | solution.py:411
  26.5 1.5 %collective-permute-start.13 = (bf16[2,192,384]{2,1,0:T(8,128)(2,1)S(1)}, bf16[2,192,384]{2,1,0:T(8,128)(2,1)S(1)}, u32[]{:S(2)}, u32[]{:S(2)}) collective-permute-start(bf16[2,192,384]{2,1,0:T(8,128)(2,1)S(1)} %pack.2.refs_0_), channel_id=1, source_target_pairs={{0,8},{4,20},{8,0},{12,28},{16,24},{20,4},{24,16},{28,12},{1,9},{5... | collective-permute-start | bytes 884744 | tf_op jit(solution)/shard_map/ppermute | solution.py:407
  28.0 1.7 %collective-permute-start.16 = (bf16[2,48,384]{2,1,0:T(8,128)(2,1)S(1)}, bf16[2,48,384]{2,1,0:T(8,128)(2,1)S(1)}, u32[]{:S(2)}, u32[]{:S(2)}) collective-permute-start(bf16[2,48,384]{2,1,0:T(8,128)(2,1)S(1)} %get-tuple-element.84.refs_0_), channel_id=1, source_target_pairs={{0,1},{1,2},{2,3},{3,0},{4,5},{5,6},{6,7},{7,4},{8,9},{9,10},{10,1... | collective-permute-start | bytes 221192 | tf_op jit(solution)/shard_map/ppermute | solution.py:411
  29.7 1.4 %collective-permute-start.17 = (bf16[2,48,384]{2,1,0:T(8,128)(2,1)S(1)}, bf16[2,48,384]{2,1,0:T(8,128)(2,1)S(1)}, u32[]{:S(2)}, u32[]{:S(2)}) collective-permute-start(bf16[2,48,384]{2,1,0:T(8,128)(2,1)S(1)} %get-tuple-element.84.refs_0_), channel_id=1, source_target_pairs={{0,2},{1,3},{2,0},{3,1},{4,6},{5,7},{6,4},{7,5},{8,10},{9,11},{10,... | collective-permute-start | bytes 221192 | tf_op jit(solution)/shard_map/ppermute | solution.py:411
  31.1 1.0 %collective-permute-start.18 = (bf16[2,48,384]{2,1,0:T(8,128)(2,1)S(1)}, bf16[2,48,384]{2,1,0:T(8,128)(2,1)S(1)}, u32[]{:S(2)}, u32[]{:S(2)}) collective-permute-start(bf16[2,48,384]{2,1,0:T(8,128)(2,1)S(1)} %get-tuple-element.84.refs_0_), channel_id=1, source_target_pairs={{0,3},{1,0},{2,1},{3,2},{4,7},{5,4},{6,5},{7,6},{8,11},{9,8},{10,9... | collective-permute-start | bytes 221192 | tf_op jit(solution)/shard_map/ppermute | solution.py:411
  32.1 1.5 %collective-permute-start.14 = (bf16[2,192,384]{2,1,0:T(8,128)(2,1)S(1)}, bf16[2,192,384]{2,1,0:T(8,128)(2,1)S(1)}, u32[]{:S(2)}, u32[]{:S(2)}) collective-permute-start(bf16[2,192,384]{2,1,0:T(8,128)(2,1)S(1)} %pack.2.refs_0_), channel_id=1, source_target_pairs={{0,16},{4,12},{8,24},{12,4},{16,0},{20,28},{24,8},{28,20},{1,17},{... | collective-permute-start | bytes 884744 | tf_op jit(solution)/shard_map/ppermute | solution.py:407
  33.6 0.8 %collective-permute-done.16.refs_1_ = bf16[2,48,384]{2,1,0:T(8,128)(2,1)S(1)} collective-permute-done((bf16[2,48,384]{2,1,0:T(8,128)(2,1)S(1)}, bf16[2,48,384]{2,1,0:T(8,128)(2,1)S(1)}, u32[]{:S(2)}, u32[]{:S(2)}) %collective-permute-start.16) | collective-permute-done | bytes 73760 | tf_op jit(solution)/shard_map/ppermute | solution.py:411
  34.4 2.2 %collective-permute-done.17.refs_2_ = bf16[2,48,384]{2,1,0:T(8,128)(2,1)S(1)} collective-permute-done((bf16[2,48,384]{2,1,0:T(8,128)(2,1)S(1)}, bf16[2,48,384]{2,1,0:T(8,128)(2,1)S(1)}, u32[]{:S(2)}, u32[]{:S(2)}) %collective-permute-start.17) | collective-permute-done | bytes 73760 | tf_op jit(solution)/shard_map/ppermute | solution.py:411
  36.7 1.4 %collective-permute-start.19 = (bf16[2,192,384]{2,1,0:T(8,128)(2,1)S(1)}, bf16[2,192,384]{2,1,0:T(8,128)(2,1)S(1)}, u32[]{:S(2)}, u32[]{:S(2)}) collective-permute-start(bf16[2,192,384]{2,1,0:T(8,128)(2,1)S(1)} %pack.3.refs_0_), channel_id=1, source_target_pairs={{0,8},{4,20},{8,0},{12,28},{16,24},{20,4},{24,16},{28,12},{1,9},{5... | collective-permute-start | bytes 884744 | tf_op jit(solution)/shard_map/ppermute | solution.py:407
  38.9 1.2 %collective-permute-start.3 = (bf16[2,192,384]{2,1,0:T(8,128)(2,1)S(1)}, bf16[2,192,384]{2,1,0:T(8,128)(2,1)S(1)}, u32[]{:S(2)}, u32[]{:S(2)}) collective-permute-start(bf16[2,192,384]{2,1,0:T(8,128)(2,1)S(1)} %get-tuple-element.68), channel_id=1, source_target_pairs={{0,8},{4,12},{8,0},{12,4},{16,24},{20,28},{24,16},{28,20},{1,9},{5... | collective-permute-start | bytes 884744 | tf_op jit(solution)/shard_map/ppermute | solution.py:437
  40.8 1.5 %collective-permute-start.5 = (bf16[2,192,384]{2,1,0:T(8,128)(2,1)S(1)}, bf16[2,192,384]{2,1,0:T(8,128)(2,1)S(1)}, u32[]{:S(2)}, u32[]{:S(2)}) collective-permute-start(bf16[2,192,384]{2,1,0:T(8,128)(2,1)S(1)} %get-tuple-element.70), channel_id=1, source_target_pairs={{0,24},{4,28},{8,16},{12,20},{16,8},{20,12},{24,0},{28,4},{1,25},{... | collective-permute-start | bytes 884744 | tf_op jit(solution)/shard_map/ppermute | solution.py:437
  42.6 4.1 %collective-permute-done.19.refs_1_ = bf16[2,192,384]{2,1,0:T(8,128)(2,1)S(1)} collective-permute-done((bf16[2,192,384]{2,1,0:T(8,128)(2,1)S(1)}, bf16[2,192,384]{2,1,0:T(8,128)(2,1)S(1)}, u32[]{:S(2)}, u32[]{:S(2)}) %collective-permute-start.19) | collective-permute-done | bytes 294944 | tf_op jit(solution)/shard_map/ppermute | solution.py:407
  46.7 1.3 %collective-permute-done.20.refs_2_ = bf16[2,192,384]{2,1,0:T(8,128)(2,1)S(1)} collective-permute-done((bf16[2,192,384]{2,1,0:T(8,128)(2,1)S(1)}, bf16[2,192,384]{2,1,0:T(8,128)(2,1)S(1)}, u32[]{:S(2)}, u32[]{:S(2)}) %collective-permute-start.20) | collective-permute-done | bytes 294944 | tf_op jit(solution)/shard_map/ppermute | solution.py:407
  48.3 4.7 %collective-permute-done.3.refs_1_ = bf16[2,192,384]{2,1,0:T(8,128)(2,1)S(1)} collective-permute-done((bf16[2,192,384]{2,1,0:T(8,128)(2,1)S(1)}, bf16[2,192,384]{2,1,0:T(8,128)(2,1)S(1)}, u32[]{:S(2)}, u32[]{:S(2)}) %collective-permute-start.3) | collective-permute-done | bytes 294944 | tf_op jit(solution)/shard_map/ppermute | solution.py:437
  53.0 1.3 %collective-permute-start.22 = (bf16[2,192,384]{2,1,0:T(8,128)(2,1)S(1)}, bf16[2,192,384]{2,1,0:T(8,128)(2,1)S(1)}, u32[]{:S(2)}, u32[]{:S(2)}) collective-permute-start(bf16[2,192,384]{2,1,0:T(8,128)(2,1)S(1)} %collective-permute-done.13.refs_1_), channel_id=1, source_target_pairs={{0,16},{4,12},{8,24},{12,4},{16,0},{20,28},{24,8},{28,20},{1,17},{... | collective-permute-start | bytes 884744 | tf_op jit(solution)/shard_map/ppermute | solution.py:407
  55.0 5.1 %collective-permute-done.5.refs_3_ = bf16[2,192,384]{2,1,0:T(8,128)(2,1)S(1)} collective-permute-done((bf16[2,192,384]{2,1,0:T(8,128)(2,1)S(1)}, bf16[2,192,384]{2,1,0:T(8,128)(2,1)S(1)}, u32[]{:S(2)}, u32[]{:S(2)}) %collective-permute-start.5) | collective-permute-done | bytes 294944 | tf_op jit(solution)/shard_map/ppermute | solution.py:437
  60.1 0.8 %join.4 = bf16[4,192,384]{2,1,0:T(8,128)(2,1)S(1)} custom-call(bf16[2,192,384]{2,1,0:T(8,128)(2,1)S(1)} %get-tuple-element.67.refs_0_, bf16[2,192,384]{2,1,0:T(8,128)(2,1)S(1)} %collective-permute-done.3.refs_1_, bf16[2,192,384]{2,1,0:T(8,128)(2,1)S(1)} %collective-permute-done.4.refs_2_, bf16[2,192,384]{2,1,0:T(8,128)(2,1)S(1)} %collective-permute-done.5.refs_3_), custom_call_target="tpu_custom_call" | custom-call | tf_op jit(solution)/shard_map/join/pallas_call | solution.py:229
  60.9 1.4 %collective-permute-done.22.refs_0_ = bf16[2,192,384]{2,1,0:T(8,128)(2,1)S(1)} collective-permute-done((bf16[2,192,384]{2,1,0:T(8,128)(2,1)S(1)}, bf16[2,192,384]{2,1,0:T(8,128)(2,1)S(1)}, u32[]{:S(2)}, u32[]{:S(2)}) %collective-permute-start.22) | collective-permute-done | bytes 294944 | tf_op jit(solution)/shard_map/ppermute | solution.py:407
  62.4 3.2 %collective-permute-done.23.refs_1_ = bf16[2,192,384]{2,1,0:T(8,128)(2,1)S(1)} collective-permute-done((bf16[2,192,384]{2,1,0:T(8,128)(2,1)S(1)}, bf16[2,192,384]{2,1,0:T(8,128)(2,1)S(1)}, u32[]{:S(2)}, u32[]{:S(2)}) %collective-permute-start.23) | collective-permute-done | bytes 294944 | tf_op jit(solution)/shard_map/ppermute | solution.py:407
  66.3 1.2 %amplitudes.2 = (f32[384,768]{1,0:T(8,128)S(1)}, bf16[2,768,384]{2,1,0:T(8,128)(2,1)S(1)}, bf16[2,384,384]{2,1,0:T(8,128)(2,1)S(1)}) custom-call(bf16[384,1536]{1,0:T(8,128)(2,1)S(1)} %prep.1.own_t, bf16[3,2,192,384]{3,2,1,0:T(8,128)(2,1)S(1)} %join.5.early, bf16[3,2,192,384]{3,2,1,0:T(8,128)(2,1)S(1)} %collective-permute-done.15.other), custom_call_target="tpu_custom_call" | custom-call | flops 452984832 | bytes 3145728 | tf_op jit(solution)/shard_map/amplitudes/pallas_call | solution.py:303
  67.6 1.2 %amplitudes.3 = (f32[384,768]{1,0:T(8,128)S(1)}, bf16[2,768,384]{2,1,0:T(8,128)(2,1)S(1)}, bf16[2,384,384]{2,1,0:T(8,128)(2,1)S(1)}) custom-call(bf16[384,1536]{1,0:T(8,128)(2,1)S(1)} %prep.1.own_t, bf16[3,2,192,384]{3,2,1,0:T(8,128)(2,1)S(1)} %join.6.early, bf16[3,2,192,384]{3,2,1,0:T(8,128)(2,1)S(1)} %collective-permute-done.21.other), custom_call_target="tpu_custom_call" | custom-call | flops 452984832 | bytes 3145728 | tf_op jit(solution)/shard_map/amplitudes/pallas_call | solution.py:303
  68.9 4.9 %pair_terms.1 = (bf16[384,1536]{1,0:T(8,128)(2,1)}, f32[1,1]{1,0:T(1,128)}) custom-call(s32[32]{0:T(128)S(1)} %copy-done, s32[1,4]{1,0:T(1,128)S(1)} %copy-done.2, s32[1,384]{1,0:T(1,128)S(1)} %reshape.16.row_ref, s32[384,1]{1,0:T(8,128)S(1)} %reshape.19.col_ref, bf16[384,1536]{1,0:T(8,128)(2,1)S(1)} %prep.1.own_t, ...), custom_call_target="tpu_custom_call" | custom-call | tf_op jit(solution)/shard_map/pair_terms/pallas_call | solution.py:386
  (33 shorter events, 4.8 us)
Async XLA Ops:
  0.6 15.8 %copy-start.2 = (s32[1,4]{1,0:T(1,128)S(1)}, s32[1,4]{1,0:T(1,128)}, u32[]{:S(2)}) copy-start(s32[1,4]{1,0:T(1,128)} %plan_ref.3) | copy-start | bytes 52
  5.5 7.8 %collective-permute-start.7 = (bf16[2,48,384]{2,1,0:T(8,128)(2,1)S(1)}, bf16[2,48,384]{2,1,0:T(8,128)(2,1)S(1)}, u32[]{:S(2)}, u32[]{:S(2)}) collective-permute-start(bf16[2,48,384]{2,1,0:T(8,128)(2,1)S(1)} %get-tuple-element.73), channel_id=1, source_target_pairs={{0,1},{1,2},{2,3},{3,0},{4,5},{5,6},{6,7},{7,4},{8,9},{9,10},{10,1... | collective-permute-start | bytes 221192 | tf_op jit(solution)/shard_map/ppermute | solution.py:411
  8.6 7.6 %collective-permute-start.8 = (bf16[2,48,384]{2,1,0:T(8,128)(2,1)S(1)}, bf16[2,48,384]{2,1,0:T(8,128)(2,1)S(1)}, u32[]{:S(2)}, u32[]{:S(2)}) collective-permute-start(bf16[2,48,384]{2,1,0:T(8,128)(2,1)S(1)} %get-tuple-element.74), channel_id=1, source_target_pairs={{0,2},{1,3},{2,0},{3,1},{4,6},{5,7},{6,4},{7,5},{8,10},{9,11},{10,... | collective-permute-start | bytes 221192 | tf_op jit(solution)/shard_map/ppermute | solution.py:411
  11.2 5.2 %collective-permute-start.9 = (bf16[2,48,384]{2,1,0:T(8,128)(2,1)S(1)}, bf16[2,48,384]{2,1,0:T(8,128)(2,1)S(1)}, u32[]{:S(2)}, u32[]{:S(2)}) collective-permute-start(bf16[2,48,384]{2,1,0:T(8,128)(2,1)S(1)} %get-tuple-element.75), channel_id=1, source_target_pairs={{0,3},{1,0},{2,1},{3,2},{4,7},{5,4},{6,5},{7,6},{8,11},{9,8},{10,9... | collective-permute-start | bytes 221192 | tf_op jit(solution)/shard_map/ppermute | solution.py:411
  17.3 6.7 %collective-permute-start.10 = (bf16[2,48,384]{2,1,0:T(8,128)(2,1)S(1)}, bf16[2,48,384]{2,1,0:T(8,128)(2,1)S(1)}, u32[]{:S(2)}, u32[]{:S(2)}) collective-permute-start(bf16[2,48,384]{2,1,0:T(8,128)(2,1)S(1)} %get-tuple-element.80.refs_0_), channel_id=1, source_target_pairs={{0,1},{1,2},{2,3},{3,0},{4,5},{5,6},{6,7},{7,4},{8,9},{9,10},{10,1... | collective-permute-start | bytes 221192 | tf_op jit(solution)/shard_map/ppermute | solution.py:411
  19.2 7.1 %collective-permute-start.11 = (bf16[2,48,384]{2,1,0:T(8,128)(2,1)S(1)}, bf16[2,48,384]{2,1,0:T(8,128)(2,1)S(1)}, u32[]{:S(2)}, u32[]{:S(2)}) collective-permute-start(bf16[2,48,384]{2,1,0:T(8,128)(2,1)S(1)} %get-tuple-element.80.refs_0_), channel_id=1, source_target_pairs={{0,2},{1,3},{2,0},{3,1},{4,6},{5,7},{6,4},{7,5},{8,10},{9,11},{10,... | collective-permute-start | bytes 221192 | tf_op jit(solution)/shard_map/ppermute | solution.py:411
  21.1 5.4 %collective-permute-start.12 = (bf16[2,48,384]{2,1,0:T(8,128)(2,1)S(1)}, bf16[2,48,384]{2,1,0:T(8,128)(2,1)S(1)}, u32[]{:S(2)}, u32[]{:S(2)}) collective-permute-start(bf16[2,48,384]{2,1,0:T(8,128)(2,1)S(1)} %get-tuple-element.80.refs_0_), channel_id=1, source_target_pairs={{0,3},{1,0},{2,1},{3,2},{4,7},{5,4},{6,5},{7,6},{8,11},{9,8},{10,9... | collective-permute-start | bytes 221192 | tf_op jit(solution)/shard_map/ppermute | solution.py:411
  26.5 13.6 %collective-permute-start.13 = (bf16[2,192,384]{2,1,0:T(8,128)(2,1)S(1)}, bf16[2,192,384]{2,1,0:T(8,128)(2,1)S(1)}, u32[]{:S(2)}, u32[]{:S(2)}) collective-permute-start(bf16[2,192,384]{2,1,0:T(8,128)(2,1)S(1)} %pack.2.refs_0_), channel_id=1, source_target_pairs={{0,8},{4,20},{8,0},{12,28},{16,24},{20,4},{24,16},{28,12},{1,9},{5... | collective-permute-start | bytes 884744 | tf_op jit(solution)/shard_map/ppermute | solution.py:407
  28.0 6.4 %collective-permute-start.16 = (bf16[2,48,384]{2,1,0:T(8,128)(2,1)S(1)}, bf16[2,48,384]{2,1,0:T(8,128)(2,1)S(1)}, u32[]{:S(2)}, u32[]{:S(2)}) collective-permute-start(bf16[2,48,384]{2,1,0:T(8,128)(2,1)S(1)} %get-tuple-element.84.refs_0_), channel_id=1, source_target_pairs={{0,1},{1,2},{2,3},{3,0},{4,5},{5,6},{6,7},{7,4},{8,9},{9,10},{10,1... | collective-permute-start | bytes 221192 | tf_op jit(solution)/shard_map/ppermute | solution.py:411
  29.7 6.9 %collective-permute-start.17 = (bf16[2,48,384]{2,1,0:T(8,128)(2,1)S(1)}, bf16[2,48,384]{2,1,0:T(8,128)(2,1)S(1)}, u32[]{:S(2)}, u32[]{:S(2)}) collective-permute-start(bf16[2,48,384]{2,1,0:T(8,128)(2,1)S(1)} %get-tuple-element.84.refs_0_), channel_id=1, source_target_pairs={{0,2},{1,3},{2,0},{3,1},{4,6},{5,7},{6,4},{7,5},{8,10},{9,11},{10,... | collective-permute-start | bytes 221192 | tf_op jit(solution)/shard_map/ppermute | solution.py:411
  31.1 5.5 %collective-permute-start.18 = (bf16[2,48,384]{2,1,0:T(8,128)(2,1)S(1)}, bf16[2,48,384]{2,1,0:T(8,128)(2,1)S(1)}, u32[]{:S(2)}, u32[]{:S(2)}) collective-permute-start(bf16[2,48,384]{2,1,0:T(8,128)(2,1)S(1)} %get-tuple-element.84.refs_0_), channel_id=1, source_target_pairs={{0,3},{1,0},{2,1},{3,2},{4,7},{5,4},{6,5},{7,6},{8,11},{9,8},{10,9... | collective-permute-start | bytes 221192 | tf_op jit(solution)/shard_map/ppermute | solution.py:411
  32.1 8.8 %collective-permute-start.14 = (bf16[2,192,384]{2,1,0:T(8,128)(2,1)S(1)}, bf16[2,192,384]{2,1,0:T(8,128)(2,1)S(1)}, u32[]{:S(2)}, u32[]{:S(2)}) collective-permute-start(bf16[2,192,384]{2,1,0:T(8,128)(2,1)S(1)} %pack.2.refs_0_), channel_id=1, source_target_pairs={{0,16},{4,12},{8,24},{12,4},{16,0},{20,28},{24,8},{28,20},{1,17},{... | collective-permute-start | bytes 884744 | tf_op jit(solution)/shard_map/ppermute | solution.py:407
  36.7 9.9 %collective-permute-start.19 = (bf16[2,192,384]{2,1,0:T(8,128)(2,1)S(1)}, bf16[2,192,384]{2,1,0:T(8,128)(2,1)S(1)}, u32[]{:S(2)}, u32[]{:S(2)}) collective-permute-start(bf16[2,192,384]{2,1,0:T(8,128)(2,1)S(1)} %pack.3.refs_0_), channel_id=1, source_target_pairs={{0,8},{4,20},{8,0},{12,28},{16,24},{20,4},{24,16},{28,12},{1,9},{5... | collective-permute-start | bytes 884744 | tf_op jit(solution)/shard_map/ppermute | solution.py:407
  38.1 9.9 %collective-permute-start.20 = (bf16[2,192,384]{2,1,0:T(8,128)(2,1)S(1)}, bf16[2,192,384]{2,1,0:T(8,128)(2,1)S(1)}, u32[]{:S(2)}, u32[]{:S(2)}) collective-permute-start(bf16[2,192,384]{2,1,0:T(8,128)(2,1)S(1)} %pack.3.refs_0_), channel_id=1, source_target_pairs={{0,16},{4,12},{8,24},{12,4},{16,0},{20,28},{24,8},{28,20},{1,17},{... | collective-permute-start | bytes 884744 | tf_op jit(solution)/shard_map/ppermute | solution.py:407
  38.9 14.1 %collective-permute-start.3 = (bf16[2,192,384]{2,1,0:T(8,128)(2,1)S(1)}, bf16[2,192,384]{2,1,0:T(8,128)(2,1)S(1)}, u32[]{:S(2)}, u32[]{:S(2)}) collective-permute-start(bf16[2,192,384]{2,1,0:T(8,128)(2,1)S(1)} %get-tuple-element.68), channel_id=1, source_target_pairs={{0,8},{4,12},{8,0},{12,4},{16,24},{20,28},{24,16},{28,20},{1,9},{5... | collective-permute-start | bytes 884744 | tf_op jit(solution)/shard_map/ppermute | solution.py:437
  40.1 14.2 %collective-permute-start.4 = (bf16[2,192,384]{2,1,0:T(8,128)(2,1)S(1)}, bf16[2,192,384]{2,1,0:T(8,128)(2,1)S(1)}, u32[]{:S(2)}, u32[]{:S(2)}) collective-permute-start(bf16[2,192,384]{2,1,0:T(8,128)(2,1)S(1)} %get-tuple-element.69), channel_id=1, source_target_pairs={{0,16},{4,20},{8,24},{12,28},{16,0},{20,4},{24,8},{28,12},{1,17},{... | collective-permute-start | bytes 884744 | tf_op jit(solution)/shard_map/ppermute | solution.py:437
  40.8 19.2 %collective-permute-start.5 = (bf16[2,192,384]{2,1,0:T(8,128)(2,1)S(1)}, bf16[2,192,384]{2,1,0:T(8,128)(2,1)S(1)}, u32[]{:S(2)}, u32[]{:S(2)}) collective-permute-start(bf16[2,192,384]{2,1,0:T(8,128)(2,1)S(1)} %get-tuple-element.70), channel_id=1, source_target_pairs={{0,24},{4,28},{8,16},{12,20},{16,8},{20,12},{24,0},{28,4},{1,25},{... | collective-permute-start | bytes 884744 | tf_op jit(solution)/shard_map/ppermute | solution.py:437
  46.7 19.6 %collective-permute-start.15 = (bf16[3,2,192,384]{3,2,1,0:T(8,128)(2,1)S(1)}, bf16[3,2,192,384]{3,2,1,0:T(8,128)(2,1)S(1)}, u32[]{:S(2)}, u32[]{:S(2)}) collective-permute-start(bf16[3,2,192,384]{3,2,1,0:T(8,128)(2,1)S(1)} %join.5.early), channel_id=1, source_target_pairs={{0,4},{4,0},{8,12},{12,8},{16,20},{20,16},{24,28},{28,24},{1,5},{5... | collective-permute-start | bytes 2654216 | tf_op jit(solution)/shard_map/ppermute | solution.py:403
  48.2 19.3 %collective-permute-start.21 = (bf16[3,2,192,384]{3,2,1,0:T(8,128)(2,1)S(1)}, bf16[3,2,192,384]{3,2,1,0:T(8,128)(2,1)S(1)}, u32[]{:S(2)}, u32[]{:S(2)}) collective-permute-start(bf16[3,2,192,384]{3,2,1,0:T(8,128)(2,1)S(1)} %join.6.early), channel_id=1, source_target_pairs={{0,4},{4,0},{8,12},{12,8},{16,20},{20,16},{24,28},{28,24},{1,5},{5... | collective-permute-start | bytes 2654216 | tf_op jit(solution)/shard_map/ppermute | solution.py:403
  53.0 9.4 %collective-permute-start.22 = (bf16[2,192,384]{2,1,0:T(8,128)(2,1)S(1)}, bf16[2,192,384]{2,1,0:T(8,128)(2,1)S(1)}, u32[]{:S(2)}, u32[]{:S(2)}) collective-permute-start(bf16[2,192,384]{2,1,0:T(8,128)(2,1)S(1)} %collective-permute-done.13.refs_1_), channel_id=1, source_target_pairs={{0,16},{4,12},{8,24},{12,4},{16,0},{20,28},{24,8},{28,20},{1,17},{... | collective-permute-start | bytes 884744 | tf_op jit(solution)/shard_map/ppermute | solution.py:407
  54.3 11.2 %collective-permute-start.23 = (bf16[2,192,384]{2,1,0:T(8,128)(2,1)S(1)}, bf16[2,192,384]{2,1,0:T(8,128)(2,1)S(1)}, u32[]{:S(2)}, u32[]{:S(2)}) collective-permute-start(bf16[2,192,384]{2,1,0:T(8,128)(2,1)S(1)} %collective-permute-done.19.refs_1_), channel_id=1, source_target_pairs={{0,16},{4,12},{8,24},{12,4},{16,0},{20,28},{24,8},{28,20},{1,17},{... | collective-permute-start | bytes 884744 | tf_op jit(solution)/shard_map/ppermute | solution.py:407
  60.1 5.7 %copy-start.1 = (s32[384]{0:T(512)S(1)}, s32[384]{0:T(512)}, u32[]{:S(2)}) copy-start(s32[384]{0:T(512)} %param.10) | copy-start | bytes 4612
  60.9 5.0 %collective-permute-start.6 = (bf16[4,192,384]{2,1,0:T(8,128)(2,1)S(1)}, bf16[4,192,384]{2,1,0:T(8,128)(2,1)S(1)}, u32[]{:S(2)}, u32[]{:S(2)}) collective-permute-start(bf16[4,192,384]{2,1,0:T(8,128)(2,1)S(1)} %join.4), channel_id=1, source_target_pairs={{0,4},{4,0},{8,12},{12,8},{16,20},{20,16},{24,28},{28,24},{1,5},{5... | collective-permute-start | bytes 1769480 | tf_op jit(solution)/shard_map/ppermute | solution.py:403
  65.7 3.2 %collective-permute-start.24 = (bf16[2,2,192,384]{3,2,1,0:T(8,128)(2,1)S(1)}, bf16[2,2,192,384]{3,2,1,0:T(8,128)(2,1)S(1)}, u32[]{:S(2)}, u32[]{:S(2)}) collective-permute-start(bf16[2,2,192,384]{3,2,1,0:T(8,128)(2,1)S(1)} %join.7.rest_6_), channel_id=1, source_target_pairs={{0,4},{4,0},{8,12},{12,8},{16,20},{20,16},{24,28},{28,24},{1,5},{5... | collective-permute-start | bytes 1769480 | tf_op jit(solution)/shard_map/ppermute | solution.py:403
  67.6 1.3 %copy-start = (s32[32]{0:T(128)S(1)}, s32[32]{0:T(128)}, u32[]{:S(2)}) copy-start(s32[32]{0:T(128)} %occ_ref.1) | copy-start | bytes 388

commit v4 on v3

--- a/solution.py
+++ b/solution.py
@@ -192,11 +192,10 @@
 
 def pack_kernel(*refs):
     parts, out = refs[:-1], refs[-1]
-    n_half = len(parts)
     per, sub, _ = parts[0].shape
     z = lax.axis_index("half")
     for d, part in enumerate(parts):
-        at = pl.multiple_of(lax.rem(z - d + n_half, n_half) * sub, sub)
+        at = pl.multiple_of(lax.bitwise_xor(z, d) * sub, sub)
         for s in range(per):
             out[s, pl.ds(at, sub)] = part[s]
 
@@ -411,6 +410,10 @@
     return lax.ppermute(x, "half", [(h, (h + d) % n) for h in range(n)])
 
 
+def across(x, bits, n):
+    return lax.ppermute(x, "half", [(h, h ^ bits) for h in range(n)])
+
+
 GROUPS = 2
 
 
@@ -449,9 +452,9 @@
     mine = lax.switch(crowd[0], [roomy, crowded], got, spill)
     ins, late = [], []
     for g in range(GROUPS):
-        parts = [mine[g]]
-        for d in range(1, n_half):
-            parts.append(shift(mine[g], d, n_half))
+        far = across(mine[g], 2, n_half)
+        beside = across(mine[g], 1, n_half)
+        parts = [mine[g], beside, far, across(far, 1, n_half)]
         z0 = pack(parts)
         r1 = plane(z0, n_aux, 0)
         r2 = plane(z0, n_aux, 1)

time: 73.9 us -> 73.6 us (level)
  waiting for transfers between devices: 30.7 us -> 27.5 us
  starting transfers between devices: 26.5 us -> 29.5 us
    ppermute x0 -> x6, waiting for transfers between devices: none -> 9.99 us  [across(): return lax.ppermute(x, 'half', [(h, h ^ bits) for h in range(n)])]
    ppermute x0 -> x6, starting transfers between devices: none -> 9.42 us  [across(): return lax.ppermute(x, 'half', [(h, h ^ bits) for h in range(n)])]
    ppermute x9 -> x3, starting transfers between devices: 15.6 us -> 7.04 us  [shift(): return lax.ppermute(x, 'half', [(h, (h + d) % n) for h in range(n)])]
    ppermute x9 -> x3, waiting for transfers between devices: 11 us -> 3.2 us  [shift(): return lax.ppermute(x, 'half', [(h, (h + d) % n) for h in range(n)])]
    ppermute x3, waiting for transfers between devices: 9.73 us -> 4.35 us  [stages(): lax.ppermute(near[r], 'aux', [(a, a ^ 2 * r) for a in range(n_aux)])]
    ppermute x6, starting transfers between devices: 7.16 us -> 8.9 us  [plane(): lax.ppermute(x, 'aux', [(a, a ^ (Y if a & CORE ^ flip else X)) for a in r...]
  transfers between devices with their start and end apart: 22 -> 22, of which waited for: 14 -> 15; matrix products, arithmetic and copies ran while one was open for 0% -> 0% of each run, Pallas kernels for 6% -> 6%
where the time goes in v4:
time: 73.6 us; the launch traced here: 73.5 us
  starting transfers between devices  29.5 us (40%)
  waiting for transfers between devices  27.5 us (37%)
  Pallas kernels  14.9 us (20%)
  between operations  1.48 us (2%)
    ppermute x6, waiting for transfers between devices, across(): return lax.ppermute(x, 'half', [(h, h ^ bits) for h in range(n)])  9.99 us
    ppermute x6, waiting for transfers between devices, plane(): lax.ppermute(x, 'aux', [(a, a ^ (Y if a & CORE ^ flip else X)) for a in r...  9.91 us
    ppermute x6, starting transfers between devices, across(): return lax.ppermute(x, 'half', [(h, h ^ bits) for h in range(n)])  9.42 us
    ppermute x6, starting transfers between devices, plane(): lax.ppermute(x, 'aux', [(a, a ^ (Y if a & CORE ^ flip else X)) for a in r...  8.9 us
    ppermute x3, starting transfers between devices, shift(): return lax.ppermute(x, 'half', [(h, (h + d) % n) for h in range(n)])  7.04 us
    pallas_call x1, Pallas kernels, pair_terms(): pl.pallas_call(functools.partial(pair_kernel, n_orb=n_orb, groups=groups)...  4.85 us
    pallas_call x1, Pallas kernels, transform(): pl.pallas_call(functools.partial(transform_kernel, n_half=n_half, order=o...  4.83 us
    ppermute x3, waiting for transfers between devices, stages(): lax.ppermute(near[r], 'aux', [(a, a ^ 2 * r) for a in range(n_aux)])  4.35 us
  transfers between devices with their start and end apart: 22, of which 15 were waited for; matrix products, arithmetic and copies ran while one was open for 0% of the time, Pallas kernels for 6%

profile of v4, /device:TPU:0, one launch (start us, length us, event | category | flops | bytes accessed | tf_op | source)
XLA Modules:
  0.0 73.5 jit_solution(11768400384860189842)
XLA Ops:
  0.6 4.8 %transform.1 = (s32[1]{0:T(128)}, bf16[2,192,384]{2,1,0:T(8,128)(2,1)S(1)}, bf16[2,192,384]{2,1,0:T(8,128)(2,1)S(1)}, bf16[2,192,384]{2,1,0:T(8,128)(2,1)S(1)}, ...) custom-call(s32[1,4]{1,0:T(1,128)} %plan_ref.3, ...), custom_call_target="tpu_custom_call" | custom-call | tf_op jit(solution)/shard_map/transform/pallas_call | solution.py:125
  5.5 3.1 %collective-permute-start.7 = (bf16[2,48,384]{2,1,0:T(8,128)(2,1)S(1)}, bf16[2,48,384]{2,1,0:T(8,128)(2,1)S(1)}, u32[]{:S(2)}, u32[]{:S(2)}) collective-permute-start(bf16[2,48,384]{2,1,0:T(8,128)(2,1)S(1)} %get-tuple-element.73), channel_id=1, source_target_pairs={{0,1},{1,2},{2,3},{3,0},{4,5},{5,6},{6,7},{7,4},{8,9},{9,10},{10,1... | collective-permute-start | bytes 221192 | tf_op jit(solution)/shard_map/ppermute | solution.py:410
  8.6 2.6 %collective-permute-start.8 = (bf16[2,48,384]{2,1,0:T(8,128)(2,1)S(1)}, bf16[2,48,384]{2,1,0:T(8,128)(2,1)S(1)}, u32[]{:S(2)}, u32[]{:S(2)}) collective-permute-start(bf16[2,48,384]{2,1,0:T(8,128)(2,1)S(1)} %get-tuple-element.74), channel_id=1, source_target_pairs={{0,2},{1,3},{2,0},{3,1},{4,6},{5,7},{6,4},{7,5},{8,10},{9,11},{10,... | collective-permute-start | bytes 221192 | tf_op jit(solution)/shard_map/ppermute | solution.py:410
  11.2 1.3 %collective-permute-start.9 = (bf16[2,48,384]{2,1,0:T(8,128)(2,1)S(1)}, bf16[2,48,384]{2,1,0:T(8,128)(2,1)S(1)}, u32[]{:S(2)}, u32[]{:S(2)}) collective-permute-start(bf16[2,48,384]{2,1,0:T(8,128)(2,1)S(1)} %get-tuple-element.75), channel_id=1, source_target_pairs={{0,3},{1,0},{2,1},{3,2},{4,7},{5,4},{6,5},{7,6},{8,11},{9,8},{10,9... | collective-permute-start | bytes 221192 | tf_op jit(solution)/shard_map/ppermute | solution.py:410
  13.3 2.9 %collective-permute-done.8 = bf16[2,48,384]{2,1,0:T(8,128)(2,1)S(1)} collective-permute-done((bf16[2,48,384]{2,1,0:T(8,128)(2,1)S(1)}, bf16[2,48,384]{2,1,0:T(8,128)(2,1)S(1)}, u32[]{:S(2)}, u32[]{:S(2)}) %collective-permute-start.8) | collective-permute-done | bytes 73760 | tf_op jit(solution)/shard_map/ppermute | solution.py:410
  17.3 1.6 %collective-permute-start.11 = (bf16[2,48,384]{2,1,0:T(8,128)(2,1)S(1)}, bf16[2,48,384]{2,1,0:T(8,128)(2,1)S(1)}, u32[]{:S(2)}, u32[]{:S(2)}) collective-permute-start(bf16[2,48,384]{2,1,0:T(8,128)(2,1)S(1)} %get-tuple-element.80.refs_0_), channel_id=1, source_target_pairs={{0,2},{1,3},{2,0},{3,1},{4,6},{5,7},{6,4},{7,5},{8,10},{9,11},{10,... | collective-permute-start | bytes 221192 | tf_op jit(solution)/shard_map/ppermute | solution.py:414
  18.9 2.2 %collective-permute-start.10 = (bf16[2,48,384]{2,1,0:T(8,128)(2,1)S(1)}, bf16[2,48,384]{2,1,0:T(8,128)(2,1)S(1)}, u32[]{:S(2)}, u32[]{:S(2)}) collective-permute-start(bf16[2,48,384]{2,1,0:T(8,128)(2,1)S(1)} %get-tuple-element.80.refs_0_), channel_id=1, source_target_pairs={{0,1},{1,0},{2,3},{3,2},{4,5},{5,4},{6,7},{7,6},{8,9},{9,8},{10,11... | collective-permute-start | bytes 221192 | tf_op jit(solution)/shard_map/ppermute | solution.py:414
  21.1 2.6 %collective-permute-done.11.refs_2_ = bf16[2,48,384]{2,1,0:T(8,128)(2,1)S(1)} collective-permute-done((bf16[2,48,384]{2,1,0:T(8,128)(2,1)S(1)}, bf16[2,48,384]{2,1,0:T(8,128)(2,1)S(1)}, u32[]{:S(2)}, u32[]{:S(2)}) %collective-permute-start.11) | collective-permute-done | bytes 73760 | tf_op jit(solution)/shard_map/ppermute | solution.py:414
  23.7 1.3 %collective-permute-start.12 = (bf16[2,48,384]{2,1,0:T(8,128)(2,1)S(1)}, bf16[2,48,384]{2,1,0:T(8,128)(2,1)S(1)}, u32[]{:S(2)}, u32[]{:S(2)}) collective-permute-start(bf16[2,48,384]{2,1,0:T(8,128)(2,1)S(1)} %collective-permute-done.11.refs_2_), channel_id=1, source_target_pairs={{0,1},{1,0},{2,3},{3,2},{4,5},{5,4},{6,7},{7,6},{8,9},{9,8},{10,11... | collective-permute-start | bytes 221192 | tf_op jit(solution)/shard_map/ppermute | solution.py:414
  25.1 3.0 %collective-permute-done.12.refs_3_ = bf16[2,48,384]{2,1,0:T(8,128)(2,1)S(1)} collective-permute-done((bf16[2,48,384]{2,1,0:T(8,128)(2,1)S(1)}, bf16[2,48,384]{2,1,0:T(8,128)(2,1)S(1)}, u32[]{:S(2)}, u32[]{:S(2)}) %collective-permute-start.12) | collective-permute-done | bytes 73760 | tf_op jit(solution)/shard_map/ppermute | solution.py:414
  28.1 1.6 %collective-permute-start.13 = (bf16[2,192,384]{2,1,0:T(8,128)(2,1)S(1)}, bf16[2,192,384]{2,1,0:T(8,128)(2,1)S(1)}, u32[]{:S(2)}, u32[]{:S(2)}) collective-permute-start(bf16[2,192,384]{2,1,0:T(8,128)(2,1)S(1)} %pack.2.refs_0_), channel_id=1, source_target_pairs={{0,8},{4,20},{8,0},{12,28},{16,24},{20,4},{24,16},{28,12},{1,9},{5... | collective-permute-start | bytes 884744 | tf_op jit(solution)/shard_map/ppermute | solution.py:406
  29.7 1.0 %collective-permute-start.17 = (bf16[2,48,384]{2,1,0:T(8,128)(2,1)S(1)}, bf16[2,48,384]{2,1,0:T(8,128)(2,1)S(1)}, u32[]{:S(2)}, u32[]{:S(2)}) collective-permute-start(bf16[2,48,384]{2,1,0:T(8,128)(2,1)S(1)} %get-tuple-element.84.refs_0_), channel_id=1, source_target_pairs={{0,2},{1,3},{2,0},{3,1},{4,6},{5,7},{6,4},{7,5},{8,10},{9,11},{10,... | collective-permute-start | bytes 221192 | tf_op jit(solution)/shard_map/ppermute | solution.py:414
  30.7 2.0 %collective-permute-start.16 = (bf16[2,48,384]{2,1,0:T(8,128)(2,1)S(1)}, bf16[2,48,384]{2,1,0:T(8,128)(2,1)S(1)}, u32[]{:S(2)}, u32[]{:S(2)}) collective-permute-start(bf16[2,48,384]{2,1,0:T(8,128)(2,1)S(1)} %get-tuple-element.84.refs_0_), channel_id=1, source_target_pairs={{0,1},{1,0},{2,3},{3,2},{4,5},{5,4},{6,7},{7,6},{8,9},{9,8},{10,11... | collective-permute-start | bytes 221192 | tf_op jit(solution)/shard_map/ppermute | solution.py:414
  32.7 2.5 %collective-permute-done.17.refs_2_ = bf16[2,48,384]{2,1,0:T(8,128)(2,1)S(1)} collective-permute-done((bf16[2,48,384]{2,1,0:T(8,128)(2,1)S(1)}, bf16[2,48,384]{2,1,0:T(8,128)(2,1)S(1)}, u32[]{:S(2)}, u32[]{:S(2)}) %collective-permute-start.17) | collective-permute-done | bytes 73760 | tf_op jit(solution)/shard_map/ppermute | solution.py:414
  35.2 1.3 %collective-permute-start.18 = (bf16[2,48,384]{2,1,0:T(8,128)(2,1)S(1)}, bf16[2,48,384]{2,1,0:T(8,128)(2,1)S(1)}, u32[]{:S(2)}, u32[]{:S(2)}) collective-permute-start(bf16[2,48,384]{2,1,0:T(8,128)(2,1)S(1)} %collective-permute-done.17.refs_2_), channel_id=1, source_target_pairs={{0,1},{1,0},{2,3},{3,2},{4,5},{5,4},{6,7},{7,6},{8,9},{9,8},{10,11... | collective-permute-start | bytes 221192 | tf_op jit(solution)/shard_map/ppermute | solution.py:414
  36.5 1.2 %collective-permute-start.14 = (bf16[2,192,384]{2,1,0:T(8,128)(2,1)S(1)}, bf16[2,192,384]{2,1,0:T(8,128)(2,1)S(1)}, u32[]{:S(2)}, u32[]{:S(2)}) collective-permute-start(bf16[2,192,384]{2,1,0:T(8,128)(2,1)S(1)} %pack.2.refs_0_), channel_id=1, source_target_pairs={{0,16},{4,12},{8,24},{12,4},{16,0},{20,28},{24,8},{28,20},{1,17},{... | collective-permute-start | bytes 884744 | tf_op jit(solution)/shard_map/ppermute | solution.py:406
  37.7 1.8 %collective-permute-done.18.refs_3_ = bf16[2,48,384]{2,1,0:T(8,128)(2,1)S(1)} collective-permute-done((bf16[2,48,384]{2,1,0:T(8,128)(2,1)S(1)}, bf16[2,48,384]{2,1,0:T(8,128)(2,1)S(1)}, u32[]{:S(2)}, u32[]{:S(2)}) %collective-permute-start.18) | collective-permute-done | bytes 73760 | tf_op jit(solution)/shard_map/ppermute | solution.py:414
  40.0 1.7 %collective-permute-start.20 = (bf16[2,192,384]{2,1,0:T(8,128)(2,1)S(1)}, bf16[2,192,384]{2,1,0:T(8,128)(2,1)S(1)}, u32[]{:S(2)}, u32[]{:S(2)}) collective-permute-start(bf16[2,192,384]{2,1,0:T(8,128)(2,1)S(1)} %pack.3.refs_0_), channel_id=1, source_target_pairs={{0,16},{4,12},{8,24},{12,4},{16,0},{20,28},{24,8},{28,20},{1,17},{... | collective-permute-start | bytes 884744 | tf_op jit(solution)/shard_map/ppermute | solution.py:406
  41.8 1.9 %collective-permute-start.3 = (bf16[2,192,384]{2,1,0:T(8,128)(2,1)S(1)}, bf16[2,192,384]{2,1,0:T(8,128)(2,1)S(1)}, u32[]{:S(2)}, u32[]{:S(2)}) collective-permute-start(bf16[2,192,384]{2,1,0:T(8,128)(2,1)S(1)} %get-tuple-element.68), channel_id=1, source_target_pairs={{0,8},{4,12},{8,0},{12,4},{16,24},{20,28},{24,16},{28,20},{1,9},{5... | collective-permute-start | bytes 884744 | tf_op jit(solution)/shard_map/ppermute | solution.py:440
  43.7 2.1 %collective-permute-done.14.refs_2_ = bf16[2,192,384]{2,1,0:T(8,128)(2,1)S(1)} collective-permute-done((bf16[2,192,384]{2,1,0:T(8,128)(2,1)S(1)}, bf16[2,192,384]{2,1,0:T(8,128)(2,1)S(1)}, u32[]{:S(2)}, u32[]{:S(2)}) %collective-permute-start.14) | collective-permute-done | bytes 294944 | tf_op jit(solution)/shard_map/ppermute | solution.py:406
  45.8 2.0 %collective-permute-start.5 = (bf16[2,192,384]{2,1,0:T(8,128)(2,1)S(1)}, bf16[2,192,384]{2,1,0:T(8,128)(2,1)S(1)}, u32[]{:S(2)}, u32[]{:S(2)}) collective-permute-start(bf16[2,192,384]{2,1,0:T(8,128)(2,1)S(1)} %get-tuple-element.70), channel_id=1, source_target_pairs={{0,24},{4,28},{8,16},{12,20},{16,8},{20,12},{24,0},{28,4},{1,25},{... | collective-permute-start | bytes 884744 | tf_op jit(solution)/shard_map/ppermute | solution.py:440
  48.1 1.5 %collective-permute-done.19.refs_1_ = bf16[2,192,384]{2,1,0:T(8,128)(2,1)S(1)} collective-permute-done((bf16[2,192,384]{2,1,0:T(8,128)(2,1)S(1)}, bf16[2,192,384]{2,1,0:T(8,128)(2,1)S(1)}, u32[]{:S(2)}, u32[]{:S(2)}) %collective-permute-start.19) | collective-permute-done | bytes 294944 | tf_op jit(solution)/shard_map/ppermute | solution.py:406
  49.5 2.4 %collective-permute-done.20.refs_2_ = bf16[2,192,384]{2,1,0:T(8,128)(2,1)S(1)} collective-permute-done((bf16[2,192,384]{2,1,0:T(8,128)(2,1)S(1)}, bf16[2,192,384]{2,1,0:T(8,128)(2,1)S(1)}, u32[]{:S(2)}, u32[]{:S(2)}) %collective-permute-start.20) | collective-permute-done | bytes 294944 | tf_op jit(solution)/shard_map/ppermute | solution.py:406
  52.3 1.6 %collective-permute-done.3.refs_1_ = bf16[2,192,384]{2,1,0:T(8,128)(2,1)S(1)} collective-permute-done((bf16[2,192,384]{2,1,0:T(8,128)(2,1)S(1)}, bf16[2,192,384]{2,1,0:T(8,128)(2,1)S(1)}, u32[]{:S(2)}, u32[]{:S(2)}) %collective-permute-start.3) | collective-permute-done | bytes 294944 | tf_op jit(solution)/shard_map/ppermute | solution.py:440
  53.9 1.5 %collective-permute-start.22 = (bf16[2,192,384]{2,1,0:T(8,128)(2,1)S(1)}, bf16[2,192,384]{2,1,0:T(8,128)(2,1)S(1)}, u32[]{:S(2)}, u32[]{:S(2)}) collective-permute-start(bf16[2,192,384]{2,1,0:T(8,128)(2,1)S(1)} %collective-permute-done.13.refs_1_), channel_id=1, source_target_pairs={{0,16},{4,12},{8,24},{12,4},{16,0},{20,28},{24,8},{28,20},{1,17},{... | collective-permute-start | bytes 884744 | tf_op jit(solution)/shard_map/ppermute | solution.py:406
  55.4 1.0 %collective-permute-done.4.refs_2_ = bf16[2,192,384]{2,1,0:T(8,128)(2,1)S(1)} collective-permute-done((bf16[2,192,384]{2,1,0:T(8,128)(2,1)S(1)}, bf16[2,192,384]{2,1,0:T(8,128)(2,1)S(1)}, u32[]{:S(2)}, u32[]{:S(2)}) %collective-permute-start.4) | collective-permute-done | bytes 294944 | tf_op jit(solution)/shard_map/ppermute | solution.py:440
  56.4 2.4 %collective-permute-start.23 = (bf16[2,192,384]{2,1,0:T(8,128)(2,1)S(1)}, bf16[2,192,384]{2,1,0:T(8,128)(2,1)S(1)}, u32[]{:S(2)}, u32[]{:S(2)}) collective-permute-start(bf16[2,192,384]{2,1,0:T(8,128)(2,1)S(1)} %collective-permute-done.19.refs_1_), channel_id=1, source_target_pairs={{0,16},{4,12},{8,24},{12,4},{16,0},{20,28},{24,8},{28,20},{1,17},{... | collective-permute-start | bytes 884744 | tf_op jit(solution)/shard_map/ppermute | solution.py:406
  58.8 1.7 %collective-permute-done.5.refs_3_ = bf16[2,192,384]{2,1,0:T(8,128)(2,1)S(1)} collective-permute-done((bf16[2,192,384]{2,1,0:T(8,128)(2,1)S(1)}, bf16[2,192,384]{2,1,0:T(8,128)(2,1)S(1)}, u32[]{:S(2)}, u32[]{:S(2)}) %collective-permute-start.5) | collective-permute-done | bytes 294944 | tf_op jit(solution)/shard_map/ppermute | solution.py:440
  62.1 3.2 %collective-permute-done.23.refs_1_ = bf16[2,192,384]{2,1,0:T(8,128)(2,1)S(1)} collective-permute-done((bf16[2,192,384]{2,1,0:T(8,128)(2,1)S(1)}, bf16[2,192,384]{2,1,0:T(8,128)(2,1)S(1)}, u32[]{:S(2)}, u32[]{:S(2)}) %collective-permute-start.23) | collective-permute-done | bytes 294944 | tf_op jit(solution)/shard_map/ppermute | solution.py:406
  66.1 1.2 %amplitudes.2 = (f32[384,768]{1,0:T(8,128)S(1)}, bf16[2,768,384]{2,1,0:T(8,128)(2,1)S(1)}, bf16[2,384,384]{2,1,0:T(8,128)(2,1)S(1)}) custom-call(bf16[384,1536]{1,0:T(8,128)(2,1)S(1)} %prep.1.own_t, bf16[3,2,192,384]{3,2,1,0:T(8,128)(2,1)S(1)} %join.5.early, bf16[3,2,192,384]{3,2,1,0:T(8,128)(2,1)S(1)} %collective-permute-done.15.other), custom_call_target="tpu_custom_call" | custom-call | flops 452984832 | bytes 3145728 | tf_op jit(solution)/shard_map/amplitudes/pallas_call | solution.py:302
  67.4 1.2 %amplitudes.3 = (f32[384,768]{1,0:T(8,128)S(1)}, bf16[2,768,384]{2,1,0:T(8,128)(2,1)S(1)}, bf16[2,384,384]{2,1,0:T(8,128)(2,1)S(1)}) custom-call(bf16[384,1536]{1,0:T(8,128)(2,1)S(1)} %prep.1.own_t, bf16[3,2,192,384]{3,2,1,0:T(8,128)(2,1)S(1)} %join.6.early, bf16[3,2,192,384]{3,2,1,0:T(8,128)(2,1)S(1)} %collective-permute-done.21.other), custom_call_target="tpu_custom_call" | custom-call | flops 452984832 | bytes 3145728 | tf_op jit(solution)/shard_map/amplitudes/pallas_call | solution.py:302
  68.6 4.9 %pair_terms.1 = (bf16[384,1536]{1,0:T(8,128)(2,1)}, f32[1,1]{1,0:T(1,128)}) custom-call(s32[32]{0:T(128)S(1)} %copy-done, s32[1,4]{1,0:T(1,128)S(1)} %copy-done.2, s32[1,384]{1,0:T(1,128)S(1)} %reshape.16.row_ref, s32[384,1]{1,0:T(8,128)S(1)} %reshape.19.col_ref, bf16[384,1536]{1,0:T(8,128)(2,1)S(1)} %prep.1.own_t, ...), custom_call_target="tpu_custom_call" | custom-call | tf_op jit(solution)/shard_map/pair_terms/pallas_call | solution.py:385
  (33 shorter events, 5.5 us)
Async XLA Ops:
  0.6 15.8 %copy-start.2 = (s32[1,4]{1,0:T(1,128)S(1)}, s32[1,4]{1,0:T(1,128)}, u32[]{:S(2)}) copy-start(s32[1,4]{1,0:T(1,128)} %plan_ref.3) | copy-start | bytes 52
  5.5 7.8 %collective-permute-start.7 = (bf16[2,48,384]{2,1,0:T(8,128)(2,1)S(1)}, bf16[2,48,384]{2,1,0:T(8,128)(2,1)S(1)}, u32[]{:S(2)}, u32[]{:S(2)}) collective-permute-start(bf16[2,48,384]{2,1,0:T(8,128)(2,1)S(1)} %get-tuple-element.73), channel_id=1, source_target_pairs={{0,1},{1,2},{2,3},{3,0},{4,5},{5,6},{6,7},{7,4},{8,9},{9,10},{10,1... | collective-permute-start | bytes 221192 | tf_op jit(solution)/shard_map/ppermute | solution.py:410
  8.6 7.6 %collective-permute-start.8 = (bf16[2,48,384]{2,1,0:T(8,128)(2,1)S(1)}, bf16[2,48,384]{2,1,0:T(8,128)(2,1)S(1)}, u32[]{:S(2)}, u32[]{:S(2)}) collective-permute-start(bf16[2,48,384]{2,1,0:T(8,128)(2,1)S(1)} %get-tuple-element.74), channel_id=1, source_target_pairs={{0,2},{1,3},{2,0},{3,1},{4,6},{5,7},{6,4},{7,5},{8,10},{9,11},{10,... | collective-permute-start | bytes 221192 | tf_op jit(solution)/shard_map/ppermute | solution.py:410
  11.2 5.2 %collective-permute-start.9 = (bf16[2,48,384]{2,1,0:T(8,128)(2,1)S(1)}, bf16[2,48,384]{2,1,0:T(8,128)(2,1)S(1)}, u32[]{:S(2)}, u32[]{:S(2)}) collective-permute-start(bf16[2,48,384]{2,1,0:T(8,128)(2,1)S(1)} %get-tuple-element.75), channel_id=1, source_target_pairs={{0,3},{1,0},{2,1},{3,2},{4,7},{5,4},{6,5},{7,6},{8,11},{9,8},{10,9... | collective-permute-start | bytes 221192 | tf_op jit(solution)/shard_map/ppermute | solution.py:410
  17.3 6.4 %collective-permute-start.11 = (bf16[2,48,384]{2,1,0:T(8,128)(2,1)S(1)}, bf16[2,48,384]{2,1,0:T(8,128)(2,1)S(1)}, u32[]{:S(2)}, u32[]{:S(2)}) collective-permute-start(bf16[2,48,384]{2,1,0:T(8,128)(2,1)S(1)} %get-tuple-element.80.refs_0_), channel_id=1, source_target_pairs={{0,2},{1,3},{2,0},{3,1},{4,6},{5,7},{6,4},{7,5},{8,10},{9,11},{10,... | collective-permute-start | bytes 221192 | tf_op jit(solution)/shard_map/ppermute | solution.py:414
  18.9 6.2 %collective-permute-start.10 = (bf16[2,48,384]{2,1,0:T(8,128)(2,1)S(1)}, bf16[2,48,384]{2,1,0:T(8,128)(2,1)S(1)}, u32[]{:S(2)}, u32[]{:S(2)}) collective-permute-start(bf16[2,48,384]{2,1,0:T(8,128)(2,1)S(1)} %get-tuple-element.80.refs_0_), channel_id=1, source_target_pairs={{0,1},{1,0},{2,3},{3,2},{4,5},{5,4},{6,7},{7,6},{8,9},{9,8},{10,11... | collective-permute-start | bytes 221192 | tf_op jit(solution)/shard_map/ppermute | solution.py:414
  23.7 4.4 %collective-permute-start.12 = (bf16[2,48,384]{2,1,0:T(8,128)(2,1)S(1)}, bf16[2,48,384]{2,1,0:T(8,128)(2,1)S(1)}, u32[]{:S(2)}, u32[]{:S(2)}) collective-permute-start(bf16[2,48,384]{2,1,0:T(8,128)(2,1)S(1)} %collective-permute-done.11.refs_2_), channel_id=1, source_target_pairs={{0,1},{1,0},{2,3},{3,2},{4,5},{5,4},{6,7},{7,6},{8,9},{9,8},{10,11... | collective-permute-start | bytes 221192 | tf_op jit(solution)/shard_map/ppermute | solution.py:414
  28.1 15.6 %collective-permute-start.13 = (bf16[2,192,384]{2,1,0:T(8,128)(2,1)S(1)}, bf16[2,192,384]{2,1,0:T(8,128)(2,1)S(1)}, u32[]{:S(2)}, u32[]{:S(2)}) collective-permute-start(bf16[2,192,384]{2,1,0:T(8,128)(2,1)S(1)} %pack.2.refs_0_), channel_id=1, source_target_pairs={{0,8},{4,20},{8,0},{12,28},{16,24},{20,4},{24,16},{28,12},{1,9},{5... | collective-permute-start | bytes 884744 | tf_op jit(solution)/shard_map/ppermute | solution.py:406
  29.7 5.5 %collective-permute-start.17 = (bf16[2,48,384]{2,1,0:T(8,128)(2,1)S(1)}, bf16[2,48,384]{2,1,0:T(8,128)(2,1)S(1)}, u32[]{:S(2)}, u32[]{:S(2)}) collective-permute-start(bf16[2,48,384]{2,1,0:T(8,128)(2,1)S(1)} %get-tuple-element.84.refs_0_), channel_id=1, source_target_pairs={{0,2},{1,3},{2,0},{3,1},{4,6},{5,7},{6,4},{7,5},{8,10},{9,11},{10,... | collective-permute-start | bytes 221192 | tf_op jit(solution)/shard_map/ppermute | solution.py:414
  30.7 7.0 %collective-permute-start.16 = (bf16[2,48,384]{2,1,0:T(8,128)(2,1)S(1)}, bf16[2,48,384]{2,1,0:T(8,128)(2,1)S(1)}, u32[]{:S(2)}, u32[]{:S(2)}) collective-permute-start(bf16[2,48,384]{2,1,0:T(8,128)(2,1)S(1)} %get-tuple-element.84.refs_0_), channel_id=1, source_target_pairs={{0,1},{1,0},{2,3},{3,2},{4,5},{5,4},{6,7},{7,6},{8,9},{9,8},{10,11... | collective-permute-start | bytes 221192 | tf_op jit(solution)/shard_map/ppermute | solution.py:414
  35.2 4.4 %collective-permute-start.18 = (bf16[2,48,384]{2,1,0:T(8,128)(2,1)S(1)}, bf16[2,48,384]{2,1,0:T(8,128)(2,1)S(1)}, u32[]{:S(2)}, u32[]{:S(2)}) collective-permute-start(bf16[2,48,384]{2,1,0:T(8,128)(2,1)S(1)} %collective-permute-done.17.refs_2_), channel_id=1, source_target_pairs={{0,1},{1,0},{2,3},{3,2},{4,5},{5,4},{6,7},{7,6},{8,9},{9,8},{10,11... | collective-permute-start | bytes 221192 | tf_op jit(solution)/shard_map/ppermute | solution.py:414
  36.5 9.3 %collective-permute-start.14 = (bf16[2,192,384]{2,1,0:T(8,128)(2,1)S(1)}, bf16[2,192,384]{2,1,0:T(8,128)(2,1)S(1)}, u32[]{:S(2)}, u32[]{:S(2)}) collective-permute-start(bf16[2,192,384]{2,1,0:T(8,128)(2,1)S(1)} %pack.2.refs_0_), channel_id=1, source_target_pairs={{0,16},{4,12},{8,24},{12,4},{16,0},{20,28},{24,8},{28,20},{1,17},{... | collective-permute-start | bytes 884744 | tf_op jit(solution)/shard_map/ppermute | solution.py:406
  39.6 9.9 %collective-permute-start.19 = (bf16[2,192,384]{2,1,0:T(8,128)(2,1)S(1)}, bf16[2,192,384]{2,1,0:T(8,128)(2,1)S(1)}, u32[]{:S(2)}, u32[]{:S(2)}) collective-permute-start(bf16[2,192,384]{2,1,0:T(8,128)(2,1)S(1)} %pack.3.refs_0_), channel_id=1, source_target_pairs={{0,8},{4,20},{8,0},{12,28},{16,24},{20,4},{24,16},{28,12},{1,9},{5... | collective-permute-start | bytes 884744 | tf_op jit(solution)/shard_map/ppermute | solution.py:406
  40.0 11.9 %collective-permute-start.20 = (bf16[2,192,384]{2,1,0:T(8,128)(2,1)S(1)}, bf16[2,192,384]{2,1,0:T(8,128)(2,1)S(1)}, u32[]{:S(2)}, u32[]{:S(2)}) collective-permute-start(bf16[2,192,384]{2,1,0:T(8,128)(2,1)S(1)} %pack.3.refs_0_), channel_id=1, source_target_pairs={{0,16},{4,12},{8,24},{12,4},{16,0},{20,28},{24,8},{28,20},{1,17},{... | collective-permute-start | bytes 884744 | tf_op jit(solution)/shard_map/ppermute | solution.py:406
  41.8 12.1 %collective-permute-start.3 = (bf16[2,192,384]{2,1,0:T(8,128)(2,1)S(1)}, bf16[2,192,384]{2,1,0:T(8,128)(2,1)S(1)}, u32[]{:S(2)}, u32[]{:S(2)}) collective-permute-start(bf16[2,192,384]{2,1,0:T(8,128)(2,1)S(1)} %get-tuple-element.68), channel_id=1, source_target_pairs={{0,8},{4,12},{8,0},{12,4},{16,24},{20,28},{24,16},{28,20},{1,9},{5... | collective-permute-start | bytes 884744 | tf_op jit(solution)/shard_map/ppermute | solution.py:440
  43.7 12.7 %collective-permute-start.4 = (bf16[2,192,384]{2,1,0:T(8,128)(2,1)S(1)}, bf16[2,192,384]{2,1,0:T(8,128)(2,1)S(1)}, u32[]{:S(2)}, u32[]{:S(2)}) collective-permute-start(bf16[2,192,384]{2,1,0:T(8,128)(2,1)S(1)} %get-tuple-element.69), channel_id=1, source_target_pairs={{0,16},{4,20},{8,24},{12,28},{16,0},{20,4},{24,8},{28,12},{1,17},{... | collective-permute-start | bytes 884744 | tf_op jit(solution)/shard_map/ppermute | solution.py:440
  45.8 14.7 %collective-permute-start.5 = (bf16[2,192,384]{2,1,0:T(8,128)(2,1)S(1)}, bf16[2,192,384]{2,1,0:T(8,128)(2,1)S(1)}, u32[]{:S(2)}, u32[]{:S(2)}) collective-permute-start(bf16[2,192,384]{2,1,0:T(8,128)(2,1)S(1)} %get-tuple-element.70), channel_id=1, source_target_pairs={{0,24},{4,28},{8,16},{12,20},{16,8},{20,12},{24,0},{28,4},{1,25},{... | collective-permute-start | bytes 884744 | tf_op jit(solution)/shard_map/ppermute | solution.py:440
  49.5 16.5 %collective-permute-start.15 = (bf16[3,2,192,384]{3,2,1,0:T(8,128)(2,1)S(1)}, bf16[3,2,192,384]{3,2,1,0:T(8,128)(2,1)S(1)}, u32[]{:S(2)}, u32[]{:S(2)}) collective-permute-start(bf16[3,2,192,384]{3,2,1,0:T(8,128)(2,1)S(1)} %join.5.early), channel_id=1, source_target_pairs={{0,4},{4,0},{8,12},{12,8},{16,20},{20,16},{24,28},{28,24},{1,5},{5... | collective-permute-start | bytes 2654216 | tf_op jit(solution)/shard_map/ppermute | solution.py:402
  52.2 15.2 %collective-permute-start.21 = (bf16[3,2,192,384]{3,2,1,0:T(8,128)(2,1)S(1)}, bf16[3,2,192,384]{3,2,1,0:T(8,128)(2,1)S(1)}, u32[]{:S(2)}, u32[]{:S(2)}) collective-permute-start(bf16[3,2,192,384]{3,2,1,0:T(8,128)(2,1)S(1)} %join.6.early), channel_id=1, source_target_pairs={{0,4},{4,0},{8,12},{12,8},{16,20},{20,16},{24,28},{28,24},{1,5},{5... | collective-permute-start | bytes 2654216 | tf_op jit(solution)/shard_map/ppermute | solution.py:402
  53.9 8.3 %collective-permute-start.22 = (bf16[2,192,384]{2,1,0:T(8,128)(2,1)S(1)}, bf16[2,192,384]{2,1,0:T(8,128)(2,1)S(1)}, u32[]{:S(2)}, u32[]{:S(2)}) collective-permute-start(bf16[2,192,384]{2,1,0:T(8,128)(2,1)S(1)} %collective-permute-done.13.refs_1_), channel_id=1, source_target_pairs={{0,16},{4,12},{8,24},{12,4},{16,0},{20,28},{24,8},{28,20},{1,17},{... | collective-permute-start | bytes 884744 | tf_op jit(solution)/shard_map/ppermute | solution.py:406
  56.4 8.9 %collective-permute-start.23 = (bf16[2,192,384]{2,1,0:T(8,128)(2,1)S(1)}, bf16[2,192,384]{2,1,0:T(8,128)(2,1)S(1)}, u32[]{:S(2)}, u32[]{:S(2)}) collective-permute-start(bf16[2,192,384]{2,1,0:T(8,128)(2,1)S(1)} %collective-permute-done.19.refs_1_), channel_id=1, source_target_pairs={{0,16},{4,12},{8,24},{12,4},{16,0},{20,28},{24,8},{28,20},{1,17},{... | collective-permute-start | bytes 884744 | tf_op jit(solution)/shard_map/ppermute | solution.py:406
  60.5 5.0 %copy-start.1 = (s32[384]{0:T(512)S(1)}, s32[384]{0:T(512)}, u32[]{:S(2)}) copy-start(s32[384]{0:T(512)} %param.10) | copy-start | bytes 4612
  61.3 4.4 %collective-permute-start.6 = (bf16[4,192,384]{2,1,0:T(8,128)(2,1)S(1)}, bf16[4,192,384]{2,1,0:T(8,128)(2,1)S(1)}, u32[]{:S(2)}, u32[]{:S(2)}) collective-permute-start(bf16[4,192,384]{2,1,0:T(8,128)(2,1)S(1)} %join.4), channel_id=1, source_target_pairs={{0,4},{4,0},{8,12},{12,8},{16,20},{20,16},{24,28},{28,24},{1,5},{5... | collective-permute-start | bytes 1769480 | tf_op jit(solution)/shard_map/ppermute | solution.py:402
  65.4 3.2 %collective-permute-start.24 = (bf16[2,2,192,384]{3,2,1,0:T(8,128)(2,1)S(1)}, bf16[2,2,192,384]{3,2,1,0:T(8,128)(2,1)S(1)}, u32[]{:S(2)}, u32[]{:S(2)}) collective-permute-start(bf16[2,2,192,384]{3,2,1,0:T(8,128)(2,1)S(1)} %join.7.rest_6_), channel_id=1, source_target_pairs={{0,4},{4,0},{8,12},{12,8},{16,20},{20,16},{24,28},{28,24},{1,5},{5... | collective-permute-start | bytes 1769480 | tf_op jit(solution)/shard_map/ppermute | solution.py:402
  67.3 1.3 %copy-start = (s32[32]{0:T(128)S(1)}, s32[32]{0:T(128)}, u32[]{:S(2)}) copy-start(s32[32]{0:T(128)} %occ_ref.1) | copy-start | bytes 388

commit v5 on v4

--- a/solution.py
+++ b/solution.py
@@ -61,10 +61,11 @@
 def transform_kernel(plan_ref, slab_hbm, coeff_hbm, *rest, n_half, order, chips):
     n = len(order)
     crowd_ref, rest = rest[0], rest[1:]
-    outs, lists, spill = rest[:chips], rest[chips:chips + n], rest[chips + n:chips + 2 * n]
-    slab_v, coeff_v, acc_ref, own_v, in_sem = rest[chips + 2 * n:]
+    count = plan_ref.shape[1]
+    outs, lists = rest[:chips], rest[chips:chips + n]
     cap = lists[0].shape[0]
-    count = cap + spill[0].shape[0]
+    spill = rest[chips + n:chips + n + n * (count - cap)]
+    slab_v, coeff_v, acc_ref, own_v, in_sem = rest[chips + n + n * (count - cap):]
     n_orb = 2 * chips
     aux = lax.axis_index("aux")
     tiles, block, lanes = acc_ref.shape
@@ -91,7 +92,7 @@
     most = ranks[0]
     for r in ranks[1:]:
         most = jnp.maximum(most, r)
-    crowd_ref[0] = (most >= cap).astype(jnp.int32)
+    crowd_ref[0] = jnp.maximum(most - (cap - 1), 0)
     coeff_copy.wait()
     for i in range(len(order)):
         loads[i].wait()
@@ -109,7 +110,7 @@
             if k < cap:
                 lists[i][k] = own_v[pick[k]]
             else:
-                spill[i][k - cap] = own_v[pick[k]]
+                spill[(k - cap) * n + i][0] = own_v[pick[k]]
 
 
 def transform(half_slabs, coeff, plan, n_half, order, cap):
@@ -125,13 +126,13 @@
     return pl.pallas_call(
         functools.partial(transform_kernel, n_half=n_half, order=order, chips=chips),
         in_specs=[smem, hbm, hbm],
-        out_specs=[smem] + [vmem] * (chips + 2 * n),
+        out_specs=[smem] + [vmem] * (chips + n + n * (count - cap)),
         out_shape=[
             jax.ShapeDtypeStruct((1,), jnp.int32),
         ]
         + [jax.ShapeDtypeStruct((2, local_aux, n_virt), BF16)] * chips
         + [jax.ShapeDtypeStruct((cap, rows, n_virt), BF16)] * n
-        + [jax.ShapeDtypeStruct((count - cap, rows, n_virt), BF16)] * n,
+        + [jax.ShapeDtypeStruct((1, rows, n_virt), BF16)] * (n * (count - cap)),
         scratch_shapes=[
             pltpu.VMEM((n, rows * n_orb, n_ao), BF16),
             pltpu.VMEM((n_ao, n_virt), BF16),
@@ -149,7 +150,7 @@
 
 
 def merge_kernel(plan_ref, *refs, n_orb, n_half, spilled):
-    n_in = 2 * n_half if spilled else n_half
+    n_in = (1 + spilled) * n_half
     lists, outs, sem = refs[:n_in], refs[n_in:-1], refs[-1]
     cap = lists[0].shape[0]
     per = outs[0].shape[0]
@@ -164,11 +165,11 @@
                 src = lists[d].at[jnp.minimum(rank, cap - 1)]
                 pltpu.make_async_copy(src, outs[s // per].at[s % per], sem.at[s]).start()
 
-            if spilled:
-
-                @pl.when(jnp.logical_and(far == d, rank >= cap))
+            for e in range(spilled):
+
+                @pl.when(jnp.logical_and(far == d, rank == cap + e))
                 def _():
-                    src = lists[n_half + d].at[jnp.maximum(rank - cap, 0)]
+                    src = lists[(1 + e) * n_half + d].at[0]
                     pltpu.make_async_copy(src, outs[s // per].at[s % per], sem.at[s]).start()
 
     for s in range(per * len(outs)):
@@ -180,7 +181,7 @@
     _, rows, n_virt = lists[0].shape
     shape = jax.ShapeDtypeStruct((per, rows, n_virt), BF16)
     return pl.pallas_call(
-        functools.partial(merge_kernel, n_orb=n_orb, n_half=n_half, spilled=len(lists) > n_half),
+        functools.partial(merge_kernel, n_orb=n_orb, n_half=n_half, spilled=len(lists) // n_half - 1),
         in_specs=[pl.BlockSpec(memory_space=pltpu.SMEM)] + [pl.BlockSpec(memory_space=pl.ANY)] * len(lists),
         out_specs=[pl.BlockSpec(memory_space=pltpu.VMEM)] * (count // per),
         out_shape=[shape] * (count // per),
@@ -432,7 +433,8 @@
     crowd, *lists = transform(half_slabs, vir_coeff, plan, n_half, order, cap)
     near, lists = lists[:n_aux // 2], lists[n_aux // 2:]
     lists, spill = lists[:n_half], lists[n_half:]
-    lists, spill = [lists[-1]] + lists[:-1], [spill[-1]] + spill[:-1]
+    lists = [lists[-1]] + lists[:-1]
+    spill = [spill[e + n_half - 1:e + n_half] + spill[e:e + n_half - 1] for e in range(0, len(spill), n_half)]
     got = [lists[0]]
     for d in range(1, n_half):
         got.append(shift(lists[d], d, n_half))
@@ -445,11 +447,15 @@
     def roomy(got, spill):
         return merge(plan, got, ohalf, n_half, per)
 
-    def crowded(got, spill):
-        more = [spill[0]] + [shift(spill[d], d, n_half) for d in range(1, n_half)]
-        return merge(plan, got + more, ohalf, n_half, per)
-
-    mine = lax.switch(crowd[0], [roomy, crowded], got, spill)
+    def crowded(levels):
+        def run(got, spill):
+            for level in spill[:levels]:
+                got = got + [level[0]] + [shift(level[d], d, n_half) for d in range(1, n_half)]
+            return merge(plan, got, ohalf, n_half, per)
+
+        return run
+
+    mine = lax.switch(crowd[0], [roomy] + [crowded(e + 1) for e in range(len(spill))], got, spill)
     ins, late = [], []
     for g in range(GROUPS):
         far = across(mine[g], 2, n_half)

time: 73.6 us -> 73.6 us (level)
  no operation moved by 1% of the time
where the time goes in v5:
time: 73.6 us; the launch traced here: 73.5 us
  starting transfers between devices  29.6 us (40%)
  waiting for transfers between devices  27.4 us (37%)
  Pallas kernels  14.9 us (20%)
  between operations  1.48 us (2%)
    ppermute x6, waiting for transfers between devices, across(): return lax.ppermute(x, 'half', [(h, h ^ bits) for h in range(n)])  9.97 us
    ppermute x6, waiting for transfers between devices, plane(): lax.ppermute(x, 'aux', [(a, a ^ (Y if a & CORE ^ flip else X)) for a in r...  9.95 us
    ppermute x6, starting transfers between devices, across(): return lax.ppermute(x, 'half', [(h, h ^ bits) for h in range(n)])  9.44 us
    ppermute x6, starting transfers between devices, plane(): lax.ppermute(x, 'aux', [(a, a ^ (Y if a & CORE ^ flip else X)) for a in r...  8.9 us
    ppermute x3, starting transfers between devices, shift(): return lax.ppermute(x, 'half', [(h, (h + d) % n) for h in range(n)])  7.04 us
    pallas_call x1, Pallas kernels, pair_terms(): pl.pallas_call(functools.partial(pair_kernel, n_orb=n_orb, groups=groups)...  4.85 us
    pallas_call x1, Pallas kernels, transform(): pl.pallas_call(functools.partial(transform_kernel, n_half=n_half, order=o...  4.83 us
    ppermute x3, waiting for transfers between devices, stages(): lax.ppermute(near[r], 'aux', [(a, a ^ 2 * r) for a in range(n_aux)])  4.3 us
  transfers between devices with their start and end apart: 22, of which 15 were waited for; matrix products, arithmetic and copies ran while one was open for 0% of the time, Pallas kernels for 6%

profile of v5, /device:TPU:0, one launch (start us, length us, event | category | flops | bytes accessed | tf_op | source)
XLA Modules:
  0.0 73.5 jit_solution(2920292037628647970)
XLA Ops:
  0.6 4.8 %transform.1 = (s32[1]{0:T(128)}, bf16[2,192,384]{2,1,0:T(8,128)(2,1)S(1)}, bf16[2,192,384]{2,1,0:T(8,128)(2,1)S(1)}, bf16[2,192,384]{2,1,0:T(8,128)(2,1)S(1)}, ...) custom-call(s32[1,4]{1,0:T(1,128)} %plan_ref.3, ...), custom_call_target="tpu_custom_call" | custom-call | tf_op jit(solution)/shard_map/transform/pallas_call | solution.py:126
  5.5 3.1 %collective-permute-start.13 = (bf16[2,48,384]{2,1,0:T(8,128)(2,1)S(1)}, bf16[2,48,384]{2,1,0:T(8,128)(2,1)S(1)}, u32[]{:S(2)}, u32[]{:S(2)}) collective-permute-start(bf16[2,48,384]{2,1,0:T(8,128)(2,1)S(1)} %get-tuple-element.116), channel_id=1, source_target_pairs={{0,1},{1,2},{2,3},{3,0},{4,5},{5,6},{6,7},{7,4},{8,9},{9,10},{10,1... | collective-permute-start | bytes 221192 | tf_op jit(solution)/shard_map/ppermute | solution.py:411
  8.6 2.6 %collective-permute-start.14 = (bf16[2,48,384]{2,1,0:T(8,128)(2,1)S(1)}, bf16[2,48,384]{2,1,0:T(8,128)(2,1)S(1)}, u32[]{:S(2)}, u32[]{:S(2)}) collective-permute-start(bf16[2,48,384]{2,1,0:T(8,128)(2,1)S(1)} %get-tuple-element.117), channel_id=1, source_target_pairs={{0,2},{1,3},{2,0},{3,1},{4,6},{5,7},{6,4},{7,5},{8,10},{9,11},{10,... | collective-permute-start | bytes 221192 | tf_op jit(solution)/shard_map/ppermute | solution.py:411
  11.2 1.3 %collective-permute-start.15 = (bf16[2,48,384]{2,1,0:T(8,128)(2,1)S(1)}, bf16[2,48,384]{2,1,0:T(8,128)(2,1)S(1)}, u32[]{:S(2)}, u32[]{:S(2)}) collective-permute-start(bf16[2,48,384]{2,1,0:T(8,128)(2,1)S(1)} %get-tuple-element.118), channel_id=1, source_target_pairs={{0,3},{1,0},{2,1},{3,2},{4,7},{5,4},{6,5},{7,6},{8,11},{9,8},{10,9... | collective-permute-start | bytes 221192 | tf_op jit(solution)/shard_map/ppermute | solution.py:411
  13.3 2.9 %collective-permute-done.14 = bf16[2,48,384]{2,1,0:T(8,128)(2,1)S(1)} collective-permute-done((bf16[2,48,384]{2,1,0:T(8,128)(2,1)S(1)}, bf16[2,48,384]{2,1,0:T(8,128)(2,1)S(1)}, u32[]{:S(2)}, u32[]{:S(2)}) %collective-permute-start.14) | collective-permute-done | bytes 73760 | tf_op jit(solution)/shard_map/ppermute | solution.py:411
  17.3 1.6 %collective-permute-start.17 = (bf16[2,48,384]{2,1,0:T(8,128)(2,1)S(1)}, bf16[2,48,384]{2,1,0:T(8,128)(2,1)S(1)}, u32[]{:S(2)}, u32[]{:S(2)}) collective-permute-start(bf16[2,48,384]{2,1,0:T(8,128)(2,1)S(1)} %get-tuple-element.127.refs_0_), channel_id=1, source_target_pairs={{0,2},{1,3},{2,0},{3,1},{4,6},{5,7},{6,4},{7,5},{8,10},{9,11},{10,... | collective-permute-start | bytes 221192 | tf_op jit(solution)/shard_map/ppermute | solution.py:415
  18.9 2.2 %collective-permute-start.16 = (bf16[2,48,384]{2,1,0:T(8,128)(2,1)S(1)}, bf16[2,48,384]{2,1,0:T(8,128)(2,1)S(1)}, u32[]{:S(2)}, u32[]{:S(2)}) collective-permute-start(bf16[2,48,384]{2,1,0:T(8,128)(2,1)S(1)} %get-tuple-element.127.refs_0_), channel_id=1, source_target_pairs={{0,1},{1,0},{2,3},{3,2},{4,5},{5,4},{6,7},{7,6},{8,9},{9,8},{10,11... | collective-permute-start | bytes 221192 | tf_op jit(solution)/shard_map/ppermute | solution.py:415
  21.1 2.6 %collective-permute-done.17.refs_2_ = bf16[2,48,384]{2,1,0:T(8,128)(2,1)S(1)} collective-permute-done((bf16[2,48,384]{2,1,0:T(8,128)(2,1)S(1)}, bf16[2,48,384]{2,1,0:T(8,128)(2,1)S(1)}, u32[]{:S(2)}, u32[]{:S(2)}) %collective-permute-start.17) | collective-permute-done | bytes 73760 | tf_op jit(solution)/shard_map/ppermute | solution.py:415
  23.7 1.3 %collective-permute-start.18 = (bf16[2,48,384]{2,1,0:T(8,128)(2,1)S(1)}, bf16[2,48,384]{2,1,0:T(8,128)(2,1)S(1)}, u32[]{:S(2)}, u32[]{:S(2)}) collective-permute-start(bf16[2,48,384]{2,1,0:T(8,128)(2,1)S(1)} %collective-permute-done.17.refs_2_), channel_id=1, source_target_pairs={{0,1},{1,0},{2,3},{3,2},{4,5},{5,4},{6,7},{7,6},{8,9},{9,8},{10,11... | collective-permute-start | bytes 221192 | tf_op jit(solution)/shard_map/ppermute | solution.py:415
  25.1 3.0 %collective-permute-done.18.refs_3_ = bf16[2,48,384]{2,1,0:T(8,128)(2,1)S(1)} collective-permute-done((bf16[2,48,384]{2,1,0:T(8,128)(2,1)S(1)}, bf16[2,48,384]{2,1,0:T(8,128)(2,1)S(1)}, u32[]{:S(2)}, u32[]{:S(2)}) %collective-permute-start.18) | collective-permute-done | bytes 73760 | tf_op jit(solution)/shard_map/ppermute | solution.py:415
  28.1 1.6 %collective-permute-start.19 = (bf16[2,192,384]{2,1,0:T(8,128)(2,1)S(1)}, bf16[2,192,384]{2,1,0:T(8,128)(2,1)S(1)}, u32[]{:S(2)}, u32[]{:S(2)}) collective-permute-start(bf16[2,192,384]{2,1,0:T(8,128)(2,1)S(1)} %pack.2.refs_0_), channel_id=1, source_target_pairs={{0,8},{4,20},{8,0},{12,28},{16,24},{20,4},{24,16},{28,12},{1,9},{5... | collective-permute-start | bytes 884744 | tf_op jit(solution)/shard_map/ppermute | solution.py:407
  29.7 1.0 %collective-permute-start.23 = (bf16[2,48,384]{2,1,0:T(8,128)(2,1)S(1)}, bf16[2,48,384]{2,1,0:T(8,128)(2,1)S(1)}, u32[]{:S(2)}, u32[]{:S(2)}) collective-permute-start(bf16[2,48,384]{2,1,0:T(8,128)(2,1)S(1)} %get-tuple-element.131.refs_0_), channel_id=1, source_target_pairs={{0,2},{1,3},{2,0},{3,1},{4,6},{5,7},{6,4},{7,5},{8,10},{9,11},{10,... | collective-permute-start | bytes 221192 | tf_op jit(solution)/shard_map/ppermute | solution.py:415
  30.7 2.0 %collective-permute-start.22 = (bf16[2,48,384]{2,1,0:T(8,128)(2,1)S(1)}, bf16[2,48,384]{2,1,0:T(8,128)(2,1)S(1)}, u32[]{:S(2)}, u32[]{:S(2)}) collective-permute-start(bf16[2,48,384]{2,1,0:T(8,128)(2,1)S(1)} %get-tuple-element.131.refs_0_), channel_id=1, source_target_pairs={{0,1},{1,0},{2,3},{3,2},{4,5},{5,4},{6,7},{7,6},{8,9},{9,8},{10,11... | collective-permute-start | bytes 221192 | tf_op jit(solution)/shard_map/ppermute | solution.py:415
  32.7 2.5 %collective-permute-done.23.refs_2_ = bf16[2,48,384]{2,1,0:T(8,128)(2,1)S(1)} collective-permute-done((bf16[2,48,384]{2,1,0:T(8,128)(2,1)S(1)}, bf16[2,48,384]{2,1,0:T(8,128)(2,1)S(1)}, u32[]{:S(2)}, u32[]{:S(2)}) %collective-permute-start.23) | collective-permute-done | bytes 73760 | tf_op jit(solution)/shard_map/ppermute | solution.py:415
  35.2 1.3 %collective-permute-start.24 = (bf16[2,48,384]{2,1,0:T(8,128)(2,1)S(1)}, bf16[2,48,384]{2,1,0:T(8,128)(2,1)S(1)}, u32[]{:S(2)}, u32[]{:S(2)}) collective-permute-start(bf16[2,48,384]{2,1,0:T(8,128)(2,1)S(1)} %collective-permute-done.23.refs_2_), channel_id=1, source_target_pairs={{0,1},{1,0},{2,3},{3,2},{4,5},{5,4},{6,7},{7,6},{8,9},{9,8},{10,11... | collective-permute-start | bytes 221192 | tf_op jit(solution)/shard_map/ppermute | solution.py:415
  36.5 1.2 %collective-permute-start.20 = (bf16[2,192,384]{2,1,0:T(8,128)(2,1)S(1)}, bf16[2,192,384]{2,1,0:T(8,128)(2,1)S(1)}, u32[]{:S(2)}, u32[]{:S(2)}) collective-permute-start(bf16[2,192,384]{2,1,0:T(8,128)(2,1)S(1)} %pack.2.refs_0_), channel_id=1, source_target_pairs={{0,16},{4,12},{8,24},{12,4},{16,0},{20,28},{24,8},{28,20},{1,17},{... | collective-permute-start | bytes 884744 | tf_op jit(solution)/shard_map/ppermute | solution.py:407
  37.7 1.8 %collective-permute-done.24.refs_3_ = bf16[2,48,384]{2,1,0:T(8,128)(2,1)S(1)} collective-permute-done((bf16[2,48,384]{2,1,0:T(8,128)(2,1)S(1)}, bf16[2,48,384]{2,1,0:T(8,128)(2,1)S(1)}, u32[]{:S(2)}, u32[]{:S(2)}) %collective-permute-start.24) | collective-permute-done | bytes 73760 | tf_op jit(solution)/shard_map/ppermute | solution.py:415
  40.0 1.7 %collective-permute-start.26 = (bf16[2,192,384]{2,1,0:T(8,128)(2,1)S(1)}, bf16[2,192,384]{2,1,0:T(8,128)(2,1)S(1)}, u32[]{:S(2)}, u32[]{:S(2)}) collective-permute-start(bf16[2,192,384]{2,1,0:T(8,128)(2,1)S(1)} %pack.3.refs_0_), channel_id=1, source_target_pairs={{0,16},{4,12},{8,24},{12,4},{16,0},{20,28},{24,8},{28,20},{1,17},{... | collective-permute-start | bytes 884744 | tf_op jit(solution)/shard_map/ppermute | solution.py:407
  41.8 1.9 %collective-permute-start.9 = (bf16[2,192,384]{2,1,0:T(8,128)(2,1)S(1)}, bf16[2,192,384]{2,1,0:T(8,128)(2,1)S(1)}, u32[]{:S(2)}, u32[]{:S(2)}) collective-permute-start(bf16[2,192,384]{2,1,0:T(8,128)(2,1)S(1)} %get-tuple-element.111), channel_id=1, source_target_pairs={{0,8},{4,12},{8,0},{12,4},{16,24},{20,28},{24,16},{28,20},{1,9},{5... | collective-permute-start | bytes 884744 | tf_op jit(solution)/shard_map/ppermute | solution.py:442
  43.8 2.1 %collective-permute-done.20.refs_2_ = bf16[2,192,384]{2,1,0:T(8,128)(2,1)S(1)} collective-permute-done((bf16[2,192,384]{2,1,0:T(8,128)(2,1)S(1)}, bf16[2,192,384]{2,1,0:T(8,128)(2,1)S(1)}, u32[]{:S(2)}, u32[]{:S(2)}) %collective-permute-start.20) | collective-permute-done | bytes 294944 | tf_op jit(solution)/shard_map/ppermute | solution.py:407
  45.8 2.0 %collective-permute-start.11 = (bf16[2,192,384]{2,1,0:T(8,128)(2,1)S(1)}, bf16[2,192,384]{2,1,0:T(8,128)(2,1)S(1)}, u32[]{:S(2)}, u32[]{:S(2)}) collective-permute-start(bf16[2,192,384]{2,1,0:T(8,128)(2,1)S(1)} %get-tuple-element.113), channel_id=1, source_target_pairs={{0,24},{4,28},{8,16},{12,20},{16,8},{20,12},{24,0},{28,4},{1,25},{... | collective-permute-start | bytes 884744 | tf_op jit(solution)/shard_map/ppermute | solution.py:442
  48.1 1.4 %collective-permute-done.25.refs_1_ = bf16[2,192,384]{2,1,0:T(8,128)(2,1)S(1)} collective-permute-done((bf16[2,192,384]{2,1,0:T(8,128)(2,1)S(1)}, bf16[2,192,384]{2,1,0:T(8,128)(2,1)S(1)}, u32[]{:S(2)}, u32[]{:S(2)}) %collective-permute-start.25) | collective-permute-done | bytes 294944 | tf_op jit(solution)/shard_map/ppermute | solution.py:407
  49.5 2.5 %collective-permute-done.26.refs_2_ = bf16[2,192,384]{2,1,0:T(8,128)(2,1)S(1)} collective-permute-done((bf16[2,192,384]{2,1,0:T(8,128)(2,1)S(1)}, bf16[2,192,384]{2,1,0:T(8,128)(2,1)S(1)}, u32[]{:S(2)}, u32[]{:S(2)}) %collective-permute-start.26) | collective-permute-done | bytes 294944 | tf_op jit(solution)/shard_map/ppermute | solution.py:407
  52.3 1.6 %collective-permute-done.9.refs_1_ = bf16[2,192,384]{2,1,0:T(8,128)(2,1)S(1)} collective-permute-done((bf16[2,192,384]{2,1,0:T(8,128)(2,1)S(1)}, bf16[2,192,384]{2,1,0:T(8,128)(2,1)S(1)}, u32[]{:S(2)}, u32[]{:S(2)}) %collective-permute-start.9) | collective-permute-done | bytes 294944 | tf_op jit(solution)/shard_map/ppermute | solution.py:442
  53.9 1.5 %collective-permute-start.28 = (bf16[2,192,384]{2,1,0:T(8,128)(2,1)S(1)}, bf16[2,192,384]{2,1,0:T(8,128)(2,1)S(1)}, u32[]{:S(2)}, u32[]{:S(2)}) collective-permute-start(bf16[2,192,384]{2,1,0:T(8,128)(2,1)S(1)} %collective-permute-done.19.refs_1_), channel_id=1, source_target_pairs={{0,16},{4,12},{8,24},{12,4},{16,0},{20,28},{24,8},{28,20},{1,17},{... | collective-permute-start | bytes 884744 | tf_op jit(solution)/shard_map/ppermute | solution.py:407
  55.4 1.1 %collective-permute-done.10.refs_2_ = bf16[2,192,384]{2,1,0:T(8,128)(2,1)S(1)} collective-permute-done((bf16[2,192,384]{2,1,0:T(8,128)(2,1)S(1)}, bf16[2,192,384]{2,1,0:T(8,128)(2,1)S(1)}, u32[]{:S(2)}, u32[]{:S(2)}) %collective-permute-start.10) | collective-permute-done | bytes 294944 | tf_op jit(solution)/shard_map/ppermute | solution.py:442
  56.5 2.4 %collective-permute-start.29 = (bf16[2,192,384]{2,1,0:T(8,128)(2,1)S(1)}, bf16[2,192,384]{2,1,0:T(8,128)(2,1)S(1)}, u32[]{:S(2)}, u32[]{:S(2)}) collective-permute-start(bf16[2,192,384]{2,1,0:T(8,128)(2,1)S(1)} %collective-permute-done.25.refs_1_), channel_id=1, source_target_pairs={{0,16},{4,12},{8,24},{12,4},{16,0},{20,28},{24,8},{28,20},{1,17},{... | collective-permute-start | bytes 884744 | tf_op jit(solution)/shard_map/ppermute | solution.py:407
  58.9 1.6 %collective-permute-done.11.refs_3_ = bf16[2,192,384]{2,1,0:T(8,128)(2,1)S(1)} collective-permute-done((bf16[2,192,384]{2,1,0:T(8,128)(2,1)S(1)}, bf16[2,192,384]{2,1,0:T(8,128)(2,1)S(1)}, u32[]{:S(2)}, u32[]{:S(2)}) %collective-permute-start.11) | collective-permute-done | bytes 294944 | tf_op jit(solution)/shard_map/ppermute | solution.py:442
  62.1 3.2 %collective-permute-done.29.refs_1_ = bf16[2,192,384]{2,1,0:T(8,128)(2,1)S(1)} collective-permute-done((bf16[2,192,384]{2,1,0:T(8,128)(2,1)S(1)}, bf16[2,192,384]{2,1,0:T(8,128)(2,1)S(1)}, u32[]{:S(2)}, u32[]{:S(2)}) %collective-permute-start.29) | collective-permute-done | bytes 294944 | tf_op jit(solution)/shard_map/ppermute | solution.py:407
  66.1 1.2 %amplitudes.2 = (f32[384,768]{1,0:T(8,128)S(1)}, bf16[2,768,384]{2,1,0:T(8,128)(2,1)S(1)}, bf16[2,384,384]{2,1,0:T(8,128)(2,1)S(1)}) custom-call(bf16[384,1536]{1,0:T(8,128)(2,1)S(1)} %prep.1.own_t, bf16[3,2,192,384]{3,2,1,0:T(8,128)(2,1)S(1)} %join.5.early, bf16[3,2,192,384]{3,2,1,0:T(8,128)(2,1)S(1)} %collective-permute-done.21.other), custom_call_target="tpu_custom_call" | custom-call | flops 452984832 | bytes 3145728 | tf_op jit(solution)/shard_map/amplitudes/pallas_call | solution.py:303
  67.3 1.2 %amplitudes.3 = (f32[384,768]{1,0:T(8,128)S(1)}, bf16[2,768,384]{2,1,0:T(8,128)(2,1)S(1)}, bf16[2,384,384]{2,1,0:T(8,128)(2,1)S(1)}) custom-call(bf16[384,1536]{1,0:T(8,128)(2,1)S(1)} %prep.1.own_t, bf16[3,2,192,384]{3,2,1,0:T(8,128)(2,1)S(1)} %join.6.early, bf16[3,2,192,384]{3,2,1,0:T(8,128)(2,1)S(1)} %collective-permute-done.27.other), custom_call_target="tpu_custom_call" | custom-call | flops 452984832 | bytes 3145728 | tf_op jit(solution)/shard_map/amplitudes/pallas_call | solution.py:303
  68.6 4.9 %pair_terms.1 = (bf16[384,1536]{1,0:T(8,128)(2,1)}, f32[1,1]{1,0:T(1,128)}) custom-call(s32[32]{0:T(128)S(1)} %copy-done, s32[1,4]{1,0:T(1,128)S(1)} %copy-done.1, s32[1,384]{1,0:T(1,128)S(1)} %reshape.16.row_ref, s32[384,1]{1,0:T(8,128)S(1)} %reshape.19.col_ref, bf16[384,1536]{1,0:T(8,128)(2,1)S(1)} %prep.1.own_t, ...), custom_call_target="tpu_custom_call" | custom-call | tf_op jit(solution)/shard_map/pair_terms/pallas_call | solution.py:386
  (33 shorter events, 5.6 us)
Async XLA Ops:
  0.6 15.8 %copy-start.1 = (s32[1,4]{1,0:T(1,128)S(1)}, s32[1,4]{1,0:T(1,128)}, u32[]{:S(2)}) copy-start(s32[1,4]{1,0:T(1,128)} %plan_ref.3) | copy-start | bytes 52
  5.5 7.8 %collective-permute-start.13 = (bf16[2,48,384]{2,1,0:T(8,128)(2,1)S(1)}, bf16[2,48,384]{2,1,0:T(8,128)(2,1)S(1)}, u32[]{:S(2)}, u32[]{:S(2)}) collective-permute-start(bf16[2,48,384]{2,1,0:T(8,128)(2,1)S(1)} %get-tuple-element.116), channel_id=1, source_target_pairs={{0,1},{1,2},{2,3},{3,0},{4,5},{5,6},{6,7},{7,4},{8,9},{9,10},{10,1... | collective-permute-start | bytes 221192 | tf_op jit(solution)/shard_map/ppermute | solution.py:411
  8.6 7.5 %collective-permute-start.14 = (bf16[2,48,384]{2,1,0:T(8,128)(2,1)S(1)}, bf16[2,48,384]{2,1,0:T(8,128)(2,1)S(1)}, u32[]{:S(2)}, u32[]{:S(2)}) collective-permute-start(bf16[2,48,384]{2,1,0:T(8,128)(2,1)S(1)} %get-tuple-element.117), channel_id=1, source_target_pairs={{0,2},{1,3},{2,0},{3,1},{4,6},{5,7},{6,4},{7,5},{8,10},{9,11},{10,... | collective-permute-start | bytes 221192 | tf_op jit(solution)/shard_map/ppermute | solution.py:411
  11.2 5.2 %collective-permute-start.15 = (bf16[2,48,384]{2,1,0:T(8,128)(2,1)S(1)}, bf16[2,48,384]{2,1,0:T(8,128)(2,1)S(1)}, u32[]{:S(2)}, u32[]{:S(2)}) collective-permute-start(bf16[2,48,384]{2,1,0:T(8,128)(2,1)S(1)} %get-tuple-element.118), channel_id=1, source_target_pairs={{0,3},{1,0},{2,1},{3,2},{4,7},{5,4},{6,5},{7,6},{8,11},{9,8},{10,9... | collective-permute-start | bytes 221192 | tf_op jit(solution)/shard_map/ppermute | solution.py:411
  17.3 6.4 %collective-permute-start.17 = (bf16[2,48,384]{2,1,0:T(8,128)(2,1)S(1)}, bf16[2,48,384]{2,1,0:T(8,128)(2,1)S(1)}, u32[]{:S(2)}, u32[]{:S(2)}) collective-permute-start(bf16[2,48,384]{2,1,0:T(8,128)(2,1)S(1)} %get-tuple-element.127.refs_0_), channel_id=1, source_target_pairs={{0,2},{1,3},{2,0},{3,1},{4,6},{5,7},{6,4},{7,5},{8,10},{9,11},{10,... | collective-permute-start | bytes 221192 | tf_op jit(solution)/shard_map/ppermute | solution.py:415
  18.9 6.2 %collective-permute-start.16 = (bf16[2,48,384]{2,1,0:T(8,128)(2,1)S(1)}, bf16[2,48,384]{2,1,0:T(8,128)(2,1)S(1)}, u32[]{:S(2)}, u32[]{:S(2)}) collective-permute-start(bf16[2,48,384]{2,1,0:T(8,128)(2,1)S(1)} %get-tuple-element.127.refs_0_), channel_id=1, source_target_pairs={{0,1},{1,0},{2,3},{3,2},{4,5},{5,4},{6,7},{7,6},{8,9},{9,8},{10,11... | collective-permute-start | bytes 221192 | tf_op jit(solution)/shard_map/ppermute | solution.py:415
  23.7 4.4 %collective-permute-start.18 = (bf16[2,48,384]{2,1,0:T(8,128)(2,1)S(1)}, bf16[2,48,384]{2,1,0:T(8,128)(2,1)S(1)}, u32[]{:S(2)}, u32[]{:S(2)}) collective-permute-start(bf16[2,48,384]{2,1,0:T(8,128)(2,1)S(1)} %collective-permute-done.17.refs_2_), channel_id=1, source_target_pairs={{0,1},{1,0},{2,3},{3,2},{4,5},{5,4},{6,7},{7,6},{8,9},{9,8},{10,11... | collective-permute-start | bytes 221192 | tf_op jit(solution)/shard_map/ppermute | solution.py:415
  28.1 15.6 %collective-permute-start.19 = (bf16[2,192,384]{2,1,0:T(8,128)(2,1)S(1)}, bf16[2,192,384]{2,1,0:T(8,128)(2,1)S(1)}, u32[]{:S(2)}, u32[]{:S(2)}) collective-permute-start(bf16[2,192,384]{2,1,0:T(8,128)(2,1)S(1)} %pack.2.refs_0_), channel_id=1, source_target_pairs={{0,8},{4,20},{8,0},{12,28},{16,24},{20,4},{24,16},{28,12},{1,9},{5... | collective-permute-start | bytes 884744 | tf_op jit(solution)/shard_map/ppermute | solution.py:407
  29.7 5.5 %collective-permute-start.23 = (bf16[2,48,384]{2,1,0:T(8,128)(2,1)S(1)}, bf16[2,48,384]{2,1,0:T(8,128)(2,1)S(1)}, u32[]{:S(2)}, u32[]{:S(2)}) collective-permute-start(bf16[2,48,384]{2,1,0:T(8,128)(2,1)S(1)} %get-tuple-element.131.refs_0_), channel_id=1, source_target_pairs={{0,2},{1,3},{2,0},{3,1},{4,6},{5,7},{6,4},{7,5},{8,10},{9,11},{10,... | collective-permute-start | bytes 221192 | tf_op jit(solution)/shard_map/ppermute | solution.py:415
  30.7 7.0 %collective-permute-start.22 = (bf16[2,48,384]{2,1,0:T(8,128)(2,1)S(1)}, bf16[2,48,384]{2,1,0:T(8,128)(2,1)S(1)}, u32[]{:S(2)}, u32[]{:S(2)}) collective-permute-start(bf16[2,48,384]{2,1,0:T(8,128)(2,1)S(1)} %get-tuple-element.131.refs_0_), channel_id=1, source_target_pairs={{0,1},{1,0},{2,3},{3,2},{4,5},{5,4},{6,7},{7,6},{8,9},{9,8},{10,11... | collective-permute-start | bytes 221192 | tf_op jit(solution)/shard_map/ppermute | solution.py:415
  35.2 4.4 %collective-permute-start.24 = (bf16[2,48,384]{2,1,0:T(8,128)(2,1)S(1)}, bf16[2,48,384]{2,1,0:T(8,128)(2,1)S(1)}, u32[]{:S(2)}, u32[]{:S(2)}) collective-permute-start(bf16[2,48,384]{2,1,0:T(8,128)(2,1)S(1)} %collective-permute-done.23.refs_2_), channel_id=1, source_target_pairs={{0,1},{1,0},{2,3},{3,2},{4,5},{5,4},{6,7},{7,6},{8,9},{9,8},{10,11... | collective-permute-start | bytes 221192 | tf_op jit(solution)/shard_map/ppermute | solution.py:415
  36.5 9.3 %collective-permute-start.20 = (bf16[2,192,384]{2,1,0:T(8,128)(2,1)S(1)}, bf16[2,192,384]{2,1,0:T(8,128)(2,1)S(1)}, u32[]{:S(2)}, u32[]{:S(2)}) collective-permute-start(bf16[2,192,384]{2,1,0:T(8,128)(2,1)S(1)} %pack.2.refs_0_), channel_id=1, source_target_pairs={{0,16},{4,12},{8,24},{12,4},{16,0},{20,28},{24,8},{28,20},{1,17},{... | collective-permute-start | bytes 884744 | tf_op jit(solution)/shard_map/ppermute | solution.py:407
  39.6 9.9 %collective-permute-start.25 = (bf16[2,192,384]{2,1,0:T(8,128)(2,1)S(1)}, bf16[2,192,384]{2,1,0:T(8,128)(2,1)S(1)}, u32[]{:S(2)}, u32[]{:S(2)}) collective-permute-start(bf16[2,192,384]{2,1,0:T(8,128)(2,1)S(1)} %pack.3.refs_0_), channel_id=1, source_target_pairs={{0,8},{4,20},{8,0},{12,28},{16,24},{20,4},{24,16},{28,12},{1,9},{5... | collective-permute-start | bytes 884744 | tf_op jit(solution)/shard_map/ppermute | solution.py:407
  40.0 11.9 %collective-permute-start.26 = (bf16[2,192,384]{2,1,0:T(8,128)(2,1)S(1)}, bf16[2,192,384]{2,1,0:T(8,128)(2,1)S(1)}, u32[]{:S(2)}, u32[]{:S(2)}) collective-permute-start(bf16[2,192,384]{2,1,0:T(8,128)(2,1)S(1)} %pack.3.refs_0_), channel_id=1, source_target_pairs={{0,16},{4,12},{8,24},{12,4},{16,0},{20,28},{24,8},{28,20},{1,17},{... | collective-permute-start | bytes 884744 | tf_op jit(solution)/shard_map/ppermute | solution.py:407
  41.8 12.1 %collective-permute-start.9 = (bf16[2,192,384]{2,1,0:T(8,128)(2,1)S(1)}, bf16[2,192,384]{2,1,0:T(8,128)(2,1)S(1)}, u32[]{:S(2)}, u32[]{:S(2)}) collective-permute-start(bf16[2,192,384]{2,1,0:T(8,128)(2,1)S(1)} %get-tuple-element.111), channel_id=1, source_target_pairs={{0,8},{4,12},{8,0},{12,4},{16,24},{20,28},{24,16},{28,20},{1,9},{5... | collective-permute-start | bytes 884744 | tf_op jit(solution)/shard_map/ppermute | solution.py:442
  43.7 12.7 %collective-permute-start.10 = (bf16[2,192,384]{2,1,0:T(8,128)(2,1)S(1)}, bf16[2,192,384]{2,1,0:T(8,128)(2,1)S(1)}, u32[]{:S(2)}, u32[]{:S(2)}) collective-permute-start(bf16[2,192,384]{2,1,0:T(8,128)(2,1)S(1)} %get-tuple-element.112), channel_id=1, source_target_pairs={{0,16},{4,20},{8,24},{12,28},{16,0},{20,4},{24,8},{28,12},{1,17},{... | collective-permute-start | bytes 884744 | tf_op jit(solution)/shard_map/ppermute | solution.py:442
  45.8 14.6 %collective-permute-start.11 = (bf16[2,192,384]{2,1,0:T(8,128)(2,1)S(1)}, bf16[2,192,384]{2,1,0:T(8,128)(2,1)S(1)}, u32[]{:S(2)}, u32[]{:S(2)}) collective-permute-start(bf16[2,192,384]{2,1,0:T(8,128)(2,1)S(1)} %get-tuple-element.113), channel_id=1, source_target_pairs={{0,24},{4,28},{8,16},{12,20},{16,8},{20,12},{24,0},{28,4},{1,25},{... | collective-permute-start | bytes 884744 | tf_op jit(solution)/shard_map/ppermute | solution.py:442
  49.5 16.5 %collective-permute-start.21 = (bf16[3,2,192,384]{3,2,1,0:T(8,128)(2,1)S(1)}, bf16[3,2,192,384]{3,2,1,0:T(8,128)(2,1)S(1)}, u32[]{:S(2)}, u32[]{:S(2)}) collective-permute-start(bf16[3,2,192,384]{3,2,1,0:T(8,128)(2,1)S(1)} %join.5.early), channel_id=1, source_target_pairs={{0,4},{4,0},{8,12},{12,8},{16,20},{20,16},{24,28},{28,24},{1,5},{5... | collective-permute-start | bytes 2654216 | tf_op jit(solution)/shard_map/ppermute | solution.py:403
  52.2 15.1 %collective-permute-start.27 = (bf16[3,2,192,384]{3,2,1,0:T(8,128)(2,1)S(1)}, bf16[3,2,192,384]{3,2,1,0:T(8,128)(2,1)S(1)}, u32[]{:S(2)}, u32[]{:S(2)}) collective-permute-start(bf16[3,2,192,384]{3,2,1,0:T(8,128)(2,1)S(1)} %join.6.early), channel_id=1, source_target_pairs={{0,4},{4,0},{8,12},{12,8},{16,20},{20,16},{24,28},{28,24},{1,5},{5... | collective-permute-start | bytes 2654216 | tf_op jit(solution)/shard_map/ppermute | solution.py:403
  53.9 8.2 %collective-permute-start.28 = (bf16[2,192,384]{2,1,0:T(8,128)(2,1)S(1)}, bf16[2,192,384]{2,1,0:T(8,128)(2,1)S(1)}, u32[]{:S(2)}, u32[]{:S(2)}) collective-permute-start(bf16[2,192,384]{2,1,0:T(8,128)(2,1)S(1)} %collective-permute-done.19.refs_1_), channel_id=1, source_target_pairs={{0,16},{4,12},{8,24},{12,4},{16,0},{20,28},{24,8},{28,20},{1,17},{... | collective-permute-start | bytes 884744 | tf_op jit(solution)/shard_map/ppermute | solution.py:407
  56.5 8.8 %collective-permute-start.29 = (bf16[2,192,384]{2,1,0:T(8,128)(2,1)S(1)}, bf16[2,192,384]{2,1,0:T(8,128)(2,1)S(1)}, u32[]{:S(2)}, u32[]{:S(2)}) collective-permute-start(bf16[2,192,384]{2,1,0:T(8,128)(2,1)S(1)} %collective-permute-done.25.refs_1_), channel_id=1, source_target_pairs={{0,16},{4,12},{8,24},{12,4},{16,0},{20,28},{24,8},{28,20},{1,17},{... | collective-permute-start | bytes 884744 | tf_op jit(solution)/shard_map/ppermute | solution.py:407
  60.5 5.0 %copy-start.2 = (s32[384]{0:T(512)S(1)}, s32[384]{0:T(512)}, u32[]{:S(2)}) copy-start(s32[384]{0:T(512)} %param.11) | copy-start | bytes 4612
  61.3 4.4 %collective-permute-start.12 = (bf16[4,192,384]{2,1,0:T(8,128)(2,1)S(1)}, bf16[4,192,384]{2,1,0:T(8,128)(2,1)S(1)}, u32[]{:S(2)}, u32[]{:S(2)}) collective-permute-start(bf16[4,192,384]{2,1,0:T(8,128)(2,1)S(1)} %join.4), channel_id=1, source_target_pairs={{0,4},{4,0},{8,12},{12,8},{16,20},{20,16},{24,28},{28,24},{1,5},{5... | collective-permute-start | bytes 1769480 | tf_op jit(solution)/shard_map/ppermute | solution.py:403
  65.4 3.2 %collective-permute-start.30 = (bf16[2,2,192,384]{3,2,1,0:T(8,128)(2,1)S(1)}, bf16[2,2,192,384]{3,2,1,0:T(8,128)(2,1)S(1)}, u32[]{:S(2)}, u32[]{:S(2)}) collective-permute-start(bf16[2,2,192,384]{3,2,1,0:T(8,128)(2,1)S(1)} %join.7.rest_6_), channel_id=1, source_target_pairs={{0,4},{4,0},{8,12},{12,8},{16,20},{20,16},{24,28},{28,24},{1,5},{5... | collective-permute-start | bytes 1769480 | tf_op jit(solution)/shard_map/ppermute | solution.py:403
  67.3 1.3 %copy-start = (s32[32]{0:T(128)S(1)}, s32[32]{0:T(128)}, u32[]{:S(2)}) copy-start(s32[32]{0:T(128)} %occ_ref.1) | copy-start | bytes 388
